TPU v7x, 128 devices: a whole 4x4x4 slice. The times are simulated.
128 devices in a mesh: il: 16 (over x, z), xl: 8 (over y, core).
Axes of the slice: x: 4, y: 4, z: 4, core: 2. Of those that a mesh axis runs over, the one named last changes fastest.
Arguments:
- traces: bfloat16 [65536, 1536], P(('il', 'xl')), may hold values from -6 to 6
- fold_ids: int32 [64, 128, 4], P('il', 'xl'), may hold values from 0 to 65535, as said below
- fold_counts: int32 [64, 128], P('il', 'xl'), may hold values from 2 to 4
- conv1_w: bfloat16 [8, 64], replicated, may hold values from -2 to 2
- conv2_w: bfloat16 [512, 256], replicated, may hold values from -0.25 to 0.25
- conv3_w: bfloat16 [768, 256], replicated, may hold values from -0.21875 to 0.21875
- conv4_w: bfloat16 [768, 256], replicated, may hold values from -0.21875 to 0.21875
- lateral_w: float32 [256, 9], P('xl'), may hold values from -2 to 2
Outputs:
- encoded: bfloat16 [96, 256, 64, 128], P('il', 'xl')
Inputs may be any that keep to these rules, and one draw needn't show every extreme that they name: `fold_ids`: among the slots of one device's 4 x 16 bins, at most 4 name traces of any one shard (ids k * 512 to (k + 1) * 512 - 1, the shard of device k in il+xl order), and some shard is named exactly 4 times. Dead slots (index at or beyond the bin's count) also hold valid ids.
All inputs are finite; a program needn't handle non-finite values.
Results may differ from a plain program's by a relative error of at most 0.014.
Values may be sent and summed in bfloat16 or wider, within the bound.
A program may use at most 192 MiB of HBM per device.

v0:
```python
import jax
import jax.numpy as jnp
from jax import lax
from jax.sharding import PartitionSpec as P


def strided_conv(inputs, weight):
    batch_rows, length, channels = inputs.shape
    padded = jnp.pad(inputs, ((0, 0), (4, 0), (0, 0)))
    earlier = padded[:, :length].reshape(batch_rows * (length // 4), 4 * channels)
    current = padded[:, 4:].reshape(batch_rows * (length // 4), 4 * channels)
    result = jnp.dot(earlier, weight[: 4 * channels], preferred_element_type=jnp.float32)
    result = result + jnp.dot(current, weight[4 * channels :], preferred_element_type=jnp.float32)
    return result.reshape(batch_rows, length // 4, weight.shape[1])


def first_conv(stacked, conv1_w):
    batch_rows, length = stacked.shape
    block_count = length // 128
    out_channels = conv1_w.shape[1]
    blocks = stacked.reshape(batch_rows, block_count, 128)
    previous = jnp.pad(blocks, ((0, 0), (1, 0), (0, 0)))[:, :block_count]
    paired = jnp.concatenate([previous, blocks], axis=2).reshape(batch_rows * block_count, 256)
    sample_index = jnp.arange(256, dtype=jnp.int32)[:, None, None]
    step_index = jnp.arange(32, dtype=jnp.int32)[None, :, None]
    tap_index = jnp.arange(8, dtype=jnp.int32)[None, None, :]
    selector = (sample_index - 124 - 4 * step_index == tap_index).astype(jnp.float32)
    banded = (
        jnp.einsum("etj,jo->eto", selector, conv1_w.astype(jnp.float32))
        .astype(jnp.bfloat16)
        .reshape(256, 32 * out_channels)
    )
    result = jnp.dot(paired, banded, preferred_element_type=jnp.float32)
    return result.reshape(batch_rows, length // 4, out_channels)


def centred_conv(inputs, weight):
    batch_rows, length, channels = inputs.shape
    padded = jnp.pad(inputs, ((0, 0), (1, 1), (0, 0)))
    result = jnp.zeros((batch_rows * length, weight.shape[1]), jnp.float32)
    for offset in range(3):
        window = padded[:, offset : offset + length].reshape(batch_rows * length, channels)
        result = result + jnp.dot(
            window,
            weight[offset * channels : (offset + 1) * channels],
            preferred_element_type=jnp.float32,
        )
    return result.reshape(batch_rows, length, weight.shape[1])


def encode(stacked, conv1_w, conv2_w, conv3_w, conv4_w):
    first_layer = jax.nn.gelu(first_conv(stacked, conv1_w)).astype(jnp.bfloat16)
    second_layer = jax.nn.gelu(strided_conv(first_layer, conv2_w)).astype(jnp.bfloat16)
    third_layer = jax.nn.gelu(centred_conv(second_layer, conv3_w)).astype(jnp.bfloat16)
    return (second_layer.astype(jnp.float32) + centred_conv(third_layer, conv4_w)).astype(
        jnp.bfloat16
    )


def stack_rows(gathered, counts):
    running = jnp.zeros((gathered.shape[0], gathered.shape[2]), jnp.float32)
    for slot_index in range(gathered.shape[1]):
        live_mask = (slot_index < counts)[:, None]
        running = running + jnp.where(
            live_mask, gathered[:, slot_index].astype(jnp.float32), jnp.float32(0.0)
        )
    return (running / counts.astype(jnp.float32)[:, None]).astype(jnp.bfloat16)


def lateral_mix(block_values, weight):
    field_values = block_values.astype(jnp.float32)
    rows_out = field_values.shape[-2]
    cols_out = field_values.shape[-1]
    widths = [(0, 0)] * (field_values.ndim - 2) + [(1, 1), (1, 1)]
    padded = jnp.pad(field_values, widths)
    mixed_sum = field_values
    for row_shift in range(3):
        for col_shift in range(3):
            tap_weight = weight[:, row_shift * 3 + col_shift][:, None, None]
            mixed_sum = (
                mixed_sum
                + tap_weight
                * padded[..., row_shift : row_shift + rows_out, col_shift : col_shift + cols_out]
            )
    return mixed_sum.astype(jnp.bfloat16)


def per_device(traces, fold_ids, fold_counts, conv1_w, conv2_w, conv3_w, conv4_w, lateral_w):
    il_count = lax.axis_size("il")
    xl_count = lax.axis_size("xl")
    devices = il_count * xl_count
    rows_here = traces.shape[0]
    samples = traces.shape[1]
    bins_il, bins_xl, fold_depth = fold_ids.shape
    bin_total = bins_il * bins_xl
    slot_total = bin_total * fold_depth
    capacity = 2 * slot_total // devices
    flat_ids = fold_ids.reshape(slot_total)
    source = flat_ids // rows_here
    local_row = flat_ids % rows_here
    onehot = (source[:, None] == jnp.arange(devices, dtype=jnp.int32)[None, :]).astype(jnp.int32)
    slot_rank = jnp.sum(onehot * jnp.cumsum(onehot, axis=0), axis=1) - 1
    position = source * capacity + slot_rank
    requests = (
        jnp.zeros((devices * capacity,), jnp.int32)
        .at[position]
        .set(local_row)
        .reshape(devices, capacity)
    )
    wanted = lax.all_to_all(requests, ("il", "xl"), split_axis=0, concat_axis=0, tiled=True)
    picked = jnp.take(traces, wanted.reshape(-1), axis=0).reshape(
        wanted.shape[0], wanted.shape[1], samples
    )
    arrived = lax.all_to_all(picked, ("il", "xl"), split_axis=0, concat_axis=0, tiled=True)
    gathered = jnp.take(arrived.reshape(devices * capacity, samples), position, axis=0).reshape(
        bin_total, fold_depth, samples
    )
    features = encode(
        stack_rows(gathered, fold_counts.reshape(bin_total)), conv1_w, conv2_w, conv3_w, conv4_w
    )
    time_steps = features.shape[1]
    channels = features.shape[2]
    slab_steps = time_steps // il_count
    group_width = channels // xl_count
    tiled = features.reshape(bins_il, bins_xl, il_count, slab_steps, xl_count, group_width)
    outgoing = tiled.transpose(2, 4, 3, 0, 1, 5).reshape(
        devices, slab_steps, bin_total * group_width
    )
    received = lax.all_to_all(outgoing, ("il", "xl"), split_axis=0, concat_axis=0, tiled=True)
    steps_here = received.shape[1]
    placed = received.reshape(
        il_count, xl_count, steps_here, bins_il, bins_xl, group_width
    ).transpose(2, 5, 0, 3, 1, 4)
    return lateral_mix(
        placed.reshape(steps_here, group_width, il_count * bins_il, xl_count * bins_xl), lateral_w
    )


def solution(mesh):
    return jax.shard_map(
        per_device,
        mesh=mesh,
        in_specs=(
            P(("il", "xl"), None),
            P("il", "xl", None),
            P("il", "xl"),
            P(),
            P(),
            P(),
            P(),
            P("xl", None),
        ),
        out_specs=P("il", "xl", None, None),
        check_vma=False,
    )
```

profile of v0, /device:TPU:1, one launch (start us, length us, event | category | flops | bytes accessed | tf_op | source)
XLA Modules:
  0.0 403.8 jit_solution(4266915218006450868)
XLA Ops:
  3.4 20.8 %all_to_all.19 = s32[128,1,4]{2,1,0:T(1,128)S(1)} all-to-all(s32[128,1,4]{2,1,0:T(1,128)S(1)} %bitcast.92), channel_id=1, replica_groups=mesh['il'=16,'xl'=8] {'il','xl'}, dimensions={0} | all-to-all | bytes 4096 | tf_op jit(solution)/shard_map/all_to_all | solution.py:110
  30.3 4.9 %all-to-all-start.1 = ((bf16[128,4,1536]{2,1,0:T(4,128)(2,1)}), bf16[128,4,1536]{2,1,0:T(4,128)(2,1)S(1)}, u32[]{:S(2)}, u32[]{:S(2)}) async-start(bf16[128,4,1536]{2,1,0:T(4,128)(2,1)} %broadcast_select_fusion), calls=%async_computation.1 | async-start | bytes 3145728 | tf_op jit(solution)/shard_map/all_to_all | solution.py:114
  38.5 21.3 %all-to-all-done.1 = bf16[128,4,1536]{2,1,0:T(4,128)(2,1)S(1)} async-done(((bf16[128,4,1536]{2,1,0:T(4,128)(2,1)}), bf16[128,4,1536]{2,1,0:T(4,128)(2,1)S(1)}, u32[]{:S(2)}, u32[]{:S(2)}) %all-to-all-start.1) | async-done | bytes 1572896 | tf_op jit(solution)/shard_map/all_to_all | solution.py:114
  73.8 11.4 %reshape.407 = f32[64,384,64]{2,1,0:T(8,128)} reshape(f32[768,2048]{1,0:T(8,128)} %fusion.91) | data formatting | bytes 12582912 | tf_op jit(solution)/shard_map/reshape | solution.py:34
  85.2 7.1 %reshape.409 = f32[6144,256]{1,0:T(8,128)} reshape(f32[768,2048]{1,0:T(8,128)} %fusion.91) | data formatting | bytes 12582912 | tf_op jit(solution)/shard_map/reshape | solution.py:34
  92.3 9.8 %copy.57 = f32[64,384,64]{1,2,0:T(8,128)} copy(f32[64,384,64]{2,1,0:T(8,128)} %reshape.407) | data formatting | bytes 12582912 | tf_op jit(solution)/shard_map/reshape | solution.py:34
  102.1 3.9 fusion.17
  109.5 6.6 %copy.58 = bf16[64,384,64]{2,1,0:T(8,128)(2,1)} copy(bf16[64,384,64]{1,2,0:T(8,128)(2,1)} %pad_slice_fusion.8) | data formatting | bytes 6291456 | tf_op jit(solution)/shard_map/slice | solution.py:10
  116.1 9.9 %reshape.408 = bf16[6144,256]{1,0:T(8,128)(2,1)} reshape(bf16[64,384,64]{2,1,0:T(8,128)(2,1)} %copy.58) | data formatting | bytes 6291456 | tf_op jit(solution)/shard_map/reshape | solution.py:10
  128.9 7.9 %convolution_add_fusion.4 = f32[6144,256]{1,0:T(8,128)} fusion(f32[6144,256]{1,0:T(8,128)S(1)} %fusion.106, f32[6144,256]{1,0:T(8,128)} %reshape.409, bf16[512,256]{1,0:T(8,128)(2,1)S(1)} %copy-done.5), kind=kOutput, calls=%fused_computation.33 | convolution fusion | flops 821035008 | bytes 19005440 | tf_op jit(solution)/shard_map/dot_general | solution.py:13
  136.7 15.7 %reshape.410 = f32[4,16,16,6,8,32]{5,4,3,2,1,0:T(8,128)} reshape(f32[6144,256]{1,0:T(8,128)} %convolution_add_fusion.4) | data formatting | bytes 12582912 | tf_op jit(solution)/shard_map/reshape | solution.py:14
  156.3 4.1 %pad_slice_fusion.11 = (bf16[64,96,256]{2,1,0:T(8,128)(2,1)S(1)}, bf16[64,96,256]{2,1,0:T(8,128)(2,1)S(1)}) fusion(bf16[64,96,256]{2,1,0:T(8,128)(2,1)S(1)} %fusion.33), kind=kLoop, calls=%fused_computation.116 | loop fusion | bytes 9437184 | tf_op jit(solution)/shard_map/slice | solution.py:42
  168.7 4.3 %pad_slice_fusion.9 = (bf16[64,96,256]{2,1,0:T(8,128)(2,1)S(1)}, bf16[64,96,256]{2,1,0:T(8,128)(2,1)S(1)}) fusion(bf16[64,96,256]{2,1,0:T(8,128)(2,1)S(1)} %fusion.49), kind=kLoop, calls=%fused_computation.114 | loop fusion | bytes 9437184 | tf_op jit(solution)/shard_map/slice | solution.py:42
  179.9 15.7 %reshape.417 = f32[4,16,16,6,8,32]{5,4,3,2,1,0:T(8,128)} reshape(f32[6144,256]{1,0:T(8,128)} %convolution_add_fusion) | data formatting | bytes 12582912 | tf_op jit(solution)/shard_map/reshape | solution.py:48
  195.5 44.1 %fusion.9 = bf16[16,8,6,4,16,32]{5,4,3,1,0,2:T(8,128)(2,1)} fusion(f32[4,16,16,6,8,32]{5,4,3,2,1,0:T(8,128)} %reshape.417, f32[4,16,16,6,8,32]{5,4,3,2,1,0:T(8,128)} %reshape.410), kind=kLoop, calls=%fused_computation.22 | loop fusion | flops 18874368 | bytes 15728640 | tf_op jit(solution)/shard_map/transpose | solution.py:126
  239.6 17.3 %reshape.418 = bf16[128,6,2048]{2,0,1:T(8,128)(2,1)} reshape(bf16[16,8,6,4,16,32]{5,4,3,1,0,2:T(8,128)(2,1)} %fusion.9) | data formatting | bytes 6291456 | tf_op jit(solution)/shard_map/reshape | solution.py:126
  257.0 5.6 %copy.65 = bf16[128,6,2048]{2,1,0:T(8,128)(2,1)} copy(bf16[128,6,2048]{2,0,1:T(8,128)(2,1)} %reshape.418) | data formatting | bytes 6291456 | tf_op jit(solution)/shard_map/reshape | solution.py:126
  262.6 6.1 %all-to-all-start.2 = ((bf16[128,6,2048]{2,1,0:T(8,128)(2,1)}), bf16[128,6,2048]{2,1,0:T(8,128)(2,1)}, u32[]{:S(2)}, u32[]{:S(2)}) async-start(bf16[128,6,2048]{2,1,0:T(8,128)(2,1)} %copy.65), calls=%async_computation.2 | async-start | bytes 8388608 | tf_op jit(solution)/shard_map/all_to_all | solution.py:129
  268.7 52.5 %all-to-all-done.2 = bf16[128,6,2048]{2,1,0:T(8,128)(2,1)} async-done(((bf16[128,6,2048]{2,1,0:T(8,128)(2,1)}), bf16[128,6,2048]{2,1,0:T(8,128)(2,1)}, u32[]{:S(2)}, u32[]{:S(2)}) %all-to-all-start.2) | async-done | bytes 3145760 | tf_op jit(solution)/shard_map/all_to_all | solution.py:129
  321.2 6.7 %copy_convert_fusion = f32[128,6,2048]{2,0,1:T(8,128)} fusion(bf16[128,6,2048]{2,1,0:T(8,128)(2,1)} %all-to-all-done.2), kind=kLoop, calls=%fused_computation.101 | loop fusion | flops 1572864 | bytes 9437184 | tf_op jit(solution)/shard_map/convert_element_type | solution.py:71
  327.9 16.1 %reshape.428 = f32[16,8,6,4,16,32]{5,4,3,1,0,2:T(8,128)} reshape(f32[128,6,2048]{2,0,1:T(8,128)} %copy_convert_fusion) | data formatting | bytes 12582912 | tf_op jit(solution)/shard_map/convert_element_type | solution.py:71
  344.0 17.6 %copy.67 = f32[6,32,16,4,8,16]{1,5,4,3,2,0:T(8,128)} copy(f32[6,32,16,4,8,16]{1,5,3,4,2,0:T(8,128)} %bitcast.78) | data formatting | bytes 12582912 | tf_op jit(solution)/shard_map/convert_element_type | solution.py:71
  361.6 17.2 %copy.69 = f32[6,32,64,128]{3,2,1,0:T(8,128)} copy(f32[6,32,64,128]{1,3,2,0:T(8,128)} %bitcast.79) | data formatting | bytes 12582912 | tf_op jit(solution)/shard_map/convert_element_type | solution.py:71
  378.8 24.7 %fusion.75 = bf16[6,32,64,128]{3,2,1,0:T(8,128)(2,1)} fusion(f32[6,32,64,128]{3,2,1,0:T(8,128)} %copy.69, f32[32]{0:T(128)S(1)} %get-tuple-element.20, f32[32]{0:T(128)S(1)} %get-tuple-element.21, f32[32]{0:T(128)S(1)} %get-tuple-element.14, f32[32]{0:T(128)S(1)} %get-tuple-element.15, f32[32]{0:T(128)S(1)} %get-tuple-element.16, ...), kind=kLoop, calls=%fused_computation.99 | loop fusion | flops 29884416 | bytes 9438336 | tf_op jit(solution)/shard_map/convert_element_type | solution.py:85
  (109 shorter events, 51.8 us)
Async XLA Ops:
  0.0 25.7 %copy-start = (bf16[512,1536]{1,0:T(8,128)(2,1)S(1)}, bf16[512,1536]{1,0:T(8,128)(2,1)}, u32[]{:S(2)}) copy-start(bf16[512,1536]{1,0:T(8,128)(2,1)} %param.8) | copy-start | bytes 4718596
  27.8 7.5 %copy-start.6 = (s32[4,16,4]{1,2,0:T(4,128)S(1)}, s32[4,16,4]{1,2,0:T(4,128)}, u32[]{:S(2)}) copy-start(s32[4,16,4]{1,2,0:T(4,128)} %param.9) | copy-start | bytes 3076
  27.8 7.6 %copy-start.7 = (s32[4,16]{1,0:T(4,128)S(1)}, s32[4,16]{1,0:T(4,128)}, u32[]{:S(2)}) copy-start(s32[4,16]{1,0:T(4,128)} %param.10) | copy-start | bytes 772
  27.8 9.2 %copy-start.9 = (bf16[8,64]{1,0:T(8,128)(2,1)S(1)}, bf16[8,64]{1,0:T(8,128)(2,1)}, u32[]{:S(2)}) copy-start(bf16[8,64]{1,0:T(8,128)(2,1)} %param.11) | copy-start | bytes 3076
  30.3 29.5 %all-to-all-start.1 = ((bf16[128,4,1536]{2,1,0:T(4,128)(2,1)}), bf16[128,4,1536]{2,1,0:T(4,128)(2,1)S(1)}, u32[]{:S(2)}, u32[]{:S(2)}) async-start(bf16[128,4,1536]{2,1,0:T(4,128)(2,1)} %broadcast_select_fusion), calls=%async_computation.1 | async-start | bytes 3145728 | tf_op jit(solution)/shard_map/all_to_all | solution.py:114
  62.1 8.1 %copy-start.2 = (bf16[256,32,64]{0,2,1:T(8,128)(2,1)S(1)}, bf16[256,32,64]{0,2,1:T(8,128)(2,1)}, u32[]{:S(2)}) copy-start(bf16[256,32,64]{0,2,1:T(8,128)(2,1)} %convolution_convert_fusion) | copy-start | bytes 3145732
  116.1 9.9 %copy-start.5 = (bf16[512,256]{1,0:T(8,128)(2,1)S(1)}, bf16[512,256]{1,0:T(8,128)(2,1)}, u32[]{:S(2)}) copy-start(bf16[512,256]{1,0:T(8,128)(2,1)} %param.12) | copy-start | bytes 786436
  156.3 4.2 %copy-start.3 = (bf16[768,256]{1,0:T(8,128)(2,1)S(1)}, bf16[768,256]{1,0:T(8,128)(2,1)}, u32[]{:S(2)}) copy-start(bf16[768,256]{1,0:T(8,128)(2,1)} %param.13) | copy-start | bytes 1179652
  160.4 2.2 slice-start
  160.5 2.9 slice-start.1
  168.7 4.3 %copy-start.4 = (bf16[768,256]{1,0:T(8,128)(2,1)S(1)}, bf16[768,256]{1,0:T(8,128)(2,1)}, u32[]{:S(2)}) copy-start(bf16[768,256]{1,0:T(8,128)(2,1)} %param.14) | copy-start | bytes 1179652
  257.0 11.7 %copy-start.8 = (f32[32,9]{0,1:T(8,128)S(1)}, f32[32,9]{0,1:T(8,128)}, u32[]{:S(2)}) copy-start(f32[32,9]{0,1:T(8,128)} %param.15) | copy-start | bytes 3460
  262.6 58.6 %all-to-all-start.2 = ((bf16[128,6,2048]{2,1,0:T(8,128)(2,1)}), bf16[128,6,2048]{2,1,0:T(8,128)(2,1)}, u32[]{:S(2)}, u32[]{:S(2)}) async-start(bf16[128,6,2048]{2,1,0:T(8,128)(2,1)} %copy.65), calls=%async_computation.2 | async-start | bytes 8388608 | tf_op jit(solution)/shard_map/all_to_all | solution.py:129
  361.6 41.9 %copy-start.1 = (bf16[512,1536]{1,0:T(8,128)(2,1)S(1)}, bf16[512,1536]{1,0:T(8,128)(2,1)}, u32[]{:S(2)}) copy-start(bf16[512,1536]{1,0:T(8,128)(2,1)} %param.8) | copy-start | bytes 4718596
where the time goes:
time: 411 us; the launch traced here: 404 us
  local copies, waits for them, and re-layouts  178 us (43%)
  other arithmetic  92.9 us (23%)
  waiting for transfers between devices  73.7 us (18%)
  matrix products  27 us (7%)
  blocking collectives  20.8 us (5%)
  starting transfers between devices  11 us (3%)
    all_to_all x1, waiting for transfers between devices, per_device(): lax.all_to_all(outgoing, ('il', 'xl'), split_axis=0, concat_axis=0, tiled...  52.5 us
    convert_element_type x3, local copies, waits for them, and re-layouts, lateral_mix(): field_values = block_values.astype(jnp.float32)  50.9 us
    transpose x1, other arithmetic, per_device(): tiled.transpose(2, 4, 3, 0, 1, 5)  44.1 us
    reshape x3, local copies, waits for them, and re-layouts, first_conv(): return result.reshape(batch_rows, length // 4, out_channels)  28.3 us
    convert_element_type x1, other arithmetic, lateral_mix(): return mixed_sum.astype(jnp.bfloat16)  24.7 us
    reshape x2, local copies, waits for them, and re-layouts, per_device(): tiled.transpose(2, 4, 3, 0, 1, 5)  23 us
    all_to_all x1, waiting for transfers between devices, per_device(): lax.all_to_all(picked, ('il', 'xl'), split_axis=0, concat_axis=0, tiled=T...  21.3 us
    all_to_all x1, blocking collectives, per_device(): lax.all_to_all(requests, ('il', 'xl'), split_axis=0, concat_axis=0, tiled...  20.8 us
  transfers between devices with their start and end apart: 2, of which 2 were waited for; matrix products, arithmetic and copies ran while one was open for 1% of the time, Pallas kernels for 0%

commit v1 on v0

v1 whole, which is shorter than its diff:
```python
import functools

import jax
import jax.numpy as jnp
import numpy as np
from jax import lax
from jax.experimental import pallas as pl
from jax.experimental.pallas import tpu as pltpu
from jax.sharding import PartitionSpec as P


def stack_rows(gathered, counts):
    running = jnp.zeros((gathered.shape[0], gathered.shape[2]), jnp.float32)
    for slot_index in range(gathered.shape[1]):
        live_mask = (slot_index < counts)[:, None]
        running = running + jnp.where(
            live_mask, gathered[:, slot_index].astype(jnp.float32), jnp.float32(0.0)
        )
    return (running / counts.astype(jnp.float32)[:, None]).astype(jnp.bfloat16)


def lateral_mix(block_values, weight):
    field_values = block_values.astype(jnp.float32)
    rows_out = field_values.shape[-2]
    cols_out = field_values.shape[-1]
    widths = [(0, 0)] * (field_values.ndim - 2) + [(1, 1), (1, 1)]
    padded = jnp.pad(field_values, widths)
    mixed_sum = field_values
    for row_shift in range(3):
        for col_shift in range(3):
            tap_weight = weight[:, row_shift * 3 + col_shift][:, None, None]
            mixed_sum = (
                mixed_sum
                + tap_weight
                * padded[..., row_shift : row_shift + rows_out, col_shift : col_shift + cols_out]
            )
    return mixed_sum.astype(jnp.bfloat16)


def banded_first_weights(conv1_w):
    m_index = jnp.arange(32, dtype=jnp.int32)[:, None, None]
    u_index = jnp.arange(4, dtype=jnp.int32)[None, :, None]
    tap_index = jnp.arange(8, dtype=jnp.int32)[None, None, :]
    selector = (m_index - 4 * u_index - 12 == tap_index).astype(jnp.float32)
    return (
        jnp.einsum("muj,jc->muc", selector, conv1_w.astype(jnp.float32))
        .astype(jnp.bfloat16)
        .reshape(32, 4 * conv1_w.shape[1])
    )


def encoder_kernel(n_il, n_xl, bins, paired_ref, a1_ref, w2_ref, w3_ref, w4_ref, out_ref,
                   first_pad, second_pad, third_pad):
    rows = paired_ref.shape[0]
    width = w2_ref.shape[1]
    chunk = 8 * bins
    n_chunks = rows // chunk
    pair_rows = 2 * bins
    group = width // n_xl
    pairs_per_slab = out_ref.shape[2]
    f32 = jnp.float32

    zeros_pad = jnp.zeros((bins, width), jnp.bfloat16)
    first_pad[pl.ds(0, bins), :] = zeros_pad
    second_pad[pl.ds(0, bins), :] = zeros_pad
    second_pad[pl.ds(bins + rows, bins), :] = zeros_pad
    third_pad[pl.ds(0, bins), :] = zeros_pad
    third_pad[pl.ds(bins + rows, bins), :] = zeros_pad

    def gelu(x):
        return jax.nn.gelu(x)

    def layer1(ci, carry):
        r0 = pl.multiple_of(ci * chunk, chunk)
        x = paired_ref[pl.ds(r0, chunk), :]
        y = jnp.dot(x, a1_ref[...], preferred_element_type=f32)
        first_pad[pl.ds(bins + r0, chunk), :] = gelu(y).astype(jnp.bfloat16)
        return carry

    lax.fori_loop(0, n_chunks, layer1, 0)

    def layer2(ci, carry):
        r0 = pl.multiple_of(ci * chunk, chunk)
        earlier = first_pad[pl.ds(r0, chunk), :]
        current = first_pad[pl.ds(r0 + bins, chunk), :]
        y = jnp.dot(earlier, w2_ref[pl.ds(0, width), :], preferred_element_type=f32)
        y = y + jnp.dot(current, w2_ref[pl.ds(width, width), :], preferred_element_type=f32)
        second_pad[pl.ds(bins + r0, chunk), :] = gelu(y).astype(jnp.bfloat16)
        return carry

    lax.fori_loop(0, n_chunks, layer2, 0)

    def centred(src, w_ref, r0):
        y = jnp.dot(src[pl.ds(r0, chunk), :], w_ref[pl.ds(0, width), :], preferred_element_type=f32)
        y = y + jnp.dot(src[pl.ds(r0 + bins, chunk), :], w_ref[pl.ds(width, width), :],
                        preferred_element_type=f32)
        y = y + jnp.dot(src[pl.ds(r0 + 2 * bins, chunk), :], w_ref[pl.ds(2 * width, width), :],
                        preferred_element_type=f32)
        return y

    def layer3(ci, carry):
        r0 = pl.multiple_of(ci * chunk, chunk)
        y = centred(second_pad, w3_ref, r0)
        third_pad[pl.ds(bins + r0, chunk), :] = gelu(y).astype(jnp.bfloat16)
        return carry

    lax.fori_loop(0, n_chunks, layer3, 0)

    def layer4(ci, carry):
        r0 = pl.multiple_of(ci * chunk, chunk)
        y = centred(third_pad, w4_ref, r0)
        y = y + second_pad[pl.ds(bins + r0, chunk), :].astype(f32)
        feat = y.astype(jnp.bfloat16).astype(f32)
        for p in range(chunk // pair_rows):
            pair = ci * (chunk // pair_rows) + p
            slab = pair // pairs_per_slab
            within = pair % pairs_per_slab
            block = feat[p * pair_rows:(p + 1) * pair_rows, :].T
            out_ref[slab, :, within, :, :] = block.reshape(n_xl, group, pair_rows).astype(
                jnp.bfloat16)
        return carry

    lax.fori_loop(0, n_chunks, layer4, 0)


def encode_to_send(paired, a1, conv2_w, conv3_w, conv4_w, n_il, n_xl, bins, steps):
    rows = paired.shape[0]
    width = conv2_w.shape[1]
    out_shape = jax.ShapeDtypeStruct(
        (n_il, n_xl, steps // n_il // 2, width // n_xl, 2 * bins), jnp.bfloat16)
    return pl.pallas_call(
        functools.partial(encoder_kernel, n_il, n_xl, bins),
        out_shape=out_shape,
        in_specs=[pl.BlockSpec(memory_space=pltpu.VMEM)] * 5,
        out_specs=pl.BlockSpec(memory_space=pltpu.VMEM),
        scratch_shapes=[
            pltpu.VMEM((bins + rows, width), jnp.bfloat16),
            pltpu.VMEM((2 * bins + rows, width), jnp.bfloat16),
            pltpu.VMEM((2 * bins + rows, width), jnp.bfloat16),
        ],
        compiler_params=pltpu.CompilerParams(vmem_limit_bytes=48 * 1024 * 1024),
    )(paired, a1, conv2_w, conv3_w, conv4_w)


def per_device(traces, fold_ids, fold_counts, conv1_w, conv2_w, conv3_w, conv4_w, lateral_w):
    il_count = lax.axis_size("il")
    xl_count = lax.axis_size("xl")
    devices = il_count * xl_count
    rows_here = traces.shape[0]
    samples = traces.shape[1]
    bins_il, bins_xl, fold_depth = fold_ids.shape
    bin_total = bins_il * bins_xl
    slot_total = bin_total * fold_depth
    capacity = 2 * slot_total // devices
    flat_ids = fold_ids.reshape(slot_total)
    source = flat_ids // rows_here
    local_row = flat_ids % rows_here
    onehot = (source[:, None] == jnp.arange(devices, dtype=jnp.int32)[None, :]).astype(jnp.int32)
    slot_rank = jnp.sum(onehot * jnp.cumsum(onehot, axis=0), axis=1) - 1
    position = source * capacity + slot_rank
    requests = (
        jnp.zeros((devices * capacity,), jnp.int32)
        .at[position]
        .set(local_row)
        .reshape(devices, capacity)
    )
    wanted = lax.all_to_all(requests, ("il", "xl"), split_axis=0, concat_axis=0, tiled=True)
    picked = jnp.take(traces, wanted.reshape(-1), axis=0).reshape(
        wanted.shape[0], wanted.shape[1], samples
    )
    arrived = lax.all_to_all(picked, ("il", "xl"), split_axis=0, concat_axis=0, tiled=True)
    gathered = jnp.take(arrived.reshape(devices * capacity, samples), position, axis=0).reshape(
        bin_total, fold_depth, samples
    )
    stacked = stack_rows(gathered, fold_counts.reshape(bin_total))
    steps = samples // 16
    groups = stacked.reshape(bin_total, steps, 16).transpose(1, 0, 2)
    previous = jnp.pad(groups, ((1, 0), (0, 0), (0, 0)))[:steps]
    paired = jnp.concatenate([previous, groups], axis=2).reshape(steps * bin_total, 32)
    outgoing = encode_to_send(
        paired, banded_first_weights(conv1_w), conv2_w, conv3_w, conv4_w,
        il_count, xl_count, bin_total, steps,
    )
    pairs = outgoing.shape[2]
    group_width = outgoing.shape[3]
    outgoing = outgoing.reshape(devices, pairs, group_width, 2 * bin_total)
    received = lax.all_to_all(outgoing, ("il", "xl"), split_axis=0, concat_axis=0, tiled=True)
    placed = received.reshape(
        il_count, xl_count, pairs, group_width, 2, bins_il, bins_xl
    ).transpose(2, 4, 3, 0, 5, 1, 6)
    return lateral_mix(
        placed.reshape(2 * pairs, group_width, il_count * bins_il, xl_count * bins_xl), lateral_w
    )


def solution(mesh):
    return jax.shard_map(
        per_device,
        mesh=mesh,
        in_specs=(
            P(("il", "xl"), None),
            P("il", "xl", None),
            P("il", "xl"),
            P(),
            P(),
            P(),
            P(),
            P("xl", None),
        ),
        out_specs=P("il", "xl", None, None),
        check_vma=False,
    )
```

time: 411 us -> 208 us (0.51); the launches traced: 404 us -> 207 us
  local copies, waits for them, and re-layouts: 178 us -> 53.2 us
  other arithmetic: 92.9 us -> 36.6 us
  matrix products: 27 us -> 0.21 us
  Pallas kernels: 0 us -> 20 us
  waiting for transfers between devices: 73.7 us -> 64.8 us
    reshape x8 -> x1, local copies, waits for them, and re-layouts: 92.5 us -> 0.1 us  [banded_first_weights(): return jnp.einsum('muj,jc->muc', selector, conv1_w.astype(jnp.float32)).a...]
    transpose x1, other arithmetic: 44.1 us -> 0.34 us  [per_device(): groups = stacked.reshape(bin_total, steps, 16).transpose(1, 0, 2)]
    dot_general x10 -> x1, matrix products: 27 us -> 0.21 us  [banded_first_weights(): jnp.einsum('muj,jc->muc', selector, conv1_w.astype(jnp.float32))]
    convert_element_type x3 -> x2, local copies, waits for them, and re-layouts: 50.9 us -> 26.2 us  [lateral_mix(): field_values = block_values.astype(jnp.float32)]
    pallas_call x0 -> x1, Pallas kernels: none -> 20 us  [encode_to_send(): pl.pallas_call(functools.partial(encoder_kernel, n_il, n_xl, bins), out_s...]
    slice x5 -> x2, local copies, waits for them, and re-layouts: 18.5 us -> 0.18 us  [the longest x1 0.1 us: stack_rows(): gathered[:, slot_index].astype(jnp.float32)]
    all_to_all x1, waiting for transfers between devices: 52.5 us -> 41.5 us  [per_device(): lax.all_to_all(outgoing, ('il', 'xl'), split_axis=0, concat_axis=0, tiled...]
    all_to_all x0 -> x1, local copies, waits for them, and re-layouts: none -> 10.6 us  [per_device(): lax.all_to_all(outgoing, ('il', 'xl'), split_axis=0, concat_axis=0, tiled...]
where the time goes in v1:
time: 208 us; the launch traced here: 207 us
  waiting for transfers between devices  64.8 us (31%)
  local copies, waits for them, and re-layouts  53.2 us (26%)
  other arithmetic  36.6 us (18%)
  blocking collectives  20.8 us (10%)
  Pallas kernels  20 us (10%)
  starting transfers between devices  11 us (5%)
    all_to_all x1, waiting for transfers between devices, per_device(): lax.all_to_all(outgoing, ('il', 'xl'), split_axis=0, concat_axis=0, tiled...  41.5 us
    convert_element_type x2, local copies, waits for them, and re-layouts, lateral_mix(): field_values = block_values.astype(jnp.float32)  26.2 us
    convert_element_type x1, other arithmetic, lateral_mix(): return mixed_sum.astype(jnp.bfloat16)  24.5 us
    all_to_all x1, waiting for transfers between devices, per_device(): lax.all_to_all(picked, ('il', 'xl'), split_axis=0, concat_axis=0, tiled=T...  23.3 us
    all_to_all x1, blocking collectives, per_device(): lax.all_to_all(requests, ('il', 'xl'), split_axis=0, concat_axis=0, tiled...  20.8 us
    pallas_call x1, Pallas kernels, encode_to_send(): pl.pallas_call(functools.partial(encoder_kernel, n_il, n_xl, bins), out_s...  20 us
    all_to_all x1, local copies, waits for them, and re-layouts, per_device(): lax.all_to_all(outgoing, ('il', 'xl'), split_axis=0, concat_axis=0, tiled...  10.6 us
    convert_element_type x1, other arithmetic, lateral_mix(): field_values = block_values.astype(jnp.float32)  7.16 us
  transfers between devices with their start and end apart: 2, of which 2 were waited for; matrix products, arithmetic and copies ran while one was open for 1% of the time, Pallas kernels for 0%

profile of v1, /device:TPU:1, one launch (start us, length us, event | category | flops | bytes accessed | tf_op | source)
XLA Modules:
  0.0 207.1 jit_solution(18035012427762841190)
XLA Ops:
  0.0 0.9 copy.39
  1.9 1.4 scatter_custom_fusion
  3.4 20.8 %all_to_all.19 = s32[128,1,4]{2,1,0:T(1,128)S(1)} all-to-all(s32[128,1,4]{2,1,0:T(1,128)S(1)} %bitcast.66), channel_id=1, replica_groups=mesh['il'=16,'xl'=8] {'il','xl'}, dimensions={0} | all-to-all | bytes 4096 | tf_op jit(solution)/shard_map/all_to_all | solution.py:167
  24.2 0.5 broadcast.352
  24.7 0.8 reduce.3
  25.7 2.1 %gather_fusion = bf16[512,1536]{1,0:T(8,128)(2,1)S(1)} fusion(bf16[512,1536]{1,0:T(8,128)(2,1)S(1)} %copy-done, s32[1024]{0:T(1024)S(1)} %pad_clamp_fusion.1), kind=kCustom, calls=%fused_computation | custom fusion | bytes 3147776 | tf_op jit(solution)/shard_map/jit(_take)/gather | solution.py:168
  27.9 0.4 gather.13
  28.3 2.0 broadcast_select_fusion
  30.3 5.3 %all-to-all-start.1 = ((bf16[128,4,1536]{2,1,0:T(4,128)(2,1)}), bf16[128,4,1536]{2,1,0:T(4,128)(2,1)}, u32[]{:S(2)}, u32[]{:S(2)}) async-start(bf16[128,4,1536]{2,1,0:T(4,128)(2,1)} %broadcast_select_fusion), calls=%async_computation.1 | async-start | bytes 3145728 | tf_op jit(solution)/shard_map/all_to_all | solution.py:171
  36.8 23.3 %all-to-all-done.1 = bf16[128,4,1536]{2,1,0:T(4,128)(2,1)} async-done(((bf16[128,4,1536]{2,1,0:T(4,128)(2,1)}), bf16[128,4,1536]{2,1,0:T(4,128)(2,1)}, u32[]{:S(2)}, u32[]{:S(2)}) %all-to-all-start.1) | async-done | bytes 1572896 | tf_op jit(solution)/shard_map/all_to_all | solution.py:171
  60.1 2.7 %reshape.338 = bf16[512,1536]{1,0:T(8,128)(2,1)S(1)} reshape(bf16[128,4,1536]{2,1,0:T(4,128)(2,1)} %all-to-all-done.1) | data formatting | bytes 3145728 | tf_op jit(solution)/shard_map/reshape | solution.py:172
  62.9 2.1 %gather_fusion.1 = bf16[256,1536]{1,0:T(8,128)(2,1)} fusion(bf16[512,1536]{1,0:T(8,128)(2,1)S(1)} %reshape.338, s32[1024]{0:T(1024)S(1)} %pad_clamp_fusion), kind=kCustom, calls=%fused_computation.1 | custom fusion | bytes 1573888 | tf_op jit(solution)/shard_map/jit(_take)/gather | solution.py:172
  65.0 1.7 gather.15
  66.7 0.9 copy.46
  68.4 1.0 pad_maximum_fusion
  69.4 1.8 copy.47
  71.2 20.0 %shard_map.82 = bf16[16,8,3,32,128]{4,3,2,1,0:T(8,128)(2,1)} custom-call(bf16[6144,32]{1,0:T(8,128)(2,1)S(1)} %bitcast.56, bf16[32,256]{1,0:T(8,128)(2,1)S(1)} %reshape.340.a1_ref, bf16[512,256]{1,0:T(8,128)(2,1)S(1)} %copy-done.4, bf16[768,256]{1,0:T(8,128)(2,1)S(1)} %copy-done.2, bf16[768,256]{1,0:T(8,128)(2,1)S(1)} %copy-done.3), custom_call_target="tpu_custom_call" | custom-call | tf_op jit(solution)/shard_map/pallas_call | solution.py:131
  91.3 5.7 %all-to-all-start.2 = ((bf16[128,3,32,128]{3,2,1,0:T(8,128)(2,1)}), bf16[128,3,32,128]{3,2,1,0:T(8,128)(2,1)}, u32[]{:S(2)}, u32[]{:S(2)}) async-start(bf16[128,3,32,128]{3,2,1,0:T(8,128)(2,1)} %bitcast.15), calls=%async_computation.2 | async-start | bytes 6291456 | tf_op jit(solution)/shard_map/all_to_all | solution.py:187
  97.0 41.5 %all-to-all-done.2 = bf16[128,3,32,128]{3,2,1,0:T(8,128)(2,1)} async-done(((bf16[128,3,32,128]{3,2,1,0:T(8,128)(2,1)}), bf16[128,3,32,128]{3,2,1,0:T(8,128)(2,1)}, u32[]{:S(2)}, u32[]{:S(2)}) %all-to-all-start.2) | async-done | bytes 3145760 | tf_op jit(solution)/shard_map/all_to_all | solution.py:187
  138.5 10.6 %copy.49 = bf16[128,3,32,128]{2,3,1,0:T(8,128)(2,1)} copy(bf16[128,3,32,128]{3,2,1,0:T(8,128)(2,1)} %all-to-all-done.2) | data formatting | bytes 6291456 | tf_op jit(solution)/shard_map/all_to_all | solution.py:187
  149.1 7.2 %convert_bitcast_fusion = f32[3,2,32,16,4,8,16]{2,6,4,1,0,5,3:T(8,128)S(1)} fusion(bf16[16,8,3,32,2,4,16]{3,6,5,4,2,1,0:T(8,128)(2,1)} %bitcast.58), kind=kLoop, calls=%fused_computation.11 | loop fusion | flops 1572864 | bytes 9437184 | tf_op jit(solution)/shard_map/convert_element_type | solution.py:23
  156.3 9.0 %copy.50 = f32[3,2,32,16,4,8,16]{2,6,5,4,3,1,0:T(8,128)} copy(f32[3,2,32,16,4,8,16]{2,6,4,1,0,5,3:T(8,128)S(1)} %convert_bitcast_fusion) | data formatting | bytes 12582912 | tf_op jit(solution)/shard_map/convert_element_type | solution.py:23
  165.3 17.2 %copy.52 = f32[6,32,64,128]{3,2,1,0:T(8,128)} copy(f32[6,32,64,128]{1,3,2,0:T(8,128)} %bitcast.57) | data formatting | bytes 12582912 | tf_op jit(solution)/shard_map/convert_element_type | solution.py:23
  182.5 24.5 %fusion.17 = bf16[6,32,64,128]{3,2,1,0:T(8,128)(2,1)} fusion(f32[6,32,64,128]{3,2,1,0:T(8,128)} %copy.52, f32[32]{0:T(128)S(1)} %get-tuple-element.16, f32[32]{0:T(128)S(1)} %get-tuple-element.17, f32[32]{0:T(128)S(1)} %get-tuple-element.10, f32[32]{0:T(128)S(1)} %get-tuple-element.11, f32[32]{0:T(128)S(1)} %get-tuple-element.12, ...), kind=kLoop, calls=%fused_computation.29 | loop fusion | flops 29884416 | bytes 9438336 | tf_op jit(solution)/shard_map/convert_element_type | solution.py:37
  (62 shorter events, 3.0 us)
Async XLA Ops:
  0.0 25.7 %copy-start = (bf16[512,1536]{1,0:T(8,128)(2,1)S(1)}, bf16[512,1536]{1,0:T(8,128)(2,1)}, u32[]{:S(2)}) copy-start(bf16[512,1536]{1,0:T(8,128)(2,1)} %param.8) | copy-start | bytes 4718596
  27.8 7.9 %copy-start.5 = (s32[4,16,4]{1,2,0:T(4,128)S(1)}, s32[4,16,4]{1,2,0:T(4,128)}, u32[]{:S(2)}) copy-start(s32[4,16,4]{1,2,0:T(4,128)} %param.9) | copy-start | bytes 3076
  27.8 8.1 %copy-start.6 = (s32[4,16]{1,0:T(4,128)S(1)}, s32[4,16]{1,0:T(4,128)}, u32[]{:S(2)}) copy-start(s32[4,16]{1,0:T(4,128)} %param.10) | copy-start | bytes 772
  27.8 8.6 %copy-start.8 = (bf16[8,64]{1,0:T(8,128)(2,1)S(1)}, bf16[8,64]{1,0:T(8,128)(2,1)}, u32[]{:S(2)}) copy-start(bf16[8,64]{1,0:T(8,128)(2,1)} %param.11) | copy-start | bytes 3076
  30.3 29.9 %all-to-all-start.1 = ((bf16[128,4,1536]{2,1,0:T(4,128)(2,1)}), bf16[128,4,1536]{2,1,0:T(4,128)(2,1)}, u32[]{:S(2)}, u32[]{:S(2)}) async-start(bf16[128,4,1536]{2,1,0:T(4,128)(2,1)} %broadcast_select_fusion), calls=%async_computation.1 | async-start | bytes 3145728 | tf_op jit(solution)/shard_map/all_to_all | solution.py:171
  67.6 3.6 %copy-start.2 = (bf16[768,256]{1,0:T(8,128)(2,1)S(1)}, bf16[768,256]{1,0:T(8,128)(2,1)}, u32[]{:S(2)}) copy-start(bf16[768,256]{1,0:T(8,128)(2,1)} %w3_ref.1) | copy-start | bytes 1179652
  67.7 3.6 %copy-start.3 = (bf16[768,256]{1,0:T(8,128)(2,1)S(1)}, bf16[768,256]{1,0:T(8,128)(2,1)}, u32[]{:S(2)}) copy-start(bf16[768,256]{1,0:T(8,128)(2,1)} %w4_ref.1) | copy-start | bytes 1179652
  67.7 3.6 %copy-start.4 = (bf16[512,256]{1,0:T(8,128)(2,1)S(1)}, bf16[512,256]{1,0:T(8,128)(2,1)}, u32[]{:S(2)}) copy-start(bf16[512,256]{1,0:T(8,128)(2,1)} %w2_ref.1) | copy-start | bytes 786436
  71.2 25.7 %copy-start.7 = (f32[32,9]{0,1:T(8,128)S(1)}, f32[32,9]{0,1:T(8,128)}, u32[]{:S(2)}) copy-start(f32[32,9]{0,1:T(8,128)} %param.15) | copy-start | bytes 3460
  91.3 47.2 %all-to-all-start.2 = ((bf16[128,3,32,128]{3,2,1,0:T(8,128)(2,1)}), bf16[128,3,32,128]{3,2,1,0:T(8,128)(2,1)}, u32[]{:S(2)}, u32[]{:S(2)}) async-start(bf16[128,3,32,128]{3,2,1,0:T(8,128)(2,1)} %bitcast.15), calls=%async_computation.2 | async-start | bytes 6291456 | tf_op jit(solution)/shard_map/all_to_all | solution.py:187
  165.3 41.7 %copy-start.1 = (bf16[512,1536]{1,0:T(8,128)(2,1)S(1)}, bf16[512,1536]{1,0:T(8,128)(2,1)}, u32[]{:S(2)}) copy-start(bf16[512,1536]{1,0:T(8,128)(2,1)} %param.8) | copy-start | bytes 4718596

commit v2 on v1

--- a/solution.py
+++ b/solution.py
@@ -140,6 +140,82 @@
         ],
         compiler_params=pltpu.CompilerParams(vmem_limit_bytes=48 * 1024 * 1024),
     )(paired, a1, conv2_w, conv3_w, conv4_w)
+
+
+def merge_selectors(n_xl, lanes):
+    width = lanes // n_xl
+    kk = jnp.arange(2 * lanes, dtype=jnp.int32)[None, :, None]
+    m = jnp.arange(n_xl * lanes, dtype=jnp.int32)[None, None, :]
+    bp = jnp.arange(n_xl // 2, dtype=jnp.int32)[:, None, None]
+    b = 2 * bp + kk // lanes
+    lane = kk % lanes
+    target = (lane // width) * lanes + width * b + lane % width
+    return (m == target).astype(jnp.bfloat16)
+
+
+def receive_kernel(recv_ref, sel_ref, lw_ref, out_ref, field):
+    n_a, n_b, rows_k_o, lanes = recv_ref.shape
+    n_s, n_o, n_p, n_q = out_ref.shape
+    n_k = rows_k_o // n_o
+    width = n_q // n_b
+    n_p4 = n_p // n_a
+    f32 = jnp.float32
+
+    def merge(a, carry):
+        y = None
+        for bp in range(n_b // 2):
+            x = jnp.concatenate([recv_ref[a, 2 * bp], recv_ref[a, 2 * bp + 1]], axis=1)
+            d = jnp.dot(x, sel_ref[bp], preferred_element_type=f32)
+            y = d if y is None else y + d
+        for k in range(n_k):
+            for s2 in range(2):
+                for p4 in range(n_p4):
+                    blk = y[k * n_o:(k + 1) * n_o, (s2 * n_p4 + p4) * lanes:(s2 * n_p4 + p4 + 1) * lanes]
+                    start = (2 * k + s2) * n_o * n_p + n_p4 * a + p4
+                    field[pl.ds(start, n_o, stride=n_p), :] = blk
+        return carry
+
+    lax.fori_loop(0, n_a, merge, 0)
+
+    row = lax.broadcasted_iota(jnp.int32, (n_p, n_q), 0)
+    col = lax.broadcasted_iota(jnp.int32, (n_p, n_q), 1)
+    zero = jnp.zeros((n_p, n_q), f32)
+
+    def mix(plane, carry):
+        s = plane // n_o
+        o = plane % n_o
+        f = field[pl.ds(pl.multiple_of(plane * n_p, n_p), n_p), :]
+        shifted_rows = [
+            jnp.where(row == 0, zero, pltpu.roll(f, 1, 0)),
+            f,
+            jnp.where(row == n_p - 1, zero, pltpu.roll(f, n_p - 1, 0)),
+        ]
+        acc = f
+        for r in range(3):
+            g = shifted_rows[r]
+            taps = [
+                jnp.where(col == 0, zero, pltpu.roll(g, 1, 1)),
+                g,
+                jnp.where(col == n_q - 1, zero, pltpu.roll(g, n_q - 1, 1)),
+            ]
+            for c in range(3):
+                acc = acc + lw_ref[o, 3 * r + c] * taps[c]
+        out_ref[s, o] = acc.astype(out_ref.dtype)
+        return carry
+
+    lax.fori_loop(0, n_s * n_o, mix, 0)
+
+
+def receive_mix(received, sel, lw, n_s, n_o, n_p, n_q):
+    return pl.pallas_call(
+        receive_kernel,
+        out_shape=jax.ShapeDtypeStruct((n_s, n_o, n_p, n_q), jnp.bfloat16),
+        in_specs=[pl.BlockSpec(memory_space=pltpu.VMEM), pl.BlockSpec(memory_space=pltpu.VMEM),
+                  pl.BlockSpec(memory_space=pltpu.SMEM)],
+        out_specs=pl.BlockSpec(memory_space=pltpu.VMEM),
+        scratch_shapes=[pltpu.VMEM((n_s * n_o * n_p, n_q), jnp.float32)],
+        compiler_params=pltpu.CompilerParams(vmem_limit_bytes=48 * 1024 * 1024),
+    )(received, sel, lw)
 
 
 def per_device(traces, fold_ids, fold_counts, conv1_w, conv2_w, conv3_w, conv4_w, lateral_w):
@@ -185,11 +261,10 @@
     group_width = outgoing.shape[3]
     outgoing = outgoing.reshape(devices, pairs, group_width, 2 * bin_total)
     received = lax.all_to_all(outgoing, ("il", "xl"), split_axis=0, concat_axis=0, tiled=True)
-    placed = received.reshape(
-        il_count, xl_count, pairs, group_width, 2, bins_il, bins_xl
-    ).transpose(2, 4, 3, 0, 5, 1, 6)
-    return lateral_mix(
-        placed.reshape(2 * pairs, group_width, il_count * bins_il, xl_count * bins_xl), lateral_w
+    received = received.reshape(il_count, xl_count, pairs * group_width, 2 * bin_total)
+    return receive_mix(
+        received, merge_selectors(xl_count, 2 * bin_total), lateral_w,
+        2 * pairs, group_width, il_count * bins_il, xl_count * bins_xl,
     )
 
 

time: 208 us -> 185 us (0.89)
  Pallas kernels: 20 us -> 55.9 us
  other arithmetic: 36.6 us -> 6.78 us
  local copies, waits for them, and re-layouts: 53.2 us -> 26.4 us
    pallas_call x0 -> x1, Pallas kernels: none -> 37.6 us  [receive_mix(): pl.pallas_call(receive_kernel, out_shape=jax.ShapeDtypeStruct((n_s, n_o,...]
    convert_element_type x2 -> x1, other arithmetic: 31.7 us -> 1.76 us  [merge_selectors(): return (m == target).astype(jnp.bfloat16)]
    convert_element_type x2 -> x0, local copies, waits for them, and re-layouts: 26.2 us -> none  [lateral_mix(): field_values = block_values.astype(jnp.float32)]
    all_to_all x1 -> x0, local copies, waits for them, and re-layouts: 10.6 us -> none  [per_device(): lax.all_to_all(outgoing, ('il', 'xl'), split_axis=0, concat_axis=0, tiled...]
    unnamed x21 -> x24, local copies, waits for them, and re-layouts: 0.97 us -> 6.22 us
    gather x2, local copies, waits for them, and re-layouts: 2.53 us -> 5.81 us  [per_device(): jnp.take(traces, wanted.reshape(-1), axis=0)]
  transfers between devices with their start and end apart: 2 -> 2, of which waited for: 2 -> 2; matrix products, arithmetic and copies ran while one was open for 1% -> 2% of each run, Pallas kernels for 0% -> 0%
where the time goes in v2:
time: 185 us
  waiting for transfers between devices  62.9 us (34%)
  Pallas kernels  55.9 us (30%)
  local copies, waits for them, and re-layouts  26.4 us (14%)
  blocking collectives  20.8 us (11%)
  starting transfers between devices  11.2 us (6%)
  other arithmetic  6.78 us (4%)
    all_to_all x1, waiting for transfers between devices, per_device(): lax.all_to_all(outgoing, ('il', 'xl'), split_axis=0, concat_axis=0, tiled...  39.6 us
    pallas_call x1, Pallas kernels, receive_mix(): pl.pallas_call(receive_kernel, out_shape=jax.ShapeDtypeStruct((n_s, n_o,...  37.6 us
    all_to_all x1, waiting for transfers between devices, per_device(): lax.all_to_all(picked, ('il', 'xl'), split_axis=0, concat_axis=0, tiled=T...  23.3 us
    all_to_all x1, blocking collectives, per_device(): lax.all_to_all(requests, ('il', 'xl'), split_axis=0, concat_axis=0, tiled...  20.8 us
    pallas_call x1, Pallas kernels, encode_to_send(): pl.pallas_call(functools.partial(encoder_kernel, n_il, n_xl, bins), out_s...  18.4 us
    gather x3, local copies, waits for them, and re-layouts, per_device(): jnp.take(arrived.reshape(devices * capacity, samples), position, axis=0)  6.32 us
    unnamed x24, local copies, waits for them, and re-layouts  6.22 us
    gather x2, local copies, waits for them, and re-layouts, per_device(): jnp.take(traces, wanted.reshape(-1), axis=0)  5.81 us
  transfers between devices with their start and end apart: 2, of which 2 were waited for; matrix products, arithmetic and copies ran while one was open for 2% of the time, Pallas kernels for 0%

profile of v2, /device:TPU:1, one launch (start us, length us, event | category | flops | bytes accessed | tf_op | source)
XLA Modules:
  0.0 184.6 jit_solution(9263824497173318398)
XLA Ops:
  0.0 0.9 copy.23
  1.9 1.4 scatter_custom_fusion
  3.4 20.8 %all_to_all.19 = s32[128,1,4]{2,1,0:T(1,128)S(1)} all-to-all(s32[128,1,4]{2,1,0:T(1,128)S(1)} %bitcast.44), channel_id=1, replica_groups=mesh['il'=16,'xl'=8] {'il','xl'}, dimensions={0} | all-to-all | bytes 4096 | tf_op jit(solution)/shard_map/all_to_all | solution.py:243
  24.8 0.8 reduce.3
  25.7 2.9 %gather_fusion = bf16[512,1536]{1,0:T(8,128)(2,1)} fusion(bf16[512,1536]{1,0:T(8,128)(2,1)S(1)} %copy-done, s32[1024]{0:T(1024)S(1)} %pad_clamp_fusion.1), kind=kCustom, calls=%fused_computation | custom fusion | bytes 3147776 | tf_op jit(solution)/shard_map/jit(_take)/gather | solution.py:244
  28.6 2.9 %gather.13 = bf16[128,4,1536]{2,1,0:T(4,128)(2,1)S(1)} reshape(bf16[512,1536]{1,0:T(8,128)(2,1)} %gather_fusion) | data formatting | bytes 3145728 | tf_op jit(solution)/shard_map/jit(_take)/gather | solution.py:244
  31.5 2.0 %broadcast_select_fusion = bf16[128,4,1536]{2,1,0:T(4,128)(2,1)} fusion(bf16[128,4,1536]{2,1,0:T(4,128)(2,1)S(1)} %gather.13, pred[128,4]{1,0:T(8,128)(4,1)S(1)} %compare_and_fusion), kind=kLoop, calls=%fused_computation.5 | loop fusion | flops 786432 | bytes 3146240 | tf_op jit(solution)/shard_map/jit(_take)/select_n | solution.py:244
  33.5 5.4 %all-to-all-start.1 = ((bf16[128,4,1536]{2,1,0:T(4,128)(2,1)}), bf16[128,4,1536]{2,1,0:T(4,128)(2,1)}, u32[]{:S(2)}, u32[]{:S(2)}) async-start(bf16[128,4,1536]{2,1,0:T(4,128)(2,1)} %broadcast_select_fusion), calls=%async_computation.1 | async-start | bytes 3145728 | tf_op jit(solution)/shard_map/all_to_all | solution.py:247
  40.2 23.3 %all-to-all-done.1 = bf16[128,4,1536]{2,1,0:T(4,128)(2,1)} async-done(((bf16[128,4,1536]{2,1,0:T(4,128)(2,1)}), bf16[128,4,1536]{2,1,0:T(4,128)(2,1)}, u32[]{:S(2)}, u32[]{:S(2)}) %all-to-all-start.1) | async-done | bytes 1572896 | tf_op jit(solution)/shard_map/all_to_all | solution.py:247
  63.5 2.7 %reshape.502 = bf16[512,1536]{1,0:T(8,128)(2,1)S(1)} reshape(bf16[128,4,1536]{2,1,0:T(4,128)(2,1)} %all-to-all-done.1) | data formatting | bytes 3145728 | tf_op jit(solution)/shard_map/reshape | solution.py:248
  66.2 2.1 %gather_fusion.1 = bf16[256,1536]{1,0:T(8,128)(2,1)} fusion(bf16[512,1536]{1,0:T(8,128)(2,1)S(1)} %reshape.502, s32[1024]{0:T(1024)S(1)} %pad_clamp_fusion), kind=kCustom, calls=%fused_computation.1 | custom fusion | bytes 1573888 | tf_op jit(solution)/shard_map/jit(_take)/gather | solution.py:248
  68.4 2.4 %gather.15 = bf16[64,4,1536]{2,1,0:T(4,128)(2,1)} reshape(bf16[256,1536]{1,0:T(8,128)(2,1)} %gather_fusion.1) | data formatting | bytes 1572864 | tf_op jit(solution)/shard_map/jit(_take)/gather | solution.py:248
  70.8 1.8 copy.30
  73.3 1.0 pad_maximum_fusion
  74.3 1.8 copy.31
  76.2 1.0 copy-done.4
  77.2 0.9 copy-done.5
  78.1 18.4 %shard_map.82 = bf16[16,8,3,32,128]{4,3,2,1,0:T(8,128)(2,1)S(1)} custom-call(bf16[6144,32]{1,0:T(8,128)(2,1)S(1)} %bitcast.36, bf16[32,256]{1,0:T(8,128)(2,1)S(1)} %reshape.504.a1_ref, bf16[512,256]{1,0:T(8,128)(2,1)S(1)} %copy-done.5, bf16[768,256]{1,0:T(8,128)(2,1)S(1)} %copy-done.3, bf16[768,256]{1,0:T(8,128)(2,1)S(1)} %copy-done.4), custom_call_target="tpu_custom_call" | custom-call | tf_op jit(solution)/shard_map/pallas_call | solution.py:131
  96.5 1.7 copy-done.1
  98.1 5.8 %all-to-all-start.2 = ((bf16[128,3,32,128]{3,2,1,0:T(8,128)(2,1)}), bf16[128,3,32,128]{3,2,1,0:T(8,128)(2,1)}, u32[]{:S(2)}, u32[]{:S(2)}) async-start(bf16[128,3,32,128]{3,2,1,0:T(8,128)(2,1)} %bitcast.35), calls=%async_computation.2 | async-start | bytes 6291456 | tf_op jit(solution)/shard_map/all_to_all | solution.py:263
  104.1 1.8 fusion.sel_ref
  105.9 39.6 %all-to-all-done.2 = bf16[128,3,32,128]{3,2,1,0:T(8,128)(2,1)} async-done(((bf16[128,3,32,128]{3,2,1,0:T(8,128)(2,1)}), bf16[128,3,32,128]{3,2,1,0:T(8,128)(2,1)}, u32[]{:S(2)}, u32[]{:S(2)}) %all-to-all-start.2) | async-done | bytes 3145760 | tf_op jit(solution)/shard_map/all_to_all | solution.py:263
  145.4 1.6 copy-done.2
  147.0 37.6 %shard_map.83 = bf16[6,32,64,128]{3,2,1,0:T(8,128)(2,1)} custom-call(bf16[16,8,96,128]{3,2,1,0:T(8,128)(2,1)} %bitcast.16.recv_ref, bf16[4,256,1024]{2,1,0:T(8,128)(2,1)S(1)} %copy-done.2, f32[32,9]{1,0:T(8,128)S(1)} %copy.33.lw_ref), custom_call_target="tpu_custom_call" | custom-call | tf_op jit(solution)/shard_map/pallas_call | solution.py:210
  (65 shorter events, 3.7 us)
Async XLA Ops:
  0.0 25.7 %copy-start = (bf16[512,1536]{1,0:T(8,128)(2,1)S(1)}, bf16[512,1536]{1,0:T(8,128)(2,1)}, u32[]{:S(2)}) copy-start(bf16[512,1536]{1,0:T(8,128)(2,1)} %param.8) | copy-start | bytes 4718596
  33.5 5.5 %copy-start.6 = (s32[4,16,4]{1,2,0:T(4,128)S(1)}, s32[4,16,4]{1,2,0:T(4,128)}, u32[]{:S(2)}) copy-start(s32[4,16,4]{1,2,0:T(4,128)} %param.9) | copy-start | bytes 3076
  33.5 5.6 %copy-start.8 = (s32[4,16]{1,0:T(4,128)S(1)}, s32[4,16]{1,0:T(4,128)}, u32[]{:S(2)}) copy-start(s32[4,16]{1,0:T(4,128)} %param.10) | copy-start | bytes 772
  33.5 6.2 %copy-start.9 = (bf16[8,64]{1,0:T(8,128)(2,1)S(1)}, bf16[8,64]{1,0:T(8,128)(2,1)}, u32[]{:S(2)}) copy-start(bf16[8,64]{1,0:T(8,128)(2,1)} %param.11) | copy-start | bytes 3076
  33.5 30.0 %all-to-all-start.1 = ((bf16[128,4,1536]{2,1,0:T(4,128)(2,1)}), bf16[128,4,1536]{2,1,0:T(4,128)(2,1)}, u32[]{:S(2)}, u32[]{:S(2)}) async-start(bf16[128,4,1536]{2,1,0:T(4,128)(2,1)} %broadcast_select_fusion), calls=%async_computation.1 | async-start | bytes 3145728 | tf_op jit(solution)/shard_map/all_to_all | solution.py:247
  74.3 1.8 copy-start.3
  76.2 1.0 copy-start.4
  77.2 0.9 copy-start.5
  96.5 1.7 copy-start.1
  98.1 5.8 %copy-start.7 = (f32[32,9]{0,1:T(8,128)S(1)}, f32[32,9]{0,1:T(8,128)}, u32[]{:S(2)}) copy-start(f32[32,9]{0,1:T(8,128)} %param.15) | copy-start | bytes 3460
  98.1 47.3 %all-to-all-start.2 = ((bf16[128,3,32,128]{3,2,1,0:T(8,128)(2,1)}), bf16[128,3,32,128]{3,2,1,0:T(8,128)(2,1)}, u32[]{:S(2)}, u32[]{:S(2)}) async-start(bf16[128,3,32,128]{3,2,1,0:T(8,128)(2,1)} %bitcast.35), calls=%async_computation.2 | async-start | bytes 6291456 | tf_op jit(solution)/shard_map/all_to_all | solution.py:263
  145.4 1.6 copy-start.2

commit v3 on v2

--- a/solution.py
+++ b/solution.py
@@ -17,24 +17,6 @@
             live_mask, gathered[:, slot_index].astype(jnp.float32), jnp.float32(0.0)
         )
     return (running / counts.astype(jnp.float32)[:, None]).astype(jnp.bfloat16)
-
-
-def lateral_mix(block_values, weight):
-    field_values = block_values.astype(jnp.float32)
-    rows_out = field_values.shape[-2]
-    cols_out = field_values.shape[-1]
-    widths = [(0, 0)] * (field_values.ndim - 2) + [(1, 1), (1, 1)]
-    padded = jnp.pad(field_values, widths)
-    mixed_sum = field_values
-    for row_shift in range(3):
-        for col_shift in range(3):
-            tap_weight = weight[:, row_shift * 3 + col_shift][:, None, None]
-            mixed_sum = (
-                mixed_sum
-                + tap_weight
-                * padded[..., row_shift : row_shift + rows_out, col_shift : col_shift + cols_out]
-            )
-    return mixed_sum.astype(jnp.bfloat16)
 
 
 def banded_first_weights(conv1_w):
@@ -48,6 +30,46 @@
         .reshape(32, 4 * conv1_w.shape[1])
     )
 
+
+MESH = pl.DeviceIdType.MESH
+
+
+def exchange_kernel(n_il, n_xl, x_ref, y_ref, send_sem, recv_sem):
+    n = n_il * n_xl
+    me = lax.axis_index("il") * n_xl + lax.axis_index("xl")
+    barrier = pltpu.get_barrier_semaphore()
+
+    def greet(k, carry):
+        d = lax.rem(me + 1 + k, n)
+        pl.semaphore_signal(barrier, inc=1, device_id=(d // n_xl, d % n_xl), device_id_type=MESH)
+        return carry
+
+    lax.fori_loop(0, n - 1, greet, 0)
+    pl.semaphore_wait(barrier, n - 1)
+    pltpu.make_async_copy(x_ref.at[me], y_ref.at[me], recv_sem).start()
+
+    def send(k, carry):
+        d = lax.rem(me + 1 + k, n)
+        pltpu.make_async_remote_copy(
+            src_ref=x_ref.at[d], dst_ref=y_ref.at[me], send_sem=send_sem, recv_sem=recv_sem,
+            device_id=(d // n_xl, d % n_xl), device_id_type=MESH,
+        ).start()
+        return carry
+
+    lax.fori_loop(0, n - 1, send, 0)
+    pltpu.make_async_copy(y_ref, y_ref, recv_sem).wait()
+    pltpu.make_async_copy(x_ref.at[pl.ds(0, n - 1)], y_ref.at[pl.ds(0, n - 1)], send_sem).wait()
+
+
+def exchange(x, n_il, n_xl, collective_id):
+    return pl.pallas_call(
+        functools.partial(exchange_kernel, n_il, n_xl),
+        out_shape=jax.ShapeDtypeStruct(x.shape, x.dtype),
+        in_specs=[pl.BlockSpec(memory_space=pl.ANY)],
+        out_specs=pl.BlockSpec(memory_space=pl.ANY),
+        scratch_shapes=[pltpu.SemaphoreType.DMA(()), pltpu.SemaphoreType.DMA(())],
+        compiler_params=pltpu.CompilerParams(collective_id=collective_id, has_side_effects=True),
+    )(x)
 
 def encoder_kernel(n_il, n_xl, bins, paired_ref, a1_ref, w2_ref, w3_ref, w4_ref, out_ref,
                    first_pad, second_pad, third_pad):
@@ -260,7 +282,7 @@
     pairs = outgoing.shape[2]
     group_width = outgoing.shape[3]
     outgoing = outgoing.reshape(devices, pairs, group_width, 2 * bin_total)
-    received = lax.all_to_all(outgoing, ("il", "xl"), split_axis=0, concat_axis=0, tiled=True)
+    received = exchange(outgoing, il_count, xl_count, 0)
     received = received.reshape(il_count, xl_count, pairs * group_width, 2 * bin_total)
     return receive_mix(
         received, merge_selectors(xl_count, 2 * bin_total), lateral_w,

time: 185 us -> 203 us (1.097)
  the two profiles are of different devices: /device:TPU:1 before, /device:TPU:117 now
where the time goes in v3:
time: 203 us
  Pallas kernels  127 us (63%)
  local copies, waits for them, and re-layouts  30.9 us (15%)
  starting transfers between devices  21 us (10%)
  waiting for transfers between devices  15.4 us (8%)
  other arithmetic  8.15 us (4%)
    pallas_call x1, Pallas kernels, exchange(): pl.pallas_call(functools.partial(exchange_kernel, n_il, n_xl), out_shape=...  71.8 us
    pallas_call x1, Pallas kernels, receive_mix(): pl.pallas_call(receive_kernel, out_shape=jax.ShapeDtypeStruct((n_s, n_o,...  36.5 us
    pallas_call x1, Pallas kernels, encode_to_send(): pl.pallas_call(functools.partial(encoder_kernel, n_il, n_xl, bins), out_s...  18.4 us
    all_to_all x1, waiting for transfers between devices, per_device(): lax.all_to_all(picked, ('il', 'xl'), split_axis=0, concat_axis=0, tiled=T...  15.4 us
    all_to_all x1, starting transfers between devices, per_device(): lax.all_to_all(picked, ('il', 'xl'), split_axis=0, concat_axis=0, tiled=T...  10.9 us
    unnamed x22, local copies, waits for them, and re-layouts  10.1 us
    all_to_all x1, starting transfers between devices, per_device(): lax.all_to_all(requests, ('il', 'xl'), split_axis=0, concat_axis=0, tiled...  10.1 us
    gather x3, local copies, waits for them, and re-layouts, per_device(): jnp.take(arrived.reshape(devices * capacity, samples), position, axis=0)  6.33 us
  transfers between devices with their start and end apart: 2, of which 1 were waited for; matrix products, arithmetic and copies ran while one was open for 3% of the time, Pallas kernels for 0%

profile of v3, /device:TPU:117, one launch (start us, length us, event | category | flops | bytes accessed | tf_op | source)
XLA Modules:
  0.0 202.6 jit_solution(8376579488201455192)
XLA Ops:
  0.0 0.9 copy.23
  1.9 1.4 scatter_custom_fusion
  4.0 10.1 %all-to-all-start = ((s32[128,1,4]{2,1,0:T(1,128)}), s32[128,1,4]{2,1,0:T(1,128)S(1)}, u32[]{:S(2)}, u32[]{:S(2)}) async-start(s32[128,1,4]{2,1,0:T(1,128)} %bitcast.5), calls=%async_computation | async-start | bytes 131072 | tf_op jit(solution)/shard_map/all_to_all | solution.py:265
  16.8 1.4 copy.33.lw_ref
  19.7 2.9 %gather_fusion = bf16[512,1536]{1,0:T(8,128)(2,1)} fusion(bf16[512,1536]{1,0:T(8,128)(2,1)S(1)} %copy-done, s32[1024]{0:T(1024)S(1)} %pad_clamp_fusion.1), kind=kCustom, calls=%fused_computation | custom fusion | bytes 3147776 | tf_op jit(solution)/shard_map/jit(_take)/gather | solution.py:266
  22.6 2.9 %gather.13 = bf16[128,4,1536]{2,1,0:T(4,128)(2,1)S(1)} reshape(bf16[512,1536]{1,0:T(8,128)(2,1)} %gather_fusion) | data formatting | bytes 3145728 | tf_op jit(solution)/shard_map/jit(_take)/gather | solution.py:266
  25.5 2.0 broadcast_select_fusion
  27.5 10.9 %all-to-all-start.1 = ((bf16[128,4,1536]{2,1,0:T(4,128)(2,1)}), bf16[128,4,1536]{2,1,0:T(4,128)(2,1)}, u32[]{:S(2)}, u32[]{:S(2)}) async-start(bf16[128,4,1536]{2,1,0:T(4,128)(2,1)} %broadcast_select_fusion), calls=%async_computation.1 | async-start | bytes 3145728 | tf_op jit(solution)/shard_map/all_to_all | solution.py:269
  39.0 1.8 fusion.sel_ref
  40.8 15.4 %all-to-all-done.1 = bf16[128,4,1536]{2,1,0:T(4,128)(2,1)} async-done(((bf16[128,4,1536]{2,1,0:T(4,128)(2,1)}), bf16[128,4,1536]{2,1,0:T(4,128)(2,1)}, u32[]{:S(2)}, u32[]{:S(2)}) %all-to-all-start.1) | async-done | bytes 1572896 | tf_op jit(solution)/shard_map/all_to_all | solution.py:269
  56.2 2.7 %reshape.502 = bf16[512,1536]{1,0:T(8,128)(2,1)S(1)} reshape(bf16[128,4,1536]{2,1,0:T(4,128)(2,1)} %all-to-all-done.1) | data formatting | bytes 3145728 | tf_op jit(solution)/shard_map/reshape | solution.py:270
  58.9 2.1 %gather_fusion.1 = bf16[256,1536]{1,0:T(8,128)(2,1)} fusion(bf16[512,1536]{1,0:T(8,128)(2,1)S(1)} %reshape.502, s32[1024]{0:T(1024)S(1)} %pad_clamp_fusion), kind=kCustom, calls=%fused_computation.1 | custom fusion | bytes 1573888 | tf_op jit(solution)/shard_map/jit(_take)/gather | solution.py:270
  61.1 2.4 %gather.15 = bf16[64,4,1536]{2,1,0:T(4,128)(2,1)} reshape(bf16[256,1536]{1,0:T(8,128)(2,1)} %gather_fusion.1) | data formatting | bytes 1572864 | tf_op jit(solution)/shard_map/jit(_take)/gather | solution.py:270
  63.4 1.8 copy.30
  66.0 1.0 pad_maximum_fusion
  67.0 1.8 copy.31
  68.9 1.0 copy-done.5
  69.8 0.9 copy-done.6
  70.8 18.4 %shard_map.82 = bf16[16,8,3,32,128]{4,3,2,1,0:T(8,128)(2,1)S(1)} custom-call(bf16[6144,32]{1,0:T(8,128)(2,1)S(1)} %bitcast.37, bf16[32,256]{1,0:T(8,128)(2,1)S(1)} %reshape.504.a1_ref, bf16[512,256]{1,0:T(8,128)(2,1)S(1)} %copy-done.6, bf16[768,256]{1,0:T(8,128)(2,1)S(1)} %copy-done.4, bf16[768,256]{1,0:T(8,128)(2,1)S(1)} %copy-done.5), custom_call_target="tpu_custom_call" | custom-call | tf_op jit(solution)/shard_map/pallas_call | solution.py:153
  89.2 1.7 copy-done.2
  90.8 71.8 %shard_map.83 = bf16[128,3,32,128]{3,2,1,0:T(8,128)(2,1)} custom-call(bf16[128,3,32,128]{3,2,1,0:T(8,128)(2,1)} %bitcast.36), custom_call_target="tpu_custom_call" | custom-call | tf_op jit(solution)/shard_map/pallas_call | solution.py:65
  162.6 1.9 copy-done.1
  164.5 1.6 copy-done.3
  166.1 36.5 %shard_map.84 = bf16[6,32,64,128]{3,2,1,0:T(8,128)(2,1)} custom-call(bf16[16,8,96,128]{3,2,1,0:T(8,128)(2,1)S(1)} %bitcast.35, bf16[4,256,1024]{2,1,0:T(8,128)(2,1)S(1)} %copy-done.3, f32[32,9]{1,0:T(8,128)S(1)} %copy-done.7), custom_call_target="tpu_custom_call" | custom-call | tf_op jit(solution)/shard_map/pallas_call | solution.py:232
  (63 shorter events, 7.1 us)
Async XLA Ops:
  0.0 19.7 %copy-start = (bf16[512,1536]{1,0:T(8,128)(2,1)S(1)}, bf16[512,1536]{1,0:T(8,128)(2,1)}, u32[]{:S(2)}) copy-start(bf16[512,1536]{1,0:T(8,128)(2,1)} %param.8) | copy-start | bytes 4718596
  4.0 14.1 %all-to-all-start = ((s32[128,1,4]{2,1,0:T(1,128)}), s32[128,1,4]{2,1,0:T(1,128)S(1)}, u32[]{:S(2)}, u32[]{:S(2)}) async-start(s32[128,1,4]{2,1,0:T(1,128)} %bitcast.5), calls=%async_computation | async-start | bytes 131072 | tf_op jit(solution)/shard_map/all_to_all | solution.py:265
  27.5 11.0 %copy-start.8 = (bf16[8,64]{1,0:T(8,128)(2,1)S(1)}, bf16[8,64]{1,0:T(8,128)(2,1)}, u32[]{:S(2)}) copy-start(bf16[8,64]{1,0:T(8,128)(2,1)} %param.11) | copy-start | bytes 3076
  27.5 28.7 %all-to-all-start.1 = ((bf16[128,4,1536]{2,1,0:T(4,128)(2,1)}), bf16[128,4,1536]{2,1,0:T(4,128)(2,1)}, u32[]{:S(2)}, u32[]{:S(2)}) async-start(bf16[128,4,1536]{2,1,0:T(4,128)(2,1)} %broadcast_select_fusion), calls=%async_computation.1 | async-start | bytes 3145728 | tf_op jit(solution)/shard_map/all_to_all | solution.py:269
  67.0 1.8 copy-start.4
  68.8 1.0 copy-start.5
  69.8 0.9 copy-start.6
  89.2 1.7 copy-start.2
  90.8 71.8 %copy-start.7 = (f32[32,9]{1,0:T(8,128)S(1)}, f32[32,9]{1,0:T(8,128)}, u32[]{:S(2)}) copy-start(f32[32,9]{1,0:T(8,128)} %copy.33.lw_ref) | copy-start | bytes 3460
  162.6 1.9 copy-start.1
  164.5 1.6 copy-start.3

commit v4 on v3

--- a/solution.py
+++ b/solution.py
@@ -175,12 +175,25 @@
     return (m == target).astype(jnp.bfloat16)
 
 
-def receive_kernel(recv_ref, sel_ref, lw_ref, out_ref, field):
+def lane_tap_matrices(weight, lanes):
+    offset = jnp.arange(lanes)[:, None] - jnp.arange(lanes)[None, :] + 1
+    taps = weight.reshape(weight.shape[0], 3, 3)
+    picked = jnp.where(
+        (offset >= 0) & (offset <= 2),
+        jnp.take(taps, jnp.clip(offset, 0, 2), axis=2),
+        jnp.float32(0.0),
+    )
+    high = picked.astype(jnp.bfloat16)
+    low = (picked - high.astype(jnp.float32)).astype(jnp.bfloat16)
+    return jnp.stack([high, low], axis=2)
+
+
+def receive_kernel(recv_ref, sel_ref, taps_ref, out_ref, field):
     n_a, n_b, rows_k_o, lanes = recv_ref.shape
     n_s, n_o, n_p, n_q = out_ref.shape
     n_k = rows_k_o // n_o
-    width = n_q // n_b
     n_p4 = n_p // n_a
+    per_o = n_s * n_p
     f32 = jnp.float32
 
     def merge(a, carry):
@@ -193,47 +206,37 @@
             for s2 in range(2):
                 for p4 in range(n_p4):
                     blk = y[k * n_o:(k + 1) * n_o, (s2 * n_p4 + p4) * lanes:(s2 * n_p4 + p4 + 1) * lanes]
-                    start = (2 * k + s2) * n_o * n_p + n_p4 * a + p4
-                    field[pl.ds(start, n_o, stride=n_p), :] = blk
+                    start = (2 * k + s2) * n_p + n_p4 * a + p4
+                    field[pl.ds(start, n_o, stride=per_o), :] = blk
         return carry
 
     lax.fori_loop(0, n_a, merge, 0)
 
-    row = lax.broadcasted_iota(jnp.int32, (n_p, n_q), 0)
-    col = lax.broadcasted_iota(jnp.int32, (n_p, n_q), 1)
-    zero = jnp.zeros((n_p, n_q), f32)
-
-    def mix(plane, carry):
-        s = plane // n_o
-        o = plane % n_o
-        f = field[pl.ds(pl.multiple_of(plane * n_p, n_p), n_p), :]
-        shifted_rows = [
-            jnp.where(row == 0, zero, pltpu.roll(f, 1, 0)),
-            f,
-            jnp.where(row == n_p - 1, zero, pltpu.roll(f, n_p - 1, 0)),
-        ]
-        acc = f
+    row = lax.broadcasted_iota(jnp.int32, (per_o, n_q), 0) % n_p
+    zero = jnp.zeros((per_o, n_q), f32)
+
+    def mix(o, carry):
+        f = field[pl.ds(pl.multiple_of(o * per_o, per_o), per_o), :]
+        fb = f.astype(jnp.bfloat16)
+        g = []
         for r in range(3):
-            g = shifted_rows[r]
-            taps = [
-                jnp.where(col == 0, zero, pltpu.roll(g, 1, 1)),
-                g,
-                jnp.where(col == n_q - 1, zero, pltpu.roll(g, n_q - 1, 1)),
-            ]
-            for c in range(3):
-                acc = acc + lw_ref[o, 3 * r + c] * taps[c]
-        out_ref[s, o] = acc.astype(out_ref.dtype)
-        return carry
-
-    lax.fori_loop(0, n_s * n_o, mix, 0)
+            t = jnp.dot(fb, taps_ref[o, r, 0], preferred_element_type=f32)
+            t = t + jnp.dot(fb, taps_ref[o, r, 1], preferred_element_type=f32)
+            g.append(t)
+        acc = f + g[1]
+        acc = acc + jnp.where(row == 0, zero, pltpu.roll(g[0], 1, 0))
+        acc = acc + jnp.where(row == n_p - 1, zero, pltpu.roll(g[2], per_o - 1, 0))
+        out_ref[:, o] = acc.astype(out_ref.dtype).reshape(n_s, n_p, n_q)
+        return carry
+
+    lax.fori_loop(0, n_o, mix, 0)
 
 
 def receive_mix(received, sel, lw, n_s, n_o, n_p, n_q):
     return pl.pallas_call(
         receive_kernel,
         out_shape=jax.ShapeDtypeStruct((n_s, n_o, n_p, n_q), jnp.bfloat16),
-        in_specs=[pl.BlockSpec(memory_space=pltpu.VMEM), pl.BlockSpec(memory_space=pltpu.VMEM),
-                  pl.BlockSpec(memory_space=pltpu.SMEM)],
+        in_specs=[pl.BlockSpec(memory_space=pltpu.VMEM)] * 3,
         out_specs=pl.BlockSpec(memory_space=pltpu.VMEM),
         scratch_shapes=[pltpu.VMEM((n_s * n_o * n_p, n_q), jnp.float32)],
         compiler_params=pltpu.CompilerParams(vmem_limit_bytes=48 * 1024 * 1024),
@@ -282,10 +285,11 @@
     pairs = outgoing.shape[2]
     group_width = outgoing.shape[3]
     outgoing = outgoing.reshape(devices, pairs, group_width, 2 * bin_total)
-    received = exchange(outgoing, il_count, xl_count, 0)
+    received = lax.all_to_all(outgoing, ("il", "xl"), split_axis=0, concat_axis=0, tiled=True)
     received = received.reshape(il_count, xl_count, pairs * group_width, 2 * bin_total)
     return receive_mix(
-        received, merge_selectors(xl_count, 2 * bin_total), lateral_w,
+        received, merge_selectors(xl_count, 2 * bin_total),
+        lane_tap_matrices(lateral_w, xl_count * bins_xl),
         2 * pairs, group_width, il_count * bins_il, xl_count * bins_xl,
     )
 

time: 203 us -> 272 us (1.34)
  the two profiles are of different devices: /device:TPU:117 before, /device:TPU:1 now
where the time goes in v4:
time: 272 us
  local copies, waits for them, and re-layouts  159 us (58%)
  Pallas kernels  43.2 us (16%)
  waiting for transfers between devices  23.3 us (9%)
  blocking collectives  20.8 us (8%)
  other arithmetic  14.3 us (5%)
  starting transfers between devices  10 us (4%)
    gather x2, local copies, waits for them, and re-layouts, lane_tap_matrices(): jnp.take(taps, jnp.clip(offset, 0, 2), axis=2)  139 us
    pallas_call x1, Pallas kernels, receive_mix(): pl.pallas_call(receive_kernel, out_shape=jax.ShapeDtypeStruct((n_s, n_o,...  24.8 us
    all_to_all x1, waiting for transfers between devices, per_device(): lax.all_to_all(picked, ('il', 'xl'), split_axis=0, concat_axis=0, tiled=T...  23.3 us
    all_to_all x1, blocking collectives, per_device(): lax.all_to_all(requests, ('il', 'xl'), split_axis=0, concat_axis=0, tiled...  20.8 us
    pallas_call x1, Pallas kernels, encode_to_send(): pl.pallas_call(functools.partial(encoder_kernel, n_il, n_xl, bins), out_s...  18.4 us
    unnamed x31, local copies, waits for them, and re-layouts  8.39 us
  transfers between devices with their start and end apart: 2, of which 1 were waited for; matrix products, arithmetic and copies ran while one was open for 55% of the time, Pallas kernels for 0%

profile of v4, /device:TPU:1, one launch (start us, length us, event | category | flops | bytes accessed | tf_op | source)
XLA Modules:
  0.0 271.5 jit_solution(10171644296964092150)
XLA Ops:
  0.0 0.9 copy.36
  1.9 1.4 scatter_custom_fusion
  3.4 20.8 %all_to_all.19 = s32[128,1,4]{2,1,0:T(1,128)S(1)} all-to-all(s32[128,1,4]{2,1,0:T(1,128)S(1)} %bitcast.64), channel_id=1, replica_groups=mesh['il'=16,'xl'=8] {'il','xl'}, dimensions={0} | all-to-all | bytes 4096 | tf_op jit(solution)/shard_map/all_to_all | solution.py:268
  25.7 2.1 gather_fusion
  28.3 2.0 broadcast_select_fusion
  30.3 5.3 %all-to-all-start.1 = ((bf16[128,4,1536]{2,1,0:T(4,128)(2,1)}), bf16[128,4,1536]{2,1,0:T(4,128)(2,1)}, u32[]{:S(2)}, u32[]{:S(2)}) async-start(bf16[128,4,1536]{2,1,0:T(4,128)(2,1)} %broadcast_select_fusion), calls=%async_computation.1 | async-start | bytes 3145728 | tf_op jit(solution)/shard_map/all_to_all | solution.py:272
  36.8 23.3 %all-to-all-done.1 = bf16[128,4,1536]{2,1,0:T(4,128)(2,1)} async-done(((bf16[128,4,1536]{2,1,0:T(4,128)(2,1)}), bf16[128,4,1536]{2,1,0:T(4,128)(2,1)}, u32[]{:S(2)}, u32[]{:S(2)}) %all-to-all-start.1) | async-done | bytes 1572896 | tf_op jit(solution)/shard_map/all_to_all | solution.py:272
  60.1 2.7 %reshape.576 = bf16[512,1536]{1,0:T(8,128)(2,1)S(1)} reshape(bf16[128,4,1536]{2,1,0:T(4,128)(2,1)} %all-to-all-done.1) | data formatting | bytes 3145728 | tf_op jit(solution)/shard_map/reshape | solution.py:273
  62.9 1.3 gather_fusion.1
  64.3 0.9 copy.43
  66.2 0.8 copy.44
  67.0 18.4 %shard_map.82 = bf16[16,8,3,32,128]{4,3,2,1,0:T(8,128)(2,1)S(1)} custom-call(bf16[6144,32]{1,0:T(8,128)(2,1)S(1)} %bitcast.55, bf16[32,256]{1,0:T(8,128)(2,1)S(1)} %reshape.578.a1_ref, bf16[512,256]{1,0:T(8,128)(2,1)S(1)} %copy-done.8, bf16[768,256]{1,0:T(8,128)(2,1)S(1)} %copy-done.6, bf16[768,256]{1,0:T(8,128)(2,1)S(1)} %copy-done.7), custom_call_target="tpu_custom_call" | custom-call | tf_op jit(solution)/shard_map/pallas_call | solution.py:153
  85.5 1.7 copy-done.4
  87.1 4.7 %all-to-all-start.2 = ((bf16[128,3,32,128]{3,2,1,0:T(8,128)(2,1)}), bf16[128,3,32,128]{3,2,1,0:T(8,128)(2,1)S(1)}, u32[]{:S(2)}, u32[]{:S(2)}) async-start(bf16[128,3,32,128]{3,2,1,0:T(8,128)(2,1)} %bitcast.54), calls=%async_computation.2 | async-start | bytes 6291456 | tf_op jit(solution)/shard_map/all_to_all | solution.py:288
  91.9 118.7 %gather_fusion.2 = f32[16384,32,3]{1,2,0:T(4,128)} fusion(f32[32,3,3]{0,1,2:T(4,128)S(1)} %copy.46, s32[16384]{0:T(1024)S(1)} %fusion.13), kind=kCustom, calls=%fused_computation.2 | custom fusion | bytes 12648448 | tf_op jit(solution)/shard_map/jit(_take)/gather | solution.py:183
  210.6 20.2 %copy.48 = f32[128,128,32,3]{1,0,3,2:T(8,128)} copy(f32[128,128,32,3]{2,3,1,0:T(4,128)} %bitcast.56) | data formatting | bytes 12582912 | tf_op jit(solution)/shard_map/jit(_take)/gather | solution.py:183
  230.9 4.0 %fusion.1 = bf16[32,3,1,128,128]{4,3,2,1,0:T(8,128)(2,1)S(1)} fusion(f32[128,128,32,3]{1,0,3,2:T(8,128)} %copy.48, pred[128,128]{1,0:T(8,128)(4,1)S(1)} %get-tuple-element.17, pred[128,128]{1,0:T(8,128)(4,1)S(1)} %get-tuple-element.18), kind=kLoop, calls=%fused_computation.8 | loop fusion | flops 3145728 | bytes 9469952 | tf_op jit(solution)/shard_map/convert_element_type | solution.py:186
  235.5 1.1 subtract_convert_fusion
  236.6 3.2 %pad_maximum_fusion.taps_ref = bf16[32,3,2,128,128]{4,3,2,1,0:T(8,128)(2,1)} fusion(bf16[32,3,1,128,128]{4,3,2,1,0:T(8,128)(2,1)S(1)} %subtract_convert_fusion, bf16[32,3,1,128,128]{4,3,2,1,0:T(8,128)(2,1)S(1)} %fusion.1), kind=kLoop, calls=%fused_computation.4 | loop fusion | flops 3145728 | bytes 12582912 | tf_op jit(solution)/shard_map/stack | solution.py:188
  239.9 1.8 fusion.2.sel_ref
  241.6 1.7 copy-done.2
  243.3 1.9 copy-done.3
  245.2 1.6 copy-done.5
  246.8 24.8 %shard_map.83 = bf16[6,32,64,128]{3,2,1,0:T(8,128)(2,1)} custom-call(bf16[16,8,96,128]{3,2,1,0:T(8,128)(2,1)S(1)} %bitcast.53, bf16[4,256,1024]{2,1,0:T(8,128)(2,1)S(1)} %copy-done.5, bf16[32,3,2,128,128]{4,3,2,1,0:T(8,128)(2,1)} %pad_maximum_fusion.taps_ref), custom_call_target="tpu_custom_call" | custom-call | tf_op jit(solution)/shard_map/pallas_call | solution.py:236
  (81 shorter events, 5.9 us)
Async XLA Ops:
  0.0 25.7 %copy-start = (bf16[512,1536]{1,0:T(8,128)(2,1)S(1)}, bf16[512,1536]{1,0:T(8,128)(2,1)}, u32[]{:S(2)}) copy-start(bf16[512,1536]{1,0:T(8,128)(2,1)} %param.8) | copy-start | bytes 4718596
  28.3 7.4 %copy-start.10 = (s32[4,16,4]{1,2,0:T(4,128)S(1)}, s32[4,16,4]{1,2,0:T(4,128)}, u32[]{:S(2)}) copy-start(s32[4,16,4]{1,2,0:T(4,128)} %param.9) | copy-start | bytes 3076
  28.3 7.6 %copy-start.12 = (s32[4,16]{1,0:T(4,128)S(1)}, s32[4,16]{1,0:T(4,128)}, u32[]{:S(2)}) copy-start(s32[4,16]{1,0:T(4,128)} %param.10) | copy-start | bytes 772
  28.3 8.1 %copy-start.13 = (bf16[8,64]{1,0:T(8,128)(2,1)S(1)}, bf16[8,64]{1,0:T(8,128)(2,1)}, u32[]{:S(2)}) copy-start(bf16[8,64]{1,0:T(8,128)(2,1)} %param.11) | copy-start | bytes 3076
  30.3 29.9 %all-to-all-start.1 = ((bf16[128,4,1536]{2,1,0:T(4,128)(2,1)}), bf16[128,4,1536]{2,1,0:T(4,128)(2,1)}, u32[]{:S(2)}, u32[]{:S(2)}) async-start(bf16[128,4,1536]{2,1,0:T(4,128)(2,1)} %broadcast_select_fusion), calls=%async_computation.1 | async-start | bytes 3145728 | tf_op jit(solution)/shard_map/all_to_all | solution.py:272
  65.5 1.5 copy-start.6
  65.6 1.5 copy-start.7
  65.6 1.5 copy-start.8
  85.4 1.7 copy-start.4
  87.1 4.7 %copy-start.11 = (f32[32,9]{0,1:T(8,128)S(1)}, f32[32,9]{0,1:T(8,128)}, u32[]{:S(2)}) copy-start(f32[32,9]{0,1:T(8,128)} %param.15) | copy-start | bytes 3460
  87.1 154.5 %all-to-all-start.2 = ((bf16[128,3,32,128]{3,2,1,0:T(8,128)(2,1)}), bf16[128,3,32,128]{3,2,1,0:T(8,128)(2,1)S(1)}, u32[]{:S(2)}, u32[]{:S(2)}) async-start(bf16[128,3,32,128]{3,2,1,0:T(8,128)(2,1)} %bitcast.54), calls=%async_computation.2 | async-start | bytes 6291456 | tf_op jit(solution)/shard_map/all_to_all | solution.py:288
  230.9 4.6 %copy-start.9 = (f32[128,128,32,3]{1,0,3,2:T(8,128)S(1)}, f32[128,128,32,3]{1,0,3,2:T(8,128)}, u32[]{:S(2)}) copy-start(f32[128,128,32,3]{1,0,3,2:T(8,128)} %copy.48) | copy-start | bytes 18874372
  241.6 1.7 copy-start.2
  243.3 1.9 copy-start.3
  245.2 1.6 copy-start.5
  246.8 24.8 %copy-start.1 = (bf16[512,1536]{1,0:T(8,128)(2,1)S(1)}, bf16[512,1536]{1,0:T(8,128)(2,1)}, u32[]{:S(2)}) copy-start(bf16[512,1536]{1,0:T(8,128)(2,1)} %param.8) | copy-start | bytes 4718596

commit v5 on v4

--- a/solution.py
+++ b/solution.py
@@ -177,15 +177,13 @@
 
 def lane_tap_matrices(weight, lanes):
     offset = jnp.arange(lanes)[:, None] - jnp.arange(lanes)[None, :] + 1
-    taps = weight.reshape(weight.shape[0], 3, 3)
-    picked = jnp.where(
-        (offset >= 0) & (offset <= 2),
-        jnp.take(taps, jnp.clip(offset, 0, 2), axis=2),
-        jnp.float32(0.0),
-    )
-    high = picked.astype(jnp.bfloat16)
-    low = (picked - high.astype(jnp.float32)).astype(jnp.bfloat16)
-    return jnp.stack([high, low], axis=2)
+    taps = weight.reshape(weight.shape[0], 3, 3, 1, 1)
+    picked = jnp.zeros((weight.shape[0], 3, lanes, lanes), jnp.float32)
+    for c in range(3):
+        picked = picked + jnp.where(offset == c, taps[:, :, c], jnp.float32(0.0))
+    high = lax.reduce_precision(picked, exponent_bits=8, mantissa_bits=7)
+    low = (picked - high).astype(jnp.bfloat16)
+    return jnp.stack([high.astype(jnp.bfloat16), low], axis=2)
 
 
 def receive_kernel(recv_ref, sel_ref, taps_ref, out_ref, field):

time: 272 us -> 173 us (0.64)
  local copies, waits for them, and re-layouts: 159 us -> 26.6 us
  waiting for transfers between devices: 23.3 us -> 56.8 us
    gather x2 -> x0, local copies, waits for them, and re-layouts: 139 us -> none  [lane_tap_matrices(): jnp.take(taps, jnp.clip(offset, 0, 2), axis=2)]
    all_to_all x1, waiting for transfers between devices: 0.01 us -> 33.4 us  [per_device(): lax.all_to_all(outgoing, ('il', 'xl'), split_axis=0, concat_axis=0, tiled...]
    gather x3, local copies, waits for them, and re-layouts: 2.37 us -> 6.33 us  [per_device(): jnp.take(arrived.reshape(devices * capacity, samples), position, axis=0)]
    gather x2, local copies, waits for them, and re-layouts: 2.53 us -> 5.81 us  [per_device(): jnp.take(traces, wanted.reshape(-1), axis=0)]
    unnamed x31 -> x23, local copies, waits for them, and re-layouts: 8.39 us -> 6.13 us
  transfers between devices with their start and end apart: 2 -> 2, of which waited for: 1 -> 2; matrix products, arithmetic and copies ran while one was open for 55% -> 5% of each run, Pallas kernels for 0% -> 0%
where the time goes in v5:
time: 173 us
  waiting for transfers between devices  56.8 us (33%)
  Pallas kernels  44 us (25%)
  local copies, waits for them, and re-layouts  26.6 us (15%)
  blocking collectives  20.8 us (12%)
  other arithmetic  12.7 us (7%)
  starting transfers between devices  11.2 us (6%)
    all_to_all x1, waiting for transfers between devices, per_device(): lax.all_to_all(outgoing, ('il', 'xl'), split_axis=0, concat_axis=0, tiled...  33.4 us
    pallas_call x1, Pallas kernels, receive_mix(): pl.pallas_call(receive_kernel, out_shape=jax.ShapeDtypeStruct((n_s, n_o,...  25.6 us
    all_to_all x1, waiting for transfers between devices, per_device(): lax.all_to_all(picked, ('il', 'xl'), split_axis=0, concat_axis=0, tiled=T...  23.3 us
    all_to_all x1, blocking collectives, per_device(): lax.all_to_all(requests, ('il', 'xl'), split_axis=0, concat_axis=0, tiled...  20.8 us
    pallas_call x1, Pallas kernels, encode_to_send(): pl.pallas_call(functools.partial(encoder_kernel, n_il, n_xl, bins), out_s...  18.3 us
    gather x3, local copies, waits for them, and re-layouts, per_device(): jnp.take(arrived.reshape(devices * capacity, samples), position, axis=0)  6.33 us
    unnamed x23, local copies, waits for them, and re-layouts  6.13 us
    gather x2, local copies, waits for them, and re-layouts, per_device(): jnp.take(traces, wanted.reshape(-1), axis=0)  5.81 us
  transfers between devices with their start and end apart: 2, of which 2 were waited for; matrix products, arithmetic and copies ran while one was open for 5% of the time, Pallas kernels for 0%

profile of v5, /device:TPU:1, one launch (start us, length us, event | category | flops | bytes accessed | tf_op | source)
XLA Modules:
  0.0 172.6 jit_solution(10741747524851112456)
XLA Ops:
  1.9 1.4 scatter_custom_fusion
  3.4 20.8 %all_to_all.19 = s32[128,1,4]{2,1,0:T(1,128)S(1)} all-to-all(s32[128,1,4]{2,1,0:T(1,128)S(1)} %bitcast.48), channel_id=1, replica_groups=mesh['il'=16,'xl'=8] {'il','xl'}, dimensions={0} | all-to-all | bytes 4096 | tf_op jit(solution)/shard_map/all_to_all | solution.py:266
  25.7 2.9 %gather_fusion = bf16[512,1536]{1,0:T(8,128)(2,1)} fusion(bf16[512,1536]{1,0:T(8,128)(2,1)S(1)} %copy-done, s32[1024]{0:T(1024)S(1)} %pad_clamp_fusion.1), kind=kCustom, calls=%fused_computation | custom fusion | bytes 3147776 | tf_op jit(solution)/shard_map/jit(_take)/gather | solution.py:267
  28.6 2.9 %gather.13 = bf16[128,4,1536]{2,1,0:T(4,128)(2,1)S(1)} reshape(bf16[512,1536]{1,0:T(8,128)(2,1)} %gather_fusion) | data formatting | bytes 3145728 | tf_op jit(solution)/shard_map/jit(_take)/gather | solution.py:267
  31.5 2.0 %broadcast_select_fusion = bf16[128,4,1536]{2,1,0:T(4,128)(2,1)} fusion(bf16[128,4,1536]{2,1,0:T(4,128)(2,1)S(1)} %gather.13, pred[128,4]{1,0:T(8,128)(4,1)S(1)} %compare_and_fusion), kind=kLoop, calls=%fused_computation.10 | loop fusion | flops 786432 | bytes 3146240 | tf_op jit(solution)/shard_map/jit(_take)/select_n | solution.py:267
  33.5 5.4 %all-to-all-start.1 = ((bf16[128,4,1536]{2,1,0:T(4,128)(2,1)}), bf16[128,4,1536]{2,1,0:T(4,128)(2,1)}, u32[]{:S(2)}, u32[]{:S(2)}) async-start(bf16[128,4,1536]{2,1,0:T(4,128)(2,1)} %broadcast_select_fusion), calls=%async_computation.1 | async-start | bytes 3145728 | tf_op jit(solution)/shard_map/all_to_all | solution.py:270
  40.2 23.3 %all-to-all-done.1 = bf16[128,4,1536]{2,1,0:T(4,128)(2,1)} async-done(((bf16[128,4,1536]{2,1,0:T(4,128)(2,1)}), bf16[128,4,1536]{2,1,0:T(4,128)(2,1)}, u32[]{:S(2)}, u32[]{:S(2)}) %all-to-all-start.1) | async-done | bytes 1572896 | tf_op jit(solution)/shard_map/all_to_all | solution.py:270
  63.5 2.7 %reshape.535 = bf16[512,1536]{1,0:T(8,128)(2,1)S(1)} reshape(bf16[128,4,1536]{2,1,0:T(4,128)(2,1)} %all-to-all-done.1) | data formatting | bytes 3145728 | tf_op jit(solution)/shard_map/reshape | solution.py:271
  66.2 2.1 %gather_fusion.1 = bf16[256,1536]{1,0:T(8,128)(2,1)} fusion(bf16[512,1536]{1,0:T(8,128)(2,1)S(1)} %reshape.535, s32[1024]{0:T(1024)S(1)} %pad_clamp_fusion), kind=kCustom, calls=%fused_computation.1 | custom fusion | bytes 1573888 | tf_op jit(solution)/shard_map/jit(_take)/gather | solution.py:271
  68.4 2.4 %gather.15 = bf16[64,4,1536]{2,1,0:T(4,128)(2,1)} reshape(bf16[256,1536]{1,0:T(8,128)(2,1)} %gather_fusion.1) | data formatting | bytes 1572864 | tf_op jit(solution)/shard_map/jit(_take)/gather | solution.py:271
  70.8 1.8 %copy.37 = bf16[64,4,1536]{0,2,1:T(8,128)(2,1)S(1)} copy(bf16[64,4,1536]{2,1,0:T(4,128)(2,1)} %gather.15) | data formatting | bytes 1572864 | tf_op jit(solution)/shard_map/jit(_take)/gather | solution.py:271
  73.3 1.0 pad_maximum_fusion.1
  74.3 1.8 %copy.38 = bf16[96,64,32]{2,1,0:T(8,128)(2,1)S(1)} copy(bf16[96,64,32]{1,2,0:T(8,128)(2,1)} %pad_maximum_fusion.1) | data formatting | bytes 786432 | tf_op jit(solution)/shard_map/concatenate | solution.py:278
  76.1 1.0 copy-done.4
  77.1 0.9 copy-done.5
  78.1 18.3 %shard_map.82 = bf16[16,8,3,32,128]{4,3,2,1,0:T(8,128)(2,1)S(1)} custom-call(bf16[6144,32]{1,0:T(8,128)(2,1)S(1)} %bitcast.40, bf16[32,256]{1,0:T(8,128)(2,1)S(1)} %reshape.537.a1_ref, bf16[512,256]{1,0:T(8,128)(2,1)S(1)} %copy-done.5, bf16[768,256]{1,0:T(8,128)(2,1)S(1)} %copy-done.3, bf16[768,256]{1,0:T(8,128)(2,1)S(1)} %copy-done.4), custom_call_target="tpu_custom_call" | custom-call | tf_op jit(solution)/shard_map/pallas_call | solution.py:153
  96.4 1.7 copy-done.1
  98.1 5.8 %all-to-all-start.2 = ((bf16[128,3,32,128]{3,2,1,0:T(8,128)(2,1)}), bf16[128,3,32,128]{3,2,1,0:T(8,128)(2,1)}, u32[]{:S(2)}, u32[]{:S(2)}) async-start(bf16[128,3,32,128]{3,2,1,0:T(8,128)(2,1)} %bitcast.39), calls=%async_computation.2 | async-start | bytes 6291456 | tf_op jit(solution)/shard_map/all_to_all | solution.py:286
  104.3 2.7 %reduce-precision_convert_fusion = (bf16[32,3,1,128,128]{4,3,2,1,0:T(8,128)(2,1)S(1)}, bf16[32,3,1,128,128]{4,3,2,1,0:T(8,128)(2,1)S(1)}) fusion(f32[32,3]{1,0:T(8,128)S(1)} %bitcast.51, f32[32,3]{1,0:T(8,128)S(1)} %bitcast.50, f32[32,3]{1,0:T(8,128)S(1)} %bitcast.49, pred[128,128]{1,0:T(8,128)(4,1)S(1)} %get-tuple-element.22, ...), kind=kLoop, calls=%fused_computation.4 | loop fusion | flops 14155776 | bytes 6341760 | tf_op jit(solution)/shard_map/convert_element_type | solution.py:186
  107.0 3.2 %pad_maximum_fusion.taps_ref = bf16[32,3,2,128,128]{4,3,2,1,0:T(8,128)(2,1)} fusion(bf16[32,3,1,128,128]{4,3,2,1,0:T(8,128)(2,1)S(1)} %get-tuple-element.10, bf16[32,3,1,128,128]{4,3,2,1,0:T(8,128)(2,1)S(1)} %get-tuple-element.9), kind=kLoop, calls=%fused_computation.6 | loop fusion | flops 3145728 | bytes 12582912 | tf_op jit(solution)/shard_map/stack | solution.py:186
  110.2 1.7 fusion.1.sel_ref
  112.0 33.4 %all-to-all-done.2 = bf16[128,3,32,128]{3,2,1,0:T(8,128)(2,1)} async-done(((bf16[128,3,32,128]{3,2,1,0:T(8,128)(2,1)}), bf16[128,3,32,128]{3,2,1,0:T(8,128)(2,1)}, u32[]{:S(2)}, u32[]{:S(2)}) %all-to-all-start.2) | async-done | bytes 3145760 | tf_op jit(solution)/shard_map/all_to_all | solution.py:286
  145.4 1.6 copy-done.2
  147.0 25.6 %shard_map.83 = bf16[6,32,64,128]{3,2,1,0:T(8,128)(2,1)} custom-call(bf16[16,8,96,128]{3,2,1,0:T(8,128)(2,1)} %bitcast.16.recv_ref, bf16[4,256,1024]{2,1,0:T(8,128)(2,1)S(1)} %copy-done.2, bf16[32,3,2,128,128]{4,3,2,1,0:T(8,128)(2,1)} %pad_maximum_fusion.taps_ref), custom_call_target="tpu_custom_call" | custom-call | tf_op jit(solution)/shard_map/pallas_call | solution.py:234
  (73 shorter events, 5.7 us)
Async XLA Ops:
  0.0 25.7 %copy-start = (bf16[512,1536]{1,0:T(8,128)(2,1)S(1)}, bf16[512,1536]{1,0:T(8,128)(2,1)}, u32[]{:S(2)}) copy-start(bf16[512,1536]{1,0:T(8,128)(2,1)} %param.8) | copy-start | bytes 4718596
  33.5 5.6 %copy-start.6 = (s32[4,16,4]{1,2,0:T(4,128)S(1)}, s32[4,16,4]{1,2,0:T(4,128)}, u32[]{:S(2)}) copy-start(s32[4,16,4]{1,2,0:T(4,128)} %param.9) | copy-start | bytes 3076
  33.5 5.7 %copy-start.8 = (s32[4,16]{1,0:T(4,128)S(1)}, s32[4,16]{1,0:T(4,128)}, u32[]{:S(2)}) copy-start(s32[4,16]{1,0:T(4,128)} %param.10) | copy-start | bytes 772
  33.5 6.3 %copy-start.9 = (bf16[8,64]{1,0:T(8,128)(2,1)S(1)}, bf16[8,64]{1,0:T(8,128)(2,1)}, u32[]{:S(2)}) copy-start(bf16[8,64]{1,0:T(8,128)(2,1)} %param.11) | copy-start | bytes 3076
  33.5 30.0 %all-to-all-start.1 = ((bf16[128,4,1536]{2,1,0:T(4,128)(2,1)}), bf16[128,4,1536]{2,1,0:T(4,128)(2,1)}, u32[]{:S(2)}, u32[]{:S(2)}) async-start(bf16[128,4,1536]{2,1,0:T(4,128)(2,1)} %broadcast_select_fusion), calls=%async_computation.1 | async-start | bytes 3145728 | tf_op jit(solution)/shard_map/all_to_all | solution.py:270
  73.3 2.8 %copy-start.3 = (bf16[768,256]{1,0:T(8,128)(2,1)S(1)}, bf16[768,256]{1,0:T(8,128)(2,1)}, u32[]{:S(2)}) copy-start(bf16[768,256]{1,0:T(8,128)(2,1)} %w3_ref.1) | copy-start | bytes 1179652
  76.1 1.0 copy-start.4
  77.1 0.9 copy-start.5
  96.4 1.7 copy-start.1
  98.1 5.8 %copy-start.7 = (f32[32,9]{0,1:T(8,128)S(1)}, f32[32,9]{0,1:T(8,128)}, u32[]{:S(2)}) copy-start(f32[32,9]{0,1:T(8,128)} %param.15) | copy-start | bytes 3460
  98.1 47.3 %all-to-all-start.2 = ((bf16[128,3,32,128]{3,2,1,0:T(8,128)(2,1)}), bf16[128,3,32,128]{3,2,1,0:T(8,128)(2,1)}, u32[]{:S(2)}, u32[]{:S(2)}) async-start(bf16[128,3,32,128]{3,2,1,0:T(8,128)(2,1)} %bitcast.39), calls=%async_computation.2 | async-start | bytes 6291456 | tf_op jit(solution)/shard_map/all_to_all | solution.py:286
  145.4 1.6 copy-start.2

commit v6 on v5

--- a/solution.py
+++ b/solution.py
@@ -263,7 +263,7 @@
         .set(local_row)
         .reshape(devices, capacity)
     )
-    wanted = lax.all_to_all(requests, ("il", "xl"), split_axis=0, concat_axis=0, tiled=True)
+    wanted = exchange(requests, il_count, xl_count, 1)
     picked = jnp.take(traces, wanted.reshape(-1), axis=0).reshape(
         wanted.shape[0], wanted.shape[1], samples
     )

time: 173 us -> 172 us (level)
  blocking collectives: 20.8 us -> 0 us
  Pallas kernels: 44 us -> 60.6 us
  starting transfers between devices: 11.2 us -> 13.3 us
    all_to_all x1 -> x0, blocking collectives: 20.8 us -> none  [per_device(): lax.all_to_all(requests, ('il', 'xl'), split_axis=0, concat_axis=0, tiled...]
    pallas_call x0 -> x1, Pallas kernels: none -> 16.7 us  [exchange(): pl.pallas_call(functools.partial(exchange_kernel, n_il, n_xl), out_shape=...]
    all_to_all x1, starting transfers between devices: 5.44 us -> 7.57 us  [per_device(): lax.all_to_all(picked, ('il', 'xl'), split_axis=0, concat_axis=0, tiled=T...]
where the time goes in v6:
time: 172 us; the launch traced here: 171 us
  Pallas kernels  60.6 us (35%)
  waiting for transfers between devices  56.7 us (33%)
  local copies, waits for them, and re-layouts  27.6 us (16%)
  starting transfers between devices  13.3 us (8%)
  other arithmetic  12.7 us (7%)
    all_to_all x1, waiting for transfers between devices, per_device(): lax.all_to_all(outgoing, ('il', 'xl'), split_axis=0, concat_axis=0, tiled...  33.4 us
    pallas_call x1, Pallas kernels, receive_mix(): pl.pallas_call(receive_kernel, out_shape=jax.ShapeDtypeStruct((n_s, n_o,...  25.6 us
    all_to_all x1, waiting for transfers between devices, per_device(): lax.all_to_all(picked, ('il', 'xl'), split_axis=0, concat_axis=0, tiled=T...  23.2 us
    pallas_call x1, Pallas kernels, encode_to_send(): pl.pallas_call(functools.partial(encoder_kernel, n_il, n_xl, bins), out_s...  18.4 us
    pallas_call x1, Pallas kernels, exchange(): pl.pallas_call(functools.partial(exchange_kernel, n_il, n_xl), out_shape=...  16.7 us
    all_to_all x1, starting transfers between devices, per_device(): lax.all_to_all(picked, ('il', 'xl'), split_axis=0, concat_axis=0, tiled=T...  7.57 us
    gather x3, local copies, waits for them, and re-layouts, per_device(): jnp.take(arrived.reshape(devices * capacity, samples), position, axis=0)  6.32 us
    unnamed x23, local copies, waits for them, and re-layouts  6.13 us
  transfers between devices with their start and end apart: 2, of which 2 were waited for; matrix products, arithmetic and copies ran while one was open for 5% of the time, Pallas kernels for 0%

profile of v6, /device:TPU:1, one launch (start us, length us, event | category | flops | bytes accessed | tf_op | source)
XLA Modules:
  0.0 171.4 jit_solution(10170503542648739059)
XLA Ops:
  1.9 1.4 scatter_custom_fusion
  4.0 16.7 %shard_map.82 = s32[128,4]{1,0:T(8,128)} custom-call(s32[128,4]{1,0:T(8,128)} %reshape.527.x_ref), custom_call_target="tpu_custom_call" | custom-call | tf_op jit(solution)/shard_map/pallas_call | solution.py:65
  22.6 2.9 %gather_fusion = bf16[512,1536]{1,0:T(8,128)(2,1)} fusion(bf16[512,1536]{1,0:T(8,128)(2,1)S(1)} %copy-done, s32[1024]{0:T(1024)S(1)} %pad_clamp_fusion.1), kind=kCustom, calls=%fused_computation | custom fusion | bytes 3147776 | tf_op jit(solution)/shard_map/jit(_take)/gather | solution.py:267
  25.5 2.9 %gather.13 = bf16[128,4,1536]{2,1,0:T(4,128)(2,1)S(1)} reshape(bf16[512,1536]{1,0:T(8,128)(2,1)} %gather_fusion) | data formatting | bytes 3145728 | tf_op jit(solution)/shard_map/jit(_take)/gather | solution.py:267
  28.4 2.0 %broadcast_select_fusion = bf16[128,4,1536]{2,1,0:T(4,128)(2,1)} fusion(bf16[128,4,1536]{2,1,0:T(4,128)(2,1)S(1)} %gather.13, pred[128,4]{1,0:T(8,128)(4,1)S(1)} %compare_and_fusion), kind=kLoop, calls=%fused_computation.10 | loop fusion | flops 786432 | bytes 3146240 | tf_op jit(solution)/shard_map/jit(_take)/select_n | solution.py:267
  30.4 7.6 %all-to-all-start = ((bf16[128,4,1536]{2,1,0:T(4,128)(2,1)}), bf16[128,4,1536]{2,1,0:T(4,128)(2,1)}, u32[]{:S(2)}, u32[]{:S(2)}) async-start(bf16[128,4,1536]{2,1,0:T(4,128)(2,1)} %broadcast_select_fusion), calls=%async_computation | async-start | bytes 3145728 | tf_op jit(solution)/shard_map/all_to_all | solution.py:270
  39.1 23.2 %all-to-all-done = bf16[128,4,1536]{2,1,0:T(4,128)(2,1)} async-done(((bf16[128,4,1536]{2,1,0:T(4,128)(2,1)}), bf16[128,4,1536]{2,1,0:T(4,128)(2,1)}, u32[]{:S(2)}, u32[]{:S(2)}) %all-to-all-start) | async-done | bytes 1572896 | tf_op jit(solution)/shard_map/all_to_all | solution.py:270
  62.3 2.7 %reshape.529 = bf16[512,1536]{1,0:T(8,128)(2,1)S(1)} reshape(bf16[128,4,1536]{2,1,0:T(4,128)(2,1)} %all-to-all-done) | data formatting | bytes 3145728 | tf_op jit(solution)/shard_map/reshape | solution.py:271
  65.1 2.1 %gather_fusion.1 = bf16[256,1536]{1,0:T(8,128)(2,1)} fusion(bf16[512,1536]{1,0:T(8,128)(2,1)S(1)} %reshape.529, s32[1024]{0:T(1024)S(1)} %pad_clamp_fusion), kind=kCustom, calls=%fused_computation.1 | custom fusion | bytes 1573888 | tf_op jit(solution)/shard_map/jit(_take)/gather | solution.py:271
  67.2 2.4 %gather.15 = bf16[64,4,1536]{2,1,0:T(4,128)(2,1)} reshape(bf16[256,1536]{1,0:T(8,128)(2,1)} %gather_fusion.1) | data formatting | bytes 1572864 | tf_op jit(solution)/shard_map/jit(_take)/gather | solution.py:271
  69.6 1.8 %copy.23 = bf16[64,4,1536]{0,2,1:T(8,128)(2,1)S(1)} copy(bf16[64,4,1536]{2,1,0:T(4,128)(2,1)} %gather.15) | data formatting | bytes 1572864 | tf_op jit(solution)/shard_map/jit(_take)/gather | solution.py:271
  72.1 1.0 pad_maximum_fusion.1
  73.2 1.8 %copy.24 = bf16[96,64,32]{2,1,0:T(8,128)(2,1)S(1)} copy(bf16[96,64,32]{1,2,0:T(8,128)(2,1)} %pad_maximum_fusion.1) | data formatting | bytes 786432 | tf_op jit(solution)/shard_map/concatenate | solution.py:278
  75.0 1.0 copy-done.4
  76.0 0.9 copy-done.5
  76.9 18.4 %shard_map.83 = bf16[16,8,3,32,128]{4,3,2,1,0:T(8,128)(2,1)S(1)} custom-call(bf16[6144,32]{1,0:T(8,128)(2,1)S(1)} %bitcast.38, bf16[32,256]{1,0:T(8,128)(2,1)S(1)} %reshape.531.a1_ref, bf16[512,256]{1,0:T(8,128)(2,1)S(1)} %copy-done.5, bf16[768,256]{1,0:T(8,128)(2,1)S(1)} %copy-done.3, bf16[768,256]{1,0:T(8,128)(2,1)S(1)} %copy-done.4), custom_call_target="tpu_custom_call" | custom-call | tf_op jit(solution)/shard_map/pallas_call | solution.py:153
  95.3 1.7 copy-done.1
  97.0 5.8 %all-to-all-start.1 = ((bf16[128,3,32,128]{3,2,1,0:T(8,128)(2,1)}), bf16[128,3,32,128]{3,2,1,0:T(8,128)(2,1)}, u32[]{:S(2)}, u32[]{:S(2)}) async-start(bf16[128,3,32,128]{3,2,1,0:T(8,128)(2,1)} %bitcast.37), calls=%async_computation.1 | async-start | bytes 6291456 | tf_op jit(solution)/shard_map/all_to_all | solution.py:286
  103.2 2.7 %reduce-precision_convert_fusion = (bf16[32,3,1,128,128]{4,3,2,1,0:T(8,128)(2,1)S(1)}, bf16[32,3,1,128,128]{4,3,2,1,0:T(8,128)(2,1)S(1)}) fusion(f32[32,3]{1,0:T(8,128)S(1)} %bitcast.47, f32[32,3]{1,0:T(8,128)S(1)} %bitcast.46, f32[32,3]{1,0:T(8,128)S(1)} %bitcast.45, pred[128,128]{1,0:T(8,128)(4,1)S(1)} %get-tuple-element.22, ...), kind=kLoop, calls=%fused_computation.4 | loop fusion | flops 14155776 | bytes 6341760 | tf_op jit(solution)/shard_map/convert_element_type | solution.py:186
  105.9 3.2 %pad_maximum_fusion.taps_ref = bf16[32,3,2,128,128]{4,3,2,1,0:T(8,128)(2,1)} fusion(bf16[32,3,1,128,128]{4,3,2,1,0:T(8,128)(2,1)S(1)} %get-tuple-element.10, bf16[32,3,1,128,128]{4,3,2,1,0:T(8,128)(2,1)S(1)} %get-tuple-element.9), kind=kLoop, calls=%fused_computation.6 | loop fusion | flops 3145728 | bytes 12582912 | tf_op jit(solution)/shard_map/stack | solution.py:186
  109.1 1.7 fusion.1.sel_ref
  110.8 33.4 %all-to-all-done.1 = bf16[128,3,32,128]{3,2,1,0:T(8,128)(2,1)} async-done(((bf16[128,3,32,128]{3,2,1,0:T(8,128)(2,1)}), bf16[128,3,32,128]{3,2,1,0:T(8,128)(2,1)}, u32[]{:S(2)}, u32[]{:S(2)}) %all-to-all-start.1) | async-done | bytes 3145760 | tf_op jit(solution)/shard_map/all_to_all | solution.py:286
  144.3 1.6 copy-done.2
  145.8 25.6 %shard_map.84 = bf16[6,32,64,128]{3,2,1,0:T(8,128)(2,1)} custom-call(bf16[16,8,96,128]{3,2,1,0:T(8,128)(2,1)} %bitcast.14.recv_ref, bf16[4,256,1024]{2,1,0:T(8,128)(2,1)S(1)} %copy-done.2, bf16[32,3,2,128,128]{4,3,2,1,0:T(8,128)(2,1)} %pad_maximum_fusion.taps_ref), custom_call_target="tpu_custom_call" | custom-call | tf_op jit(solution)/shard_map/pallas_call | solution.py:234
  (71 shorter events, 6.7 us)
Async XLA Ops:
  0.0 22.5 %copy-start = (bf16[512,1536]{1,0:T(8,128)(2,1)S(1)}, bf16[512,1536]{1,0:T(8,128)(2,1)}, u32[]{:S(2)}) copy-start(bf16[512,1536]{1,0:T(8,128)(2,1)} %param.8) | copy-start | bytes 4718596
  30.4 7.7 %copy-start.6 = (s32[4,16,4]{1,2,0:T(4,128)S(1)}, s32[4,16,4]{1,2,0:T(4,128)}, u32[]{:S(2)}) copy-start(s32[4,16,4]{1,2,0:T(4,128)} %param.9) | copy-start | bytes 3076
  30.4 7.9 %copy-start.8 = (s32[4,16]{1,0:T(4,128)S(1)}, s32[4,16]{1,0:T(4,128)}, u32[]{:S(2)}) copy-start(s32[4,16]{1,0:T(4,128)} %param.10) | copy-start | bytes 772
  30.4 8.4 %copy-start.9 = (bf16[8,64]{1,0:T(8,128)(2,1)S(1)}, bf16[8,64]{1,0:T(8,128)(2,1)}, u32[]{:S(2)}) copy-start(bf16[8,64]{1,0:T(8,128)(2,1)} %param.11) | copy-start | bytes 3076
  30.4 32.0 %all-to-all-start = ((bf16[128,4,1536]{2,1,0:T(4,128)(2,1)}), bf16[128,4,1536]{2,1,0:T(4,128)(2,1)}, u32[]{:S(2)}, u32[]{:S(2)}) async-start(bf16[128,4,1536]{2,1,0:T(4,128)(2,1)} %broadcast_select_fusion), calls=%async_computation | async-start | bytes 3145728 | tf_op jit(solution)/shard_map/all_to_all | solution.py:270
  72.1 2.8 %copy-start.3 = (bf16[768,256]{1,0:T(8,128)(2,1)S(1)}, bf16[768,256]{1,0:T(8,128)(2,1)}, u32[]{:S(2)}) copy-start(bf16[768,256]{1,0:T(8,128)(2,1)} %w3_ref.1) | copy-start | bytes 1179652
  75.0 1.0 copy-start.4
  76.0 0.9 copy-start.5
  95.3 1.7 copy-start.1
  97.0 5.8 %copy-start.7 = (f32[32,9]{0,1:T(8,128)S(1)}, f32[32,9]{0,1:T(8,128)}, u32[]{:S(2)}) copy-start(f32[32,9]{0,1:T(8,128)} %param.15) | copy-start | bytes 3460
  97.0 47.3 %all-to-all-start.1 = ((bf16[128,3,32,128]{3,2,1,0:T(8,128)(2,1)}), bf16[128,3,32,128]{3,2,1,0:T(8,128)(2,1)}, u32[]{:S(2)}, u32[]{:S(2)}) async-start(bf16[128,3,32,128]{3,2,1,0:T(8,128)(2,1)} %bitcast.37), calls=%async_computation.1 | async-start | bytes 6291456 | tf_op jit(solution)/shard_map/all_to_all | solution.py:286
  144.3 1.6 copy-start.2

commit v7 on v6

--- a/solution.py
+++ b/solution.py
@@ -9,25 +9,17 @@
 from jax.sharding import PartitionSpec as P
 
 
-def stack_rows(gathered, counts):
-    running = jnp.zeros((gathered.shape[0], gathered.shape[2]), jnp.float32)
-    for slot_index in range(gathered.shape[1]):
-        live_mask = (slot_index < counts)[:, None]
-        running = running + jnp.where(
-            live_mask, gathered[:, slot_index].astype(jnp.float32), jnp.float32(0.0)
-        )
-    return (running / counts.astype(jnp.float32)[:, None]).astype(jnp.bfloat16)
-
-
-def banded_first_weights(conv1_w):
-    m_index = jnp.arange(32, dtype=jnp.int32)[:, None, None]
-    u_index = jnp.arange(4, dtype=jnp.int32)[None, :, None]
-    tap_index = jnp.arange(8, dtype=jnp.int32)[None, None, :]
-    selector = (m_index - 4 * u_index - 12 == tap_index).astype(jnp.float32)
+def window_first_weights(conv1_w, window):
+    l_index = jnp.arange(window, dtype=jnp.int32)[None, :, None, None]
+    c_index = jnp.arange(9, dtype=jnp.int32)[:, None, None, None]
+    u_index = jnp.arange(4, dtype=jnp.int32)[None, None, :, None]
+    tap_index = jnp.arange(8, dtype=jnp.int32)[None, None, None, :]
+    start = jnp.where(c_index < 8, 16 * c_index + 12, -4)
+    selector = (l_index - start - 4 * u_index == tap_index).astype(jnp.float32)
     return (
-        jnp.einsum("muj,jc->muc", selector, conv1_w.astype(jnp.float32))
+        jnp.einsum("clut,to->cluo", selector, conv1_w.astype(jnp.float32))
         .astype(jnp.bfloat16)
-        .reshape(32, 4 * conv1_w.shape[1])
+        .reshape(9, window, 4 * conv1_w.shape[1])
     )
 
 
@@ -71,15 +63,17 @@
         compiler_params=pltpu.CompilerParams(collective_id=collective_id, has_side_effects=True),
     )(x)
 
-def encoder_kernel(n_il, n_xl, bins, paired_ref, a1_ref, w2_ref, w3_ref, w4_ref, out_ref,
-                   first_pad, second_pad, third_pad):
-    rows = paired_ref.shape[0]
+def encoder_kernel(n_il, n_xl, bins, gathered_ref, counts_ref, b1_ref, w2_ref, w3_ref, w4_ref,
+                   out_ref, stacked, paired, first_pad, second_pad, third_pad):
+    fold, _, samples = gathered_ref.shape
     width = w2_ref.shape[1]
+    rows = first_pad.shape[0] - bins
     chunk = 8 * bins
     n_chunks = rows // chunk
     pair_rows = 2 * bins
     group = width // n_xl
     pairs_per_slab = out_ref.shape[2]
+    blocks = samples // 128
     f32 = jnp.float32
 
     zeros_pad = jnp.zeros((bins, width), jnp.bfloat16)
@@ -89,17 +83,36 @@
     third_pad[pl.ds(0, bins), :] = zeros_pad
     third_pad[pl.ds(bins + rows, bins), :] = zeros_pad
 
+    counts = counts_ref[...]
+    running = jnp.zeros((bins, samples), f32)
+    for slot in range(fold):
+        running = running + jnp.where(slot < counts, gathered_ref[slot].astype(f32), f32(0.0))
+    stacked[:, pl.ds(0, samples)] = (running / counts.astype(f32)).astype(jnp.bfloat16)
+    stacked[:, pl.ds(samples, 128)] = jnp.zeros((bins, 128), jnp.bfloat16)
+    for m in range(blocks):
+        paired[pl.ds(m * bins, bins), :] = stacked[:, pl.ds(m * 128, 256)]
+
     def gelu(x):
         return jax.nn.gelu(x)
 
-    def layer1(ci, carry):
-        r0 = pl.multiple_of(ci * chunk, chunk)
-        x = paired_ref[pl.ds(r0, chunk), :]
-        y = jnp.dot(x, a1_ref[...], preferred_element_type=f32)
-        first_pad[pl.ds(bins + r0, chunk), :] = gelu(y).astype(jnp.bfloat16)
-        return carry
-
-    lax.fori_loop(0, n_chunks, layer1, 0)
+    def layer1(c, carry):
+        y = jnp.dot(paired[...], b1_ref[c], preferred_element_type=f32)
+        y = gelu(y).astype(jnp.bfloat16)
+        for m in range(blocks):
+            step = 1 + c + 8 * m
+            if m == blocks - 1:
+                @pl.when(c < 7)
+                def _():
+                    first_pad[pl.ds(pl.multiple_of(bins + bins * step, bins), bins), :] = (
+                        y[m * bins:(m + 1) * bins])
+            else:
+                first_pad[pl.ds(pl.multiple_of(bins + bins * step, bins), bins), :] = (
+                    y[m * bins:(m + 1) * bins])
+        return carry
+
+    lax.fori_loop(0, 8, layer1, 0)
+    y0 = jnp.dot(paired[pl.ds(0, bins), :], b1_ref[8], preferred_element_type=f32)
+    first_pad[pl.ds(bins, bins), :] = gelu(y0).astype(jnp.bfloat16)
 
     def layer2(ci, carry):
         r0 = pl.multiple_of(ci * chunk, chunk)
@@ -145,23 +158,27 @@
     lax.fori_loop(0, n_chunks, layer4, 0)
 
 
-def encode_to_send(paired, a1, conv2_w, conv3_w, conv4_w, n_il, n_xl, bins, steps):
-    rows = paired.shape[0]
+def encode_to_send(gathered, counts, b1, conv2_w, conv3_w, conv4_w, n_il, n_xl):
+    fold, bins, samples = gathered.shape
+    steps = samples // 16
+    rows = steps * bins
     width = conv2_w.shape[1]
     out_shape = jax.ShapeDtypeStruct(
         (n_il, n_xl, steps // n_il // 2, width // n_xl, 2 * bins), jnp.bfloat16)
     return pl.pallas_call(
         functools.partial(encoder_kernel, n_il, n_xl, bins),
         out_shape=out_shape,
-        in_specs=[pl.BlockSpec(memory_space=pltpu.VMEM)] * 5,
+        in_specs=[pl.BlockSpec(memory_space=pltpu.VMEM)] * 6,
         out_specs=pl.BlockSpec(memory_space=pltpu.VMEM),
         scratch_shapes=[
+            pltpu.VMEM((bins, samples + 128), jnp.bfloat16),
+            pltpu.VMEM((samples // 128 * bins, 256), jnp.bfloat16),
             pltpu.VMEM((bins + rows, width), jnp.bfloat16),
             pltpu.VMEM((2 * bins + rows, width), jnp.bfloat16),
             pltpu.VMEM((2 * bins + rows, width), jnp.bfloat16),
         ],
         compiler_params=pltpu.CompilerParams(vmem_limit_bytes=48 * 1024 * 1024),
-    )(paired, a1, conv2_w, conv3_w, conv4_w)
+    )(gathered, counts, b1, conv2_w, conv3_w, conv4_w)
 
 
 def merge_selectors(n_xl, lanes):
@@ -268,17 +285,13 @@
         wanted.shape[0], wanted.shape[1], samples
     )
     arrived = lax.all_to_all(picked, ("il", "xl"), split_axis=0, concat_axis=0, tiled=True)
-    gathered = jnp.take(arrived.reshape(devices * capacity, samples), position, axis=0).reshape(
-        bin_total, fold_depth, samples
-    )
-    stacked = stack_rows(gathered, fold_counts.reshape(bin_total))
-    steps = samples // 16
-    groups = stacked.reshape(bin_total, steps, 16).transpose(1, 0, 2)
-    previous = jnp.pad(groups, ((1, 0), (0, 0), (0, 0)))[:steps]
-    paired = jnp.concatenate([previous, groups], axis=2).reshape(steps * bin_total, 32)
+    slot_major = position.reshape(bin_total, fold_depth).T.reshape(slot_total)
+    gathered = jnp.take(arrived.reshape(devices * capacity, samples), slot_major, axis=0).reshape(
+        fold_depth, bin_total, samples
+    )
     outgoing = encode_to_send(
-        paired, banded_first_weights(conv1_w), conv2_w, conv3_w, conv4_w,
-        il_count, xl_count, bin_total, steps,
+        gathered, fold_counts.reshape(bin_total, 1), window_first_weights(conv1_w, 256),
+        conv2_w, conv3_w, conv4_w, il_count, xl_count,
     )
     pairs = outgoing.shape[2]
     group_width = outgoing.shape[3]

time: 172 us -> 169 us (0.983)
  waiting for transfers between devices: 56.7 us -> 53.4 us
    all_to_all x1, waiting for transfers between devices: 23.2 us -> 20 us  [per_device(): lax.all_to_all(picked, ('il', 'xl'), split_axis=0, concat_axis=0, tiled=T...]
    reshape x1 -> x3, local copies, waits for them, and re-layouts: 0.1 us -> 2.35 us  [the longest x1 1.57 us: window_first_weights(): return jnp.einsum('clut,to->cluo', selector, conv1_w.astype(jnp.float32))...]
    gather x3 -> x1, local copies, waits for them, and re-layouts: 6.32 us -> 4.55 us  [per_device(): jnp.take(arrived.reshape(devices * capacity, samples), slot_major, axis=0)]
    concatenate x1 -> x0, local copies, waits for them, and re-layouts: 1.77 us -> none  [per_device(): jnp.concatenate([previous, groups], axis=2).reshape(steps * bin_total, 32)]
    unnamed x23 -> x25, local copies, waits for them, and re-layouts: 6.13 us -> 5.9 us
  transfers between devices with their start and end apart: 2 -> 2, of which waited for: 2 -> 2; matrix products, arithmetic and copies ran while one was open for 5% -> 7% of each run, Pallas kernels for 0% -> 0%
where the time goes in v7:
time: 169 us; the launch traced here: 168 us
  Pallas kernels  60.8 us (36%)
  waiting for transfers between devices  53.4 us (32%)
  local copies, waits for them, and re-layouts  26.4 us (16%)
  starting transfers between devices  13.4 us (8%)
  other arithmetic  12.5 us (7%)
    all_to_all x1, waiting for transfers between devices, per_device(): lax.all_to_all(outgoing, ('il', 'xl'), split_axis=0, concat_axis=0, tiled...  33.4 us
    pallas_call x1, Pallas kernels, receive_mix(): pl.pallas_call(receive_kernel, out_shape=jax.ShapeDtypeStruct((n_s, n_o,...  25.6 us
    all_to_all x1, waiting for transfers between devices, per_device(): lax.all_to_all(picked, ('il', 'xl'), split_axis=0, concat_axis=0, tiled=T...  20 us
    pallas_call x1, Pallas kernels, encode_to_send(): pl.pallas_call(functools.partial(encoder_kernel, n_il, n_xl, bins), out_s...  18.6 us
    pallas_call x1, Pallas kernels, exchange(): pl.pallas_call(functools.partial(exchange_kernel, n_il, n_xl), out_shape=...  16.7 us
    all_to_all x1, starting transfers between devices, per_device(): lax.all_to_all(picked, ('il', 'xl'), split_axis=0, concat_axis=0, tiled=T...  7.57 us
    unnamed x25, local copies, waits for them, and re-layouts  5.9 us
    gather x2, local copies, waits for them, and re-layouts, per_device(): jnp.take(traces, wanted.reshape(-1), axis=0)  5.81 us
  transfers between devices with their start and end apart: 2, of which 2 were waited for; matrix products, arithmetic and copies ran while one was open for 7% of the time, Pallas kernels for 0%

profile of v7, /device:TPU:1, one launch (start us, length us, event | category | flops | bytes accessed | tf_op | source)
XLA Modules:
  0.0 168.3 jit_solution(12365020597742995168)
XLA Ops:
  0.0 0.9 copy.18
  1.9 1.4 scatter_custom_fusion
  4.0 16.7 %shard_map.82 = s32[128,4]{1,0:T(8,128)} custom-call(s32[128,4]{1,0:T(8,128)} %reshape.503.x_ref), custom_call_target="tpu_custom_call" | custom-call | tf_op jit(solution)/shard_map/pallas_call | solution.py:57
  20.7 0.9 reshape.504
  22.6 2.9 %gather_fusion = bf16[512,1536]{1,0:T(8,128)(2,1)} fusion(bf16[512,1536]{1,0:T(8,128)(2,1)S(1)} %copy-done, s32[1024]{0:T(1024)S(1)} %pad_clamp_fusion.1), kind=kCustom, calls=%fused_computation | custom fusion | bytes 3147776 | tf_op jit(solution)/shard_map/jit(_take)/gather | solution.py:284
  25.5 2.9 %gather.13 = bf16[128,4,1536]{2,1,0:T(4,128)(2,1)S(1)} reshape(bf16[512,1536]{1,0:T(8,128)(2,1)} %gather_fusion) | data formatting | bytes 3145728 | tf_op jit(solution)/shard_map/jit(_take)/gather | solution.py:284
  28.4 2.0 %broadcast_select_fusion = bf16[128,4,1536]{2,1,0:T(4,128)(2,1)} fusion(bf16[128,4,1536]{2,1,0:T(4,128)(2,1)S(1)} %gather.13, pred[128,4]{1,0:T(8,128)(4,1)S(1)} %compare_and_fusion), kind=kLoop, calls=%fused_computation.10 | loop fusion | flops 786432 | bytes 3146240 | tf_op jit(solution)/shard_map/jit(_take)/select_n | solution.py:284
  30.4 7.6 %all-to-all-start = ((bf16[128,4,1536]{2,1,0:T(4,128)(2,1)}), bf16[128,4,1536]{2,1,0:T(4,128)(2,1)}, u32[]{:S(2)}, u32[]{:S(2)}) async-start(bf16[128,4,1536]{2,1,0:T(4,128)(2,1)} %broadcast_select_fusion), calls=%async_computation | async-start | bytes 3145728 | tf_op jit(solution)/shard_map/all_to_all | solution.py:287
  38.5 1.5 convolution_convert_fusion
  40.1 1.6 copy.25.b1_ref
  42.4 20.0 %all-to-all-done = bf16[128,4,1536]{2,1,0:T(4,128)(2,1)} async-done(((bf16[128,4,1536]{2,1,0:T(4,128)(2,1)}), bf16[128,4,1536]{2,1,0:T(4,128)(2,1)}, u32[]{:S(2)}, u32[]{:S(2)}) %all-to-all-start) | async-done | bytes 1572896 | tf_op jit(solution)/shard_map/all_to_all | solution.py:287
  62.4 3.7 %reshape.505 = bf16[512,1536]{1,0:T(8,128)(2,1)} reshape(bf16[128,4,1536]{2,1,0:T(4,128)(2,1)} %all-to-all-done) | data formatting | bytes 3145728 | tf_op jit(solution)/shard_map/reshape | solution.py:289
  66.1 4.6 %gather_fusion.1 = bf16[256,1536]{1,0:T(8,128)(2,1)} fusion(bf16[512,1536]{1,0:T(8,128)(2,1)} %reshape.505, s32[1024]{0:T(1024)S(1)} %pad_clamp_fusion), kind=kCustom, calls=%fused_computation.1 | custom fusion | bytes 1573888 | tf_op jit(solution)/shard_map/jit(_take)/gather | solution.py:289
  70.6 1.3 broadcast_select_fusion.1.gathered_ref
  71.9 0.9 copy-done.5
  73.6 18.6 %shard_map.83 = bf16[16,8,3,32,128]{4,3,2,1,0:T(8,128)(2,1)S(1)} custom-call(bf16[4,64,1536]{2,1,0:T(8,128)(2,1)S(1)} %broadcast_select_fusion.1.gathered_ref, s32[64,1]{1,0:T(8,128)S(1)} %copy-done.6, bf16[9,256,256]{2,1,0:T(8,128)(2,1)S(1)} %copy.25.b1_ref, bf16[512,256]{1,0:T(8,128)(2,1)S(1)} %copy-done.5, bf16[768,256]{1,0:T(8,128)(2,1)S(1)} %copy-done.3, ...), custom_call_target="tpu_custom_call" | custom-call | tf_op jit(solution)/shard_map/pallas_call | solution.py:168
  92.2 1.7 copy-done.1
  93.9 5.8 %all-to-all-start.1 = ((bf16[128,3,32,128]{3,2,1,0:T(8,128)(2,1)}), bf16[128,3,32,128]{3,2,1,0:T(8,128)(2,1)}, u32[]{:S(2)}, u32[]{:S(2)}) async-start(bf16[128,3,32,128]{3,2,1,0:T(8,128)(2,1)} %bitcast.34), calls=%async_computation.1 | async-start | bytes 6291456 | tf_op jit(solution)/shard_map/all_to_all | solution.py:299
  100.1 2.7 %reduce-precision_convert_fusion = (bf16[32,3,1,128,128]{4,3,2,1,0:T(8,128)(2,1)S(1)}, bf16[32,3,1,128,128]{4,3,2,1,0:T(8,128)(2,1)S(1)}) fusion(f32[32,3]{1,0:T(8,128)S(1)} %bitcast.41, f32[32,3]{1,0:T(8,128)S(1)} %bitcast.40, f32[32,3]{1,0:T(8,128)S(1)} %bitcast.39, pred[128,128]{1,0:T(8,128)(4,1)S(1)} %get-tuple-element.16, ...), kind=kLoop, calls=%fused_computation.4 | loop fusion | flops 14155776 | bytes 6341760 | tf_op jit(solution)/shard_map/convert_element_type | solution.py:203
  102.8 3.2 %pad_maximum_fusion.taps_ref = bf16[32,3,2,128,128]{4,3,2,1,0:T(8,128)(2,1)} fusion(bf16[32,3,1,128,128]{4,3,2,1,0:T(8,128)(2,1)S(1)} %get-tuple-element.8, bf16[32,3,1,128,128]{4,3,2,1,0:T(8,128)(2,1)S(1)} %get-tuple-element.7), kind=kLoop, calls=%fused_computation.6 | loop fusion | flops 3145728 | bytes 12582912 | tf_op jit(solution)/shard_map/stack | solution.py:203
  106.0 1.7 %fusion.1.sel_ref = bf16[4,256,1024]{2,1,0:T(8,128)(2,1)} fusion(s32[4,256]{1,0:T(4,128)S(1)} %add_add_fusion), kind=kLoop, calls=%fused_computation.9 | loop fusion | flops 2097152 | bytes 2101248 | tf_op jit(solution)/shard_map/convert_element_type | solution.py:192
  107.7 33.4 %all-to-all-done.1 = bf16[128,3,32,128]{3,2,1,0:T(8,128)(2,1)} async-done(((bf16[128,3,32,128]{3,2,1,0:T(8,128)(2,1)}), bf16[128,3,32,128]{3,2,1,0:T(8,128)(2,1)}, u32[]{:S(2)}, u32[]{:S(2)}) %all-to-all-start.1) | async-done | bytes 3145760 | tf_op jit(solution)/shard_map/all_to_all | solution.py:299
  141.2 1.6 copy-done.2
  142.8 25.6 %shard_map.84 = bf16[6,32,64,128]{3,2,1,0:T(8,128)(2,1)} custom-call(bf16[16,8,96,128]{3,2,1,0:T(8,128)(2,1)} %bitcast.13.recv_ref, bf16[4,256,1024]{2,1,0:T(8,128)(2,1)S(1)} %copy-done.2, bf16[32,3,2,128,128]{4,3,2,1,0:T(8,128)(2,1)} %pad_maximum_fusion.taps_ref), custom_call_target="tpu_custom_call" | custom-call | tf_op jit(solution)/shard_map/pallas_call | solution.py:251
  (63 shorter events, 5.0 us)
Async XLA Ops:
  0.0 22.5 %copy-start = (bf16[512,1536]{1,0:T(8,128)(2,1)S(1)}, bf16[512,1536]{1,0:T(8,128)(2,1)}, u32[]{:S(2)}) copy-start(bf16[512,1536]{1,0:T(8,128)(2,1)} %param.8) | copy-start | bytes 4718596
  28.4 9.7 %copy-start.7 = (s32[4,16,4]{1,2,0:T(4,128)S(1)}, s32[4,16,4]{1,2,0:T(4,128)}, u32[]{:S(2)}) copy-start(s32[4,16,4]{1,2,0:T(4,128)} %param.9) | copy-start | bytes 3076
  28.4 10.1 %copy-start.9 = (bf16[8,64]{1,0:T(8,128)(2,1)S(1)}, bf16[8,64]{1,0:T(8,128)(2,1)}, u32[]{:S(2)}) copy-start(bf16[8,64]{1,0:T(8,128)(2,1)} %param.11) | copy-start | bytes 3076
  30.4 11.3 %copy-start.10 = (s32[4,16]{1,0:T(4,128)S(1)}, s32[4,16]{1,0:T(4,128)}, u32[]{:S(2)}) copy-start(s32[4,16]{1,0:T(4,128)} %param.10) | copy-start | bytes 772
  30.4 32.0 %all-to-all-start = ((bf16[128,4,1536]{2,1,0:T(4,128)(2,1)}), bf16[128,4,1536]{2,1,0:T(4,128)(2,1)}, u32[]{:S(2)}, u32[]{:S(2)}) async-start(bf16[128,4,1536]{2,1,0:T(4,128)(2,1)} %broadcast_select_fusion), calls=%async_computation | async-start | bytes 3145728 | tf_op jit(solution)/shard_map/all_to_all | solution.py:287
  66.1 5.8 %copy-start.3 = (bf16[768,256]{1,0:T(8,128)(2,1)S(1)}, bf16[768,256]{1,0:T(8,128)(2,1)}, u32[]{:S(2)}) copy-start(bf16[768,256]{1,0:T(8,128)(2,1)} %w3_ref.1) | copy-start | bytes 1179652
  66.1 5.8 %copy-start.4 = (bf16[768,256]{1,0:T(8,128)(2,1)S(1)}, bf16[768,256]{1,0:T(8,128)(2,1)}, u32[]{:S(2)}) copy-start(bf16[768,256]{1,0:T(8,128)(2,1)} %w4_ref.1) | copy-start | bytes 1179652
  71.9 1.0 copy-start.5
  72.9 0.8 copy-start.6
  92.2 1.7 copy-start.1
  93.9 5.8 %copy-start.8 = (f32[32,9]{0,1:T(8,128)S(1)}, f32[32,9]{0,1:T(8,128)}, u32[]{:S(2)}) copy-start(f32[32,9]{0,1:T(8,128)} %param.15) | copy-start | bytes 3460
  93.9 47.3 %all-to-all-start.1 = ((bf16[128,3,32,128]{3,2,1,0:T(8,128)(2,1)}), bf16[128,3,32,128]{3,2,1,0:T(8,128)(2,1)}, u32[]{:S(2)}, u32[]{:S(2)}) async-start(bf16[128,3,32,128]{3,2,1,0:T(8,128)(2,1)} %bitcast.34), calls=%async_computation.1 | async-start | bytes 6291456 | tf_op jit(solution)/shard_map/all_to_all | solution.py:299
  141.2 1.6 copy-start.2

commit v8 on v7

--- a/solution.py
+++ b/solution.py
@@ -63,9 +63,9 @@
         compiler_params=pltpu.CompilerParams(collective_id=collective_id, has_side_effects=True),
     )(x)
 
-def encoder_kernel(n_il, n_xl, bins, gathered_ref, counts_ref, b1_ref, w2_ref, w3_ref, w4_ref,
-                   out_ref, stacked, paired, first_pad, second_pad, third_pad):
-    fold, _, samples = gathered_ref.shape
+def encoder_kernel(n_il, n_xl, bins, arrived_ref, select_ref, counts_ref, b1_ref, w2_ref, w3_ref,
+                   w4_ref, out_ref, stacked, paired, first_pad, second_pad, third_pad):
+    samples = arrived_ref.shape[1]
     width = w2_ref.shape[1]
     rows = first_pad.shape[0] - bins
     chunk = 8 * bins
@@ -84,9 +84,7 @@
     third_pad[pl.ds(bins + rows, bins), :] = zeros_pad
 
     counts = counts_ref[...]
-    running = jnp.zeros((bins, samples), f32)
-    for slot in range(fold):
-        running = running + jnp.where(slot < counts, gathered_ref[slot].astype(f32), f32(0.0))
+    running = jnp.dot(select_ref[...], arrived_ref[...], preferred_element_type=f32)
     stacked[:, pl.ds(0, samples)] = (running / counts.astype(f32)).astype(jnp.bfloat16)
     stacked[:, pl.ds(samples, 128)] = jnp.zeros((bins, 128), jnp.bfloat16)
     for m in range(blocks):
@@ -158,8 +156,9 @@
     lax.fori_loop(0, n_chunks, layer4, 0)
 
 
-def encode_to_send(gathered, counts, b1, conv2_w, conv3_w, conv4_w, n_il, n_xl):
-    fold, bins, samples = gathered.shape
+def encode_to_send(arrived, select, counts, b1, conv2_w, conv3_w, conv4_w, n_il, n_xl):
+    bins = select.shape[0]
+    samples = arrived.shape[1]
     steps = samples // 16
     rows = steps * bins
     width = conv2_w.shape[1]
@@ -168,7 +167,7 @@
     return pl.pallas_call(
         functools.partial(encoder_kernel, n_il, n_xl, bins),
         out_shape=out_shape,
-        in_specs=[pl.BlockSpec(memory_space=pltpu.VMEM)] * 6,
+        in_specs=[pl.BlockSpec(memory_space=pltpu.VMEM)] * 7,
         out_specs=pl.BlockSpec(memory_space=pltpu.VMEM),
         scratch_shapes=[
             pltpu.VMEM((bins, samples + 128), jnp.bfloat16),
@@ -178,7 +177,7 @@
             pltpu.VMEM((2 * bins + rows, width), jnp.bfloat16),
         ],
         compiler_params=pltpu.CompilerParams(vmem_limit_bytes=48 * 1024 * 1024),
-    )(gathered, counts, b1, conv2_w, conv3_w, conv4_w)
+    )(arrived, select, counts, b1, conv2_w, conv3_w, conv4_w)
 
 
 def merge_selectors(n_xl, lanes):
@@ -281,16 +280,15 @@
         .reshape(devices, capacity)
     )
     wanted = exchange(requests, il_count, xl_count, 1)
-    picked = jnp.take(traces, wanted.reshape(-1), axis=0).reshape(
-        wanted.shape[0], wanted.shape[1], samples
-    )
+    picked = jnp.take(traces, wanted.reshape(-1), axis=0)
     arrived = lax.all_to_all(picked, ("il", "xl"), split_axis=0, concat_axis=0, tiled=True)
-    slot_major = position.reshape(bin_total, fold_depth).T.reshape(slot_total)
-    gathered = jnp.take(arrived.reshape(devices * capacity, samples), slot_major, axis=0).reshape(
-        fold_depth, bin_total, samples
-    )
+    live = jnp.arange(fold_depth, dtype=jnp.int32)[None, :] < fold_counts.reshape(bin_total, 1)
+    rows_in = jnp.arange(devices * capacity, dtype=jnp.int32)[None, None, :]
+    select = jnp.any(
+        (position.reshape(bin_total, fold_depth)[:, :, None] == rows_in) & live[:, :, None], axis=1
+    ).astype(jnp.bfloat16)
     outgoing = encode_to_send(
-        gathered, fold_counts.reshape(bin_total, 1), window_first_weights(conv1_w, 256),
+        arrived, select, fold_counts.reshape(bin_total, 1), window_first_weights(conv1_w, 256),
         conv2_w, conv3_w, conv4_w, il_count, xl_count,
     )
     pairs = outgoing.shape[2]

time: 169 us -> 166 us (0.982)
  local copies, waits for them, and re-layouts: 26.4 us -> 22.3 us
  Pallas kernels: 60.8 us -> 62.8 us
    gather x3 -> x2, local copies, waits for them, and re-layouts: 10.4 us -> 5.82 us  [per_device(): picked = jnp.take(traces, wanted.reshape(-1), axis=0)]
    reshape x3 -> x1, local copies, waits for them, and re-layouts: 4.72 us -> 0.94 us  [per_device(): picked = jnp.take(traces, wanted.reshape(-1), axis=0)]
    all_to_all x0 -> x1, local copies, waits for them, and re-layouts: none -> 2.73 us  [per_device(): lax.all_to_all(picked, ('il', 'xl'), split_axis=0, concat_axis=0, tiled=T...]
    pallas_call x1, Pallas kernels: 18.6 us -> 20.4 us  [encode_to_send(): pl.pallas_call(functools.partial(encoder_kernel, n_il, n_xl, bins), out_s...]
    unnamed x25 -> x27, local copies, waits for them, and re-layouts: 5.9 us -> 7.35 us
where the time goes in v8:
time: 166 us; the launch traced here: 165 us
  Pallas kernels  62.8 us (38%)
  waiting for transfers between devices  53.7 us (32%)
  local copies, waits for them, and re-layouts  22.3 us (13%)
  starting transfers between devices  13.4 us (8%)
  other arithmetic  12 us (7%)
    all_to_all x1, waiting for transfers between devices, per_device(): lax.all_to_all(outgoing, ('il', 'xl'), split_axis=0, concat_axis=0, tiled...  33.4 us
    pallas_call x1, Pallas kernels, receive_mix(): pl.pallas_call(receive_kernel, out_shape=jax.ShapeDtypeStruct((n_s, n_o,...  25.6 us
    pallas_call x1, Pallas kernels, encode_to_send(): pl.pallas_call(functools.partial(encoder_kernel, n_il, n_xl, bins), out_s...  20.4 us
    all_to_all x1, waiting for transfers between devices, per_device(): lax.all_to_all(picked, ('il', 'xl'), split_axis=0, concat_axis=0, tiled=T...  20.3 us
    pallas_call x1, Pallas kernels, exchange(): pl.pallas_call(functools.partial(exchange_kernel, n_il, n_xl), out_shape=...  16.8 us
    all_to_all x1, starting transfers between devices, per_device(): lax.all_to_all(picked, ('il', 'xl'), split_axis=0, concat_axis=0, tiled=T...  7.59 us
    unnamed x27, local copies, waits for them, and re-layouts  7.35 us
    gather x2, local copies, waits for them, and re-layouts, per_device(): picked = jnp.take(traces, wanted.reshape(-1), axis=0)  5.82 us
  transfers between devices with their start and end apart: 2, of which 2 were waited for; matrix products, arithmetic and copies ran while one was open for 7% of the time, Pallas kernels for 0%

profile of v8, /device:TPU:1, one launch (start us, length us, event | category | flops | bytes accessed | tf_op | source)
XLA Modules:
  0.0 165.0 jit_solution(15573531546807350893)
XLA Ops:
  0.0 0.9 copy.30
  1.9 1.4 scatter_custom_fusion
  4.0 16.8 %shard_map.82 = s32[128,4]{1,0:T(8,128)} custom-call(s32[128,4]{1,0:T(8,128)} %reshape.514.x_ref), custom_call_target="tpu_custom_call" | custom-call | tf_op jit(solution)/shard_map/pallas_call | solution.py:57
  20.8 0.9 reshape.515
  21.8 0.9 compare_and_fusion
  22.7 2.9 %gather_fusion = bf16[512,1536]{1,0:T(8,128)(2,1)} fusion(bf16[512,1536]{1,0:T(8,128)(2,1)S(1)} %copy-done, s32[1024]{0:T(1024)S(1)} %pad_clamp_fusion), kind=kCustom, calls=%fused_computation | custom fusion | bytes 3147776 | tf_op jit(solution)/shard_map/jit(_take)/gather | solution.py:283
  25.6 2.9 %gather.7 = bf16[128,4,1536]{2,1,0:T(4,128)(2,1)S(1)} reshape(bf16[512,1536]{1,0:T(8,128)(2,1)} %gather_fusion) | data formatting | bytes 3145728 | tf_op jit(solution)/shard_map/jit(_take)/gather | solution.py:283
  28.5 2.0 %broadcast_select_fusion = bf16[128,4,1536]{2,1,0:T(4,128)(2,1)} fusion(bf16[128,4,1536]{2,1,0:T(4,128)(2,1)S(1)} %gather.7, pred[128,4]{1,0:T(8,128)(4,1)S(1)} %compare_and_fusion), kind=kLoop, calls=%fused_computation.9 | loop fusion | flops 786432 | bytes 3146240 | tf_op jit(solution)/shard_map/jit(_take)/select_n | solution.py:283
  30.5 7.6 %all-to-all-start = ((bf16[128,4,1536]{2,1,0:T(4,128)(2,1)}), bf16[128,4,1536]{2,1,0:T(4,128)(2,1)}, u32[]{:S(2)}, u32[]{:S(2)}) async-start(bf16[128,4,1536]{2,1,0:T(4,128)(2,1)} %broadcast_select_fusion), calls=%async_computation | async-start | bytes 3145728 | tf_op jit(solution)/shard_map/all_to_all | solution.py:284
  40.7 1.5 copy.38.b1_ref
  42.2 20.3 %all-to-all-done = bf16[128,4,1536]{2,1,0:T(4,128)(2,1)} async-done(((bf16[128,4,1536]{2,1,0:T(4,128)(2,1)}), bf16[128,4,1536]{2,1,0:T(4,128)(2,1)}, u32[]{:S(2)}, u32[]{:S(2)}) %all-to-all-start) | async-done | bytes 1572896 | tf_op jit(solution)/shard_map/all_to_all | solution.py:284
  62.5 2.7 %all_to_all.9.arrived_ref = bf16[512,1536]{1,0:T(8,128)(2,1)S(1)} reshape(bf16[128,4,1536]{2,1,0:T(4,128)(2,1)} %all-to-all-done) | data formatting | bytes 3145728 | tf_op jit(solution)/shard_map/all_to_all | solution.py:284
  65.3 1.3 copy-done.2
  66.5 1.0 copy-done.4
  67.5 0.8 copy-done.5
  68.4 0.9 copy-done.6
  70.1 20.4 %shard_map.83 = bf16[16,8,3,32,128]{4,3,2,1,0:T(8,128)(2,1)} custom-call(bf16[512,1536]{1,0:T(8,128)(2,1)S(1)} %all_to_all.9.arrived_ref, bf16[64,512]{1,0:T(8,128)(2,1)S(1)} %copy-done.5, s32[64,1]{1,0:T(8,128)S(1)} %copy-done.7, bf16[9,256,256]{2,1,0:T(8,128)(2,1)S(1)} %copy-done.2, bf16[512,256]{1,0:T(8,128)(2,1)S(1)} %copy-done.6, ...), custom_call_target="tpu_custom_call" | custom-call | tf_op jit(solution)/shard_map/pallas_call | solution.py:167
  90.5 5.8 %all-to-all-start.1 = ((bf16[128,3,32,128]{3,2,1,0:T(8,128)(2,1)}), bf16[128,3,32,128]{3,2,1,0:T(8,128)(2,1)}, u32[]{:S(2)}, u32[]{:S(2)}) async-start(bf16[128,3,32,128]{3,2,1,0:T(8,128)(2,1)} %bitcast.29), calls=%async_computation.1 | async-start | bytes 6291456 | tf_op jit(solution)/shard_map/all_to_all | solution.py:297
  96.7 2.7 %reduce-precision_convert_fusion = (bf16[32,3,1,128,128]{4,3,2,1,0:T(8,128)(2,1)S(1)}, bf16[32,3,1,128,128]{4,3,2,1,0:T(8,128)(2,1)S(1)}) fusion(f32[32,3]{1,0:T(8,128)S(1)} %bitcast.35, f32[32,3]{1,0:T(8,128)S(1)} %bitcast.34, f32[32,3]{1,0:T(8,128)S(1)} %bitcast.33, pred[128,128]{1,0:T(8,128)(4,1)S(1)} %get-tuple-element.14, ...), kind=kLoop, calls=%fused_computation.3 | loop fusion | flops 14155776 | bytes 6341760 | tf_op jit(solution)/shard_map/convert_element_type | solution.py:202
  99.4 3.2 %pad_maximum_fusion.taps_ref = bf16[32,3,2,128,128]{4,3,2,1,0:T(8,128)(2,1)} fusion(bf16[32,3,1,128,128]{4,3,2,1,0:T(8,128)(2,1)S(1)} %get-tuple-element.6, bf16[32,3,1,128,128]{4,3,2,1,0:T(8,128)(2,1)S(1)} %get-tuple-element.5), kind=kLoop, calls=%fused_computation.5 | loop fusion | flops 3145728 | bytes 12582912 | tf_op jit(solution)/shard_map/stack | solution.py:202
  102.6 1.7 %fusion.1.sel_ref = bf16[4,256,1024]{2,1,0:T(8,128)(2,1)} fusion(s32[4,256]{1,0:T(4,128)S(1)} %add_add_fusion), kind=kLoop, calls=%fused_computation.8 | loop fusion | flops 2097152 | bytes 2101248 | tf_op jit(solution)/shard_map/convert_element_type | solution.py:191
  104.3 33.4 %all-to-all-done.1 = bf16[128,3,32,128]{3,2,1,0:T(8,128)(2,1)} async-done(((bf16[128,3,32,128]{3,2,1,0:T(8,128)(2,1)}), bf16[128,3,32,128]{3,2,1,0:T(8,128)(2,1)}, u32[]{:S(2)}, u32[]{:S(2)}) %all-to-all-start.1) | async-done | bytes 3145760 | tf_op jit(solution)/shard_map/all_to_all | solution.py:297
  137.8 1.6 copy-done.1
  139.4 25.6 %shard_map.84 = bf16[6,32,64,128]{3,2,1,0:T(8,128)(2,1)} custom-call(bf16[16,8,96,128]{3,2,1,0:T(8,128)(2,1)} %bitcast.10.recv_ref, bf16[4,256,1024]{2,1,0:T(8,128)(2,1)S(1)} %copy-done.1, bf16[32,3,2,128,128]{4,3,2,1,0:T(8,128)(2,1)} %pad_maximum_fusion.taps_ref), custom_call_target="tpu_custom_call" | custom-call | tf_op jit(solution)/shard_map/pallas_call | solution.py:250
  (64 shorter events, 5.4 us)
Async XLA Ops:
  0.0 22.7 %copy-start = (bf16[512,1536]{1,0:T(8,128)(2,1)S(1)}, bf16[512,1536]{1,0:T(8,128)(2,1)}, u32[]{:S(2)}) copy-start(bf16[512,1536]{1,0:T(8,128)(2,1)} %param.8) | copy-start | bytes 4718596
  28.5 9.7 %copy-start.8 = (s32[4,16,4]{1,2,0:T(4,128)S(1)}, s32[4,16,4]{1,2,0:T(4,128)}, u32[]{:S(2)}) copy-start(s32[4,16,4]{1,2,0:T(4,128)} %param.9) | copy-start | bytes 3076
  28.5 9.7 %copy-start.9 = (s32[4,16]{1,0:T(4,128)S(1)}, s32[4,16]{1,0:T(4,128)}, u32[]{:S(2)}) copy-start(s32[4,16]{1,0:T(4,128)} %param.10) | copy-start | bytes 772
  28.5 11.6 %copy-start.11 = (bf16[8,64]{1,0:T(8,128)(2,1)S(1)}, bf16[8,64]{1,0:T(8,128)(2,1)}, u32[]{:S(2)}) copy-start(bf16[8,64]{1,0:T(8,128)(2,1)} %param.11) | copy-start | bytes 3076
  30.5 32.0 %all-to-all-start = ((bf16[128,4,1536]{2,1,0:T(4,128)(2,1)}), bf16[128,4,1536]{2,1,0:T(4,128)(2,1)}, u32[]{:S(2)}, u32[]{:S(2)}) async-start(bf16[128,4,1536]{2,1,0:T(4,128)(2,1)} %broadcast_select_fusion), calls=%async_computation | async-start | bytes 3145728 | tf_op jit(solution)/shard_map/all_to_all | solution.py:284
  40.2 25.1 %copy-start.3 = (bf16[768,256]{1,0:T(8,128)(2,1)S(1)}, bf16[768,256]{1,0:T(8,128)(2,1)}, u32[]{:S(2)}) copy-start(bf16[768,256]{1,0:T(8,128)(2,1)} %w3_ref.1) | copy-start | bytes 1179652
  65.3 1.3 copy-start.2
  66.5 1.0 copy-start.4
  67.5 0.8 copy-start.5
  68.4 0.9 copy-start.6
  69.3 0.8 copy-start.7
  90.5 5.8 %copy-start.10 = (f32[32,9]{0,1:T(8,128)S(1)}, f32[32,9]{0,1:T(8,128)}, u32[]{:S(2)}) copy-start(f32[32,9]{0,1:T(8,128)} %param.15) | copy-start | bytes 3460
  90.5 47.3 %all-to-all-start.1 = ((bf16[128,3,32,128]{3,2,1,0:T(8,128)(2,1)}), bf16[128,3,32,128]{3,2,1,0:T(8,128)(2,1)}, u32[]{:S(2)}, u32[]{:S(2)}) async-start(bf16[128,3,32,128]{3,2,1,0:T(8,128)(2,1)} %bitcast.29), calls=%async_computation.1 | async-start | bytes 6291456 | tf_op jit(solution)/shard_map/all_to_all | solution.py:297
  137.8 1.6 copy-start.1

commit v9 on v8

--- a/solution.py
+++ b/solution.py
@@ -29,15 +29,6 @@
 def exchange_kernel(n_il, n_xl, x_ref, y_ref, send_sem, recv_sem):
     n = n_il * n_xl
     me = lax.axis_index("il") * n_xl + lax.axis_index("xl")
-    barrier = pltpu.get_barrier_semaphore()
-
-    def greet(k, carry):
-        d = lax.rem(me + 1 + k, n)
-        pl.semaphore_signal(barrier, inc=1, device_id=(d // n_xl, d % n_xl), device_id_type=MESH)
-        return carry
-
-    lax.fori_loop(0, n - 1, greet, 0)
-    pl.semaphore_wait(barrier, n - 1)
     pltpu.make_async_copy(x_ref.at[me], y_ref.at[me], recv_sem).start()
 
     def send(k, carry):
@@ -53,14 +44,14 @@
     pltpu.make_async_copy(x_ref.at[pl.ds(0, n - 1)], y_ref.at[pl.ds(0, n - 1)], send_sem).wait()
 
 
-def exchange(x, n_il, n_xl, collective_id):
+def exchange(x, n_il, n_xl):
     return pl.pallas_call(
         functools.partial(exchange_kernel, n_il, n_xl),
         out_shape=jax.ShapeDtypeStruct(x.shape, x.dtype),
         in_specs=[pl.BlockSpec(memory_space=pl.ANY)],
         out_specs=pl.BlockSpec(memory_space=pl.ANY),
         scratch_shapes=[pltpu.SemaphoreType.DMA(()), pltpu.SemaphoreType.DMA(())],
-        compiler_params=pltpu.CompilerParams(collective_id=collective_id, has_side_effects=True),
+        compiler_params=pltpu.CompilerParams(has_side_effects=True),
     )(x)
 
 def encoder_kernel(n_il, n_xl, bins, arrived_ref, select_ref, counts_ref, b1_ref, w2_ref, w3_ref,
@@ -279,7 +270,7 @@
         .set(local_row)
         .reshape(devices, capacity)
     )
-    wanted = exchange(requests, il_count, xl_count, 1)
+    wanted = exchange(requests, il_count, xl_count)
     picked = jnp.take(traces, wanted.reshape(-1), axis=0)
     arrived = lax.all_to_all(picked, ("il", "xl"), split_axis=0, concat_axis=0, tiled=True)
     live = jnp.arange(fold_depth, dtype=jnp.int32)[None, :] < fold_counts.reshape(bin_total, 1)

time: 166 us -> 168 us (1.012)
  Pallas kernels: 62.8 us -> 67.2 us
  starting transfers between devices: 13.4 us -> 11.4 us
    pallas_call x1, Pallas kernels: 16.8 us -> 21.2 us  [exchange(): pl.pallas_call(functools.partial(exchange_kernel, n_il, n_xl), out_shape=...]
    all_to_all x1, starting transfers between devices: 7.59 us -> 5.6 us  [per_device(): lax.all_to_all(picked, ('il', 'xl'), split_axis=0, concat_axis=0, tiled=T...]
where the time goes in v9:
time: 168 us; the launch traced here: 167 us
  Pallas kernels  67.2 us (40%)
  waiting for transfers between devices  53.7 us (32%)
  local copies, waits for them, and re-layouts  22.3 us (13%)
  other arithmetic  12 us (7%)
  starting transfers between devices  11.4 us (7%)
    all_to_all x1, waiting for transfers between devices, per_device(): lax.all_to_all(outgoing, ('il', 'xl'), split_axis=0, concat_axis=0, tiled...  33.4 us
    pallas_call x1, Pallas kernels, receive_mix(): pl.pallas_call(receive_kernel, out_shape=jax.ShapeDtypeStruct((n_s, n_o,...  25.6 us
    pallas_call x1, Pallas kernels, exchange(): pl.pallas_call(functools.partial(exchange_kernel, n_il, n_xl), out_shape=...  21.2 us
    pallas_call x1, Pallas kernels, encode_to_send(): pl.pallas_call(functools.partial(encoder_kernel, n_il, n_xl, bins), out_s...  20.4 us
    all_to_all x1, waiting for transfers between devices, per_device(): lax.all_to_all(picked, ('il', 'xl'), split_axis=0, concat_axis=0, tiled=T...  20.3 us
    unnamed x27, local copies, waits for them, and re-layouts  7.35 us
    gather x2, local copies, waits for them, and re-layouts, per_device(): picked = jnp.take(traces, wanted.reshape(-1), axis=0)  5.81 us
    all_to_all x1, starting transfers between devices, per_device(): lax.all_to_all(outgoing, ('il', 'xl'), split_axis=0, concat_axis=0, tiled...  5.77 us
  transfers between devices with their start and end apart: 2, of which 2 were waited for; matrix products, arithmetic and copies ran while one was open for 7% of the time, Pallas kernels for 0%

profile of v9, /device:TPU:1, one launch (start us, length us, event | category | flops | bytes accessed | tf_op | source)
XLA Modules:
  0.0 167.4 jit_solution(10192243097073765481)
XLA Ops:
  0.0 0.9 copy.30
  1.9 1.4 scatter_custom_fusion
  4.0 21.2 %shard_map.82 = s32[128,4]{1,0:T(8,128)} custom-call(s32[128,4]{1,0:T(8,128)} %reshape.514.x_ref), custom_call_target="tpu_custom_call" | custom-call | tf_op jit(solution)/shard_map/pallas_call | solution.py:48
  25.2 0.9 reshape.515
  26.2 0.9 compare_and_fusion
  27.1 2.9 %gather_fusion = bf16[512,1536]{1,0:T(8,128)(2,1)} fusion(bf16[512,1536]{1,0:T(8,128)(2,1)S(1)} %copy-done, s32[1024]{0:T(1024)S(1)} %pad_clamp_fusion), kind=kCustom, calls=%fused_computation | custom fusion | bytes 3147776 | tf_op jit(solution)/shard_map/jit(_take)/gather | solution.py:274
  30.0 2.9 %gather.7 = bf16[128,4,1536]{2,1,0:T(4,128)(2,1)S(1)} reshape(bf16[512,1536]{1,0:T(8,128)(2,1)} %gather_fusion) | data formatting | bytes 3145728 | tf_op jit(solution)/shard_map/jit(_take)/gather | solution.py:274
  33.0 2.0 %broadcast_select_fusion = bf16[128,4,1536]{2,1,0:T(4,128)(2,1)} fusion(bf16[128,4,1536]{2,1,0:T(4,128)(2,1)S(1)} %gather.7, pred[128,4]{1,0:T(8,128)(4,1)S(1)} %compare_and_fusion), kind=kLoop, calls=%fused_computation.9 | loop fusion | flops 786432 | bytes 3146240 | tf_op jit(solution)/shard_map/jit(_take)/select_n | solution.py:274
  34.9 5.6 %all-to-all-start = ((bf16[128,4,1536]{2,1,0:T(4,128)(2,1)}), bf16[128,4,1536]{2,1,0:T(4,128)(2,1)}, u32[]{:S(2)}, u32[]{:S(2)}) async-start(bf16[128,4,1536]{2,1,0:T(4,128)(2,1)} %broadcast_select_fusion), calls=%async_computation | async-start | bytes 3145728 | tf_op jit(solution)/shard_map/all_to_all | solution.py:275
  43.1 1.5 copy.38.b1_ref
  44.6 20.3 %all-to-all-done = bf16[128,4,1536]{2,1,0:T(4,128)(2,1)} async-done(((bf16[128,4,1536]{2,1,0:T(4,128)(2,1)}), bf16[128,4,1536]{2,1,0:T(4,128)(2,1)}, u32[]{:S(2)}, u32[]{:S(2)}) %all-to-all-start) | async-done | bytes 1572896 | tf_op jit(solution)/shard_map/all_to_all | solution.py:275
  64.9 2.7 %all_to_all.9.arrived_ref = bf16[512,1536]{1,0:T(8,128)(2,1)S(1)} reshape(bf16[128,4,1536]{2,1,0:T(4,128)(2,1)} %all-to-all-done) | data formatting | bytes 3145728 | tf_op jit(solution)/shard_map/all_to_all | solution.py:275
  67.7 1.3 copy-done.2
  69.0 1.0 copy-done.4
  70.0 0.8 copy-done.5
  70.8 0.9 copy-done.6
  72.5 20.4 %shard_map.83 = bf16[16,8,3,32,128]{4,3,2,1,0:T(8,128)(2,1)} custom-call(bf16[512,1536]{1,0:T(8,128)(2,1)S(1)} %all_to_all.9.arrived_ref, bf16[64,512]{1,0:T(8,128)(2,1)S(1)} %copy-done.5, s32[64,1]{1,0:T(8,128)S(1)} %copy-done.7, bf16[9,256,256]{2,1,0:T(8,128)(2,1)S(1)} %copy-done.2, bf16[512,256]{1,0:T(8,128)(2,1)S(1)} %copy-done.6, ...), custom_call_target="tpu_custom_call" | custom-call | tf_op jit(solution)/shard_map/pallas_call | solution.py:158
  92.9 5.8 %all-to-all-start.1 = ((bf16[128,3,32,128]{3,2,1,0:T(8,128)(2,1)}), bf16[128,3,32,128]{3,2,1,0:T(8,128)(2,1)}, u32[]{:S(2)}, u32[]{:S(2)}) async-start(bf16[128,3,32,128]{3,2,1,0:T(8,128)(2,1)} %bitcast.29), calls=%async_computation.1 | async-start | bytes 6291456 | tf_op jit(solution)/shard_map/all_to_all | solution.py:288
  99.1 2.7 %reduce-precision_convert_fusion = (bf16[32,3,1,128,128]{4,3,2,1,0:T(8,128)(2,1)S(1)}, bf16[32,3,1,128,128]{4,3,2,1,0:T(8,128)(2,1)S(1)}) fusion(f32[32,3]{1,0:T(8,128)S(1)} %bitcast.35, f32[32,3]{1,0:T(8,128)S(1)} %bitcast.34, f32[32,3]{1,0:T(8,128)S(1)} %bitcast.33, pred[128,128]{1,0:T(8,128)(4,1)S(1)} %get-tuple-element.14, ...), kind=kLoop, calls=%fused_computation.3 | loop fusion | flops 14155776 | bytes 6341760 | tf_op jit(solution)/shard_map/convert_element_type | solution.py:193
  101.8 3.2 %pad_maximum_fusion.taps_ref = bf16[32,3,2,128,128]{4,3,2,1,0:T(8,128)(2,1)} fusion(bf16[32,3,1,128,128]{4,3,2,1,0:T(8,128)(2,1)S(1)} %get-tuple-element.6, bf16[32,3,1,128,128]{4,3,2,1,0:T(8,128)(2,1)S(1)} %get-tuple-element.5), kind=kLoop, calls=%fused_computation.5 | loop fusion | flops 3145728 | bytes 12582912 | tf_op jit(solution)/shard_map/stack | solution.py:193
  105.0 1.7 %fusion.1.sel_ref = bf16[4,256,1024]{2,1,0:T(8,128)(2,1)} fusion(s32[4,256]{1,0:T(4,128)S(1)} %add_add_fusion), kind=kLoop, calls=%fused_computation.8 | loop fusion | flops 2097152 | bytes 2101248 | tf_op jit(solution)/shard_map/convert_element_type | solution.py:182
  106.7 33.4 %all-to-all-done.1 = bf16[128,3,32,128]{3,2,1,0:T(8,128)(2,1)} async-done(((bf16[128,3,32,128]{3,2,1,0:T(8,128)(2,1)}), bf16[128,3,32,128]{3,2,1,0:T(8,128)(2,1)}, u32[]{:S(2)}, u32[]{:S(2)}) %all-to-all-start.1) | async-done | bytes 3145760 | tf_op jit(solution)/shard_map/all_to_all | solution.py:288
  140.2 1.6 copy-done.1
  141.8 25.6 %shard_map.84 = bf16[6,32,64,128]{3,2,1,0:T(8,128)(2,1)} custom-call(bf16[16,8,96,128]{3,2,1,0:T(8,128)(2,1)} %bitcast.10.recv_ref, bf16[4,256,1024]{2,1,0:T(8,128)(2,1)S(1)} %copy-done.1, bf16[32,3,2,128,128]{4,3,2,1,0:T(8,128)(2,1)} %pad_maximum_fusion.taps_ref), custom_call_target="tpu_custom_call" | custom-call | tf_op jit(solution)/shard_map/pallas_call | solution.py:241
  (64 shorter events, 5.4 us)
Async XLA Ops:
  0.0 27.1 %copy-start = (bf16[512,1536]{1,0:T(8,128)(2,1)S(1)}, bf16[512,1536]{1,0:T(8,128)(2,1)}, u32[]{:S(2)}) copy-start(bf16[512,1536]{1,0:T(8,128)(2,1)} %param.8) | copy-start | bytes 4718596
  32.9 7.7 %copy-start.8 = (s32[4,16,4]{1,2,0:T(4,128)S(1)}, s32[4,16,4]{1,2,0:T(4,128)}, u32[]{:S(2)}) copy-start(s32[4,16,4]{1,2,0:T(4,128)} %param.9) | copy-start | bytes 3076
  32.9 7.7 %copy-start.9 = (s32[4,16]{1,0:T(4,128)S(1)}, s32[4,16]{1,0:T(4,128)}, u32[]{:S(2)}) copy-start(s32[4,16]{1,0:T(4,128)} %param.10) | copy-start | bytes 772
  32.9 9.6 %copy-start.11 = (bf16[8,64]{1,0:T(8,128)(2,1)S(1)}, bf16[8,64]{1,0:T(8,128)(2,1)}, u32[]{:S(2)}) copy-start(bf16[8,64]{1,0:T(8,128)(2,1)} %param.11) | copy-start | bytes 3076
  34.9 30.0 %all-to-all-start = ((bf16[128,4,1536]{2,1,0:T(4,128)(2,1)}), bf16[128,4,1536]{2,1,0:T(4,128)(2,1)}, u32[]{:S(2)}, u32[]{:S(2)}) async-start(bf16[128,4,1536]{2,1,0:T(4,128)(2,1)} %broadcast_select_fusion), calls=%async_computation | async-start | bytes 3145728 | tf_op jit(solution)/shard_map/all_to_all | solution.py:275
  42.6 25.1 %copy-start.3 = (bf16[768,256]{1,0:T(8,128)(2,1)S(1)}, bf16[768,256]{1,0:T(8,128)(2,1)}, u32[]{:S(2)}) copy-start(bf16[768,256]{1,0:T(8,128)(2,1)} %w3_ref.1) | copy-start | bytes 1179652
  67.7 1.3 copy-start.2
  69.0 1.0 copy-start.4
  70.0 0.8 copy-start.5
  70.8 0.9 copy-start.6
  71.7 0.8 copy-start.7
  92.9 5.8 %copy-start.10 = (f32[32,9]{0,1:T(8,128)S(1)}, f32[32,9]{0,1:T(8,128)}, u32[]{:S(2)}) copy-start(f32[32,9]{0,1:T(8,128)} %param.15) | copy-start | bytes 3460
  92.9 47.3 %all-to-all-start.1 = ((bf16[128,3,32,128]{3,2,1,0:T(8,128)(2,1)}), bf16[128,3,32,128]{3,2,1,0:T(8,128)(2,1)}, u32[]{:S(2)}, u32[]{:S(2)}) async-start(bf16[128,3,32,128]{3,2,1,0:T(8,128)(2,1)} %bitcast.29), calls=%async_computation.1 | async-start | bytes 6291456 | tf_op jit(solution)/shard_map/all_to_all | solution.py:288
  140.2 1.6 copy-start.1

commit v10 on v8

--- a/solution.py
+++ b/solution.py
@@ -276,12 +276,13 @@
     requests = (
         jnp.zeros((devices * capacity,), jnp.int32)
         .at[position]
-        .set(local_row)
+        .set(local_row, mode="promise_in_bounds", unique_indices=True)
         .reshape(devices, capacity)
     )
     wanted = exchange(requests, il_count, xl_count, 1)
-    picked = jnp.take(traces, wanted.reshape(-1), axis=0)
+    picked = jnp.take(traces, wanted, axis=0, mode="clip")
     arrived = lax.all_to_all(picked, ("il", "xl"), split_axis=0, concat_axis=0, tiled=True)
+    arrived = arrived.reshape(devices * capacity, samples)
     live = jnp.arange(fold_depth, dtype=jnp.int32)[None, :] < fold_counts.reshape(bin_total, 1)
     rows_in = jnp.arange(devices * capacity, dtype=jnp.int32)[None, None, :]
     select = jnp.any(

time: 166 us -> 160 us (0.964)
  other arithmetic: 12 us -> 9.16 us
  local copies, waits for them, and re-layouts: 22.3 us -> 19.9 us
    all_to_all x1 -> x0, local copies, waits for them, and re-layouts: 2.73 us -> none  [per_device(): lax.all_to_all(picked, ('il', 'xl'), split_axis=0, concat_axis=0, tiled=T...]
    gather x2, local copies, waits for them, and re-layouts: 5.82 us -> 3.47 us  [per_device(): picked = jnp.take(traces, wanted, axis=0, mode='clip')]
    select_n x2 -> x0, other arithmetic: 1.98 us -> none  [per_device(): picked = jnp.take(traces, wanted.reshape(-1), axis=0)]
    reshape x1, local copies, waits for them, and re-layouts: 0.94 us -> 2.73 us  [per_device(): arrived = arrived.reshape(devices * capacity, samples)]
  transfers between devices with their start and end apart: 2 -> 2, of which waited for: 2 -> 2; matrix products, arithmetic and copies ran while one was open for 7% -> 8% of each run, Pallas kernels for 0% -> 0%
where the time goes in v10:
time: 160 us
  Pallas kernels  62.8 us (39%)
  waiting for transfers between devices  53.8 us (34%)
  local copies, waits for them, and re-layouts  19.9 us (12%)
  starting transfers between devices  13.4 us (8%)
  other arithmetic  9.16 us (6%)
    all_to_all x1, waiting for transfers between devices, per_device(): lax.all_to_all(outgoing, ('il', 'xl'), split_axis=0, concat_axis=0, tiled...  33.4 us
    pallas_call x1, Pallas kernels, receive_mix(): pl.pallas_call(receive_kernel, out_shape=jax.ShapeDtypeStruct((n_s, n_o,...  25.6 us
    pallas_call x1, Pallas kernels, encode_to_send(): pl.pallas_call(functools.partial(encoder_kernel, n_il, n_xl, bins), out_s...  20.4 us
    all_to_all x1, waiting for transfers between devices, per_device(): lax.all_to_all(picked, ('il', 'xl'), split_axis=0, concat_axis=0, tiled=T...  20.3 us
    pallas_call x1, Pallas kernels, exchange(): pl.pallas_call(functools.partial(exchange_kernel, n_il, n_xl), out_shape=...  16.8 us
    all_to_all x1, starting transfers between devices, per_device(): lax.all_to_all(picked, ('il', 'xl'), split_axis=0, concat_axis=0, tiled=T...  7.6 us
    unnamed x27, local copies, waits for them, and re-layouts  7.35 us
    all_to_all x1, starting transfers between devices, per_device(): lax.all_to_all(outgoing, ('il', 'xl'), split_axis=0, concat_axis=0, tiled...  5.77 us
  transfers between devices with their start and end apart: 2, of which 2 were waited for; matrix products, arithmetic and copies ran while one was open for 8% of the time, Pallas kernels for 0%

profile of v10, /device:TPU:1, one launch (start us, length us, event | category | flops | bytes accessed | tf_op | source)
XLA Modules:
  0.0 159.8 jit_solution(16626216279959151342)
XLA Ops:
  0.0 0.9 copy.30
  1.9 1.4 scatter_custom_fusion
  3.3 0.7 reshape.473.x_ref
  4.0 16.8 %shard_map.82 = s32[128,4]{1,0:T(8,128)} custom-call(s32[128,4]{1,0:T(8,128)} %reshape.473.x_ref), custom_call_target="tpu_custom_call" | custom-call | tf_op jit(solution)/shard_map/pallas_call | solution.py:57
  20.8 0.9 reshape.483
  21.8 2.1 %gather_fusion = bf16[512,1536]{1,0:T(8,128)(2,1)S(1)} fusion(bf16[512,1536]{1,0:T(8,128)(2,1)S(1)} %copy-done, s32[1024]{0:T(1024)S(1)} %pad_clamp_fusion), kind=kCustom, calls=%fused_computation | custom fusion | bytes 3147776 | tf_op jit(solution)/shard_map/jit(_take)/gather | solution.py:283
  24.0 1.3 reshape.482
  25.3 7.6 %all-to-all-start = ((bf16[128,4,1536]{2,1,0:T(4,128)(2,1)}), bf16[128,4,1536]{2,1,0:T(4,128)(2,1)}, u32[]{:S(2)}, u32[]{:S(2)}) async-start(bf16[128,4,1536]{2,1,0:T(4,128)(2,1)} %reshape.482), calls=%async_computation | async-start | bytes 3145728 | tf_op jit(solution)/shard_map/all_to_all | solution.py:284
  35.5 1.5 copy.38.b1_ref
  37.0 20.3 %all-to-all-done = bf16[128,4,1536]{2,1,0:T(4,128)(2,1)} async-done(((bf16[128,4,1536]{2,1,0:T(4,128)(2,1)}), bf16[128,4,1536]{2,1,0:T(4,128)(2,1)}, u32[]{:S(2)}, u32[]{:S(2)}) %all-to-all-start) | async-done | bytes 1572896 | tf_op jit(solution)/shard_map/all_to_all | solution.py:284
  57.3 2.7 %reshape.474.arrived_ref = bf16[512,1536]{1,0:T(8,128)(2,1)S(1)} reshape(bf16[128,4,1536]{2,1,0:T(4,128)(2,1)} %all-to-all-done) | data formatting | bytes 3145728 | tf_op jit(solution)/shard_map/reshape | solution.py:285
  60.1 1.3 copy-done.2
  61.3 1.0 copy-done.4
  62.3 0.8 copy-done.5
  63.2 0.9 copy-done.6
  64.1 0.8 copy-done.7
  64.9 20.4 %shard_map.83 = bf16[16,8,3,32,128]{4,3,2,1,0:T(8,128)(2,1)} custom-call(bf16[512,1536]{1,0:T(8,128)(2,1)S(1)} %reshape.474.arrived_ref, bf16[64,512]{1,0:T(8,128)(2,1)S(1)} %copy-done.5, s32[64,1]{1,0:T(8,128)S(1)} %copy-done.7, bf16[9,256,256]{2,1,0:T(8,128)(2,1)S(1)} %copy-done.2, bf16[512,256]{1,0:T(8,128)(2,1)S(1)} %copy-done.6, ...), custom_call_target="tpu_custom_call" | custom-call | tf_op jit(solution)/shard_map/pallas_call | solution.py:167
  85.3 5.8 %all-to-all-start.1 = ((bf16[128,3,32,128]{3,2,1,0:T(8,128)(2,1)}), bf16[128,3,32,128]{3,2,1,0:T(8,128)(2,1)}, u32[]{:S(2)}, u32[]{:S(2)}) async-start(bf16[128,3,32,128]{3,2,1,0:T(8,128)(2,1)} %bitcast.28), calls=%async_computation.1 | async-start | bytes 6291456 | tf_op jit(solution)/shard_map/all_to_all | solution.py:298
  91.5 2.7 %reduce-precision_convert_fusion = (bf16[32,3,1,128,128]{4,3,2,1,0:T(8,128)(2,1)S(1)}, bf16[32,3,1,128,128]{4,3,2,1,0:T(8,128)(2,1)S(1)}) fusion(f32[32,3]{1,0:T(8,128)S(1)} %bitcast.34, f32[32,3]{1,0:T(8,128)S(1)} %bitcast.33, f32[32,3]{1,0:T(8,128)S(1)} %bitcast.32, pred[128,128]{1,0:T(8,128)(4,1)S(1)} %get-tuple-element.14, ...), kind=kLoop, calls=%fused_computation.3 | loop fusion | flops 14155776 | bytes 6341760 | tf_op jit(solution)/shard_map/convert_element_type | solution.py:202
  94.2 3.2 %pad_maximum_fusion.taps_ref = bf16[32,3,2,128,128]{4,3,2,1,0:T(8,128)(2,1)} fusion(bf16[32,3,1,128,128]{4,3,2,1,0:T(8,128)(2,1)S(1)} %get-tuple-element.6, bf16[32,3,1,128,128]{4,3,2,1,0:T(8,128)(2,1)S(1)} %get-tuple-element.5), kind=kLoop, calls=%fused_computation.5 | loop fusion | flops 3145728 | bytes 12582912 | tf_op jit(solution)/shard_map/stack | solution.py:202
  97.4 1.7 %fusion.1.sel_ref = bf16[4,256,1024]{2,1,0:T(8,128)(2,1)} fusion(s32[4,256]{1,0:T(4,128)S(1)} %add_add_fusion), kind=kLoop, calls=%fused_computation.8 | loop fusion | flops 2097152 | bytes 2101248 | tf_op jit(solution)/shard_map/convert_element_type | solution.py:191
  99.1 33.4 %all-to-all-done.1 = bf16[128,3,32,128]{3,2,1,0:T(8,128)(2,1)} async-done(((bf16[128,3,32,128]{3,2,1,0:T(8,128)(2,1)}), bf16[128,3,32,128]{3,2,1,0:T(8,128)(2,1)}, u32[]{:S(2)}, u32[]{:S(2)}) %all-to-all-start.1) | async-done | bytes 3145760 | tf_op jit(solution)/shard_map/all_to_all | solution.py:298
  132.6 1.6 copy-done.1
  134.2 25.6 %shard_map.84 = bf16[6,32,64,128]{3,2,1,0:T(8,128)(2,1)} custom-call(bf16[16,8,96,128]{3,2,1,0:T(8,128)(2,1)} %bitcast.9.recv_ref, bf16[4,256,1024]{2,1,0:T(8,128)(2,1)S(1)} %copy-done.1, bf16[32,3,2,128,128]{4,3,2,1,0:T(8,128)(2,1)} %pad_maximum_fusion.taps_ref), custom_call_target="tpu_custom_call" | custom-call | tf_op jit(solution)/shard_map/pallas_call | solution.py:250
  (61 shorter events, 3.9 us)
Async XLA Ops:
  0.0 21.8 %copy-start = (bf16[512,1536]{1,0:T(8,128)(2,1)S(1)}, bf16[512,1536]{1,0:T(8,128)(2,1)}, u32[]{:S(2)}) copy-start(bf16[512,1536]{1,0:T(8,128)(2,1)} %param.8) | copy-start | bytes 4718596
  23.9 9.1 %copy-start.8 = (s32[4,16,4]{1,2,0:T(4,128)S(1)}, s32[4,16,4]{1,2,0:T(4,128)}, u32[]{:S(2)}) copy-start(s32[4,16,4]{1,2,0:T(4,128)} %param.9) | copy-start | bytes 3076
  24.0 9.1 %copy-start.9 = (s32[4,16]{1,0:T(4,128)S(1)}, s32[4,16]{1,0:T(4,128)}, u32[]{:S(2)}) copy-start(s32[4,16]{1,0:T(4,128)} %param.10) | copy-start | bytes 772
  24.0 11.0 %copy-start.11 = (bf16[8,64]{1,0:T(8,128)(2,1)S(1)}, bf16[8,64]{1,0:T(8,128)(2,1)}, u32[]{:S(2)}) copy-start(bf16[8,64]{1,0:T(8,128)(2,1)} %param.11) | copy-start | bytes 3076
  25.3 32.0 %all-to-all-start = ((bf16[128,4,1536]{2,1,0:T(4,128)(2,1)}), bf16[128,4,1536]{2,1,0:T(4,128)(2,1)}, u32[]{:S(2)}, u32[]{:S(2)}) async-start(bf16[128,4,1536]{2,1,0:T(4,128)(2,1)} %reshape.482), calls=%async_computation | async-start | bytes 3145728 | tf_op jit(solution)/shard_map/all_to_all | solution.py:284
  35.0 25.1 %copy-start.3 = (bf16[768,256]{1,0:T(8,128)(2,1)S(1)}, bf16[768,256]{1,0:T(8,128)(2,1)}, u32[]{:S(2)}) copy-start(bf16[768,256]{1,0:T(8,128)(2,1)} %w3_ref.1) | copy-start | bytes 1179652
  60.1 1.3 copy-start.2
  61.3 1.0 copy-start.4
  62.3 0.8 copy-start.5
  63.2 0.9 copy-start.6
  64.1 0.8 copy-start.7
  85.3 5.8 %copy-start.10 = (f32[32,9]{0,1:T(8,128)S(1)}, f32[32,9]{0,1:T(8,128)}, u32[]{:S(2)}) copy-start(f32[32,9]{0,1:T(8,128)} %param.15) | copy-start | bytes 3460
  85.3 47.3 %all-to-all-start.1 = ((bf16[128,3,32,128]{3,2,1,0:T(8,128)(2,1)}), bf16[128,3,32,128]{3,2,1,0:T(8,128)(2,1)}, u32[]{:S(2)}, u32[]{:S(2)}) async-start(bf16[128,3,32,128]{3,2,1,0:T(8,128)(2,1)} %bitcast.28), calls=%async_computation.1 | async-start | bytes 6291456 | tf_op jit(solution)/shard_map/all_to_all | solution.py:298
  132.6 1.6 copy-start.1

commit v11 on v10

--- a/solution.py
+++ b/solution.py
@@ -63,8 +63,16 @@
         compiler_params=pltpu.CompilerParams(collective_id=collective_id, has_side_effects=True),
     )(x)
 
-def encoder_kernel(n_il, n_xl, bins, arrived_ref, select_ref, counts_ref, b1_ref, w2_ref, w3_ref,
-                   w4_ref, out_ref, stacked, paired, first_pad, second_pad, third_pad):
+def encoder_kernel(n_il, n_xl, bins, arrived_ref, select_ref, counts_ref, b1_hbm, w2_hbm, w3_hbm,
+                   w4_hbm, out_ref, stacked, paired, first_pad, second_pad, third_pad,
+                   b1_ref, w2_ref, w3_ref, w4_ref, weight_sems):
+    loads = [
+        pltpu.make_async_copy(src, dst, weight_sems.at[i])
+        for i, (src, dst) in enumerate(
+            ((b1_hbm, b1_ref), (w2_hbm, w2_ref), (w3_hbm, w3_ref), (w4_hbm, w4_ref)))
+    ]
+    for load in loads:
+        load.start()
     samples = arrived_ref.shape[1]
     width = w2_ref.shape[1]
     rows = first_pad.shape[0] - bins
@@ -108,6 +116,7 @@
                     y[m * bins:(m + 1) * bins])
         return carry
 
+    loads[0].wait()
     lax.fori_loop(0, 8, layer1, 0)
     y0 = jnp.dot(paired[pl.ds(0, bins), :], b1_ref[8], preferred_element_type=f32)
     first_pad[pl.ds(bins, bins), :] = gelu(y0).astype(jnp.bfloat16)
@@ -121,6 +130,7 @@
         second_pad[pl.ds(bins + r0, chunk), :] = gelu(y).astype(jnp.bfloat16)
         return carry
 
+    loads[1].wait()
     lax.fori_loop(0, n_chunks, layer2, 0)
 
     def centred(src, w_ref, r0):
@@ -137,6 +147,7 @@
         third_pad[pl.ds(bins + r0, chunk), :] = gelu(y).astype(jnp.bfloat16)
         return carry
 
+    loads[2].wait()
     lax.fori_loop(0, n_chunks, layer3, 0)
 
     def layer4(ci, carry):
@@ -153,6 +164,7 @@
                 jnp.bfloat16)
         return carry
 
+    loads[3].wait()
     lax.fori_loop(0, n_chunks, layer4, 0)
 
 
@@ -167,7 +179,7 @@
     return pl.pallas_call(
         functools.partial(encoder_kernel, n_il, n_xl, bins),
         out_shape=out_shape,
-        in_specs=[pl.BlockSpec(memory_space=pltpu.VMEM)] * 7,
+        in_specs=[pl.BlockSpec(memory_space=pltpu.VMEM)] * 3 + [pl.BlockSpec(memory_space=pl.ANY)] * 4,
         out_specs=pl.BlockSpec(memory_space=pltpu.VMEM),
         scratch_shapes=[
             pltpu.VMEM((bins, samples + 128), jnp.bfloat16),
@@ -175,6 +187,11 @@
             pltpu.VMEM((bins + rows, width), jnp.bfloat16),
             pltpu.VMEM((2 * bins + rows, width), jnp.bfloat16),
             pltpu.VMEM((2 * bins + rows, width), jnp.bfloat16),
+            pltpu.VMEM(b1.shape, b1.dtype),
+            pltpu.VMEM(conv2_w.shape, conv2_w.dtype),
+            pltpu.VMEM(conv3_w.shape, conv3_w.dtype),
+            pltpu.VMEM(conv4_w.shape, conv4_w.dtype),
+            pltpu.SemaphoreType.DMA((4,)),
         ],
         compiler_params=pltpu.CompilerParams(vmem_limit_bytes=48 * 1024 * 1024),
     )(arrived, select, counts, b1, conv2_w, conv3_w, conv4_w)
@@ -202,7 +219,9 @@
     return jnp.stack([high.astype(jnp.bfloat16), low], axis=2)
 
 
-def receive_kernel(recv_ref, sel_ref, taps_ref, out_ref, field):
+def receive_kernel(recv_ref, sel_ref, taps_hbm, out_ref, field, taps_ref, taps_sem):
+    taps_load = pltpu.make_async_copy(taps_hbm, taps_ref, taps_sem)
+    taps_load.start()
     n_a, n_b, rows_k_o, lanes = recv_ref.shape
     n_s, n_o, n_p, n_q = out_ref.shape
     n_k = rows_k_o // n_o
@@ -243,6 +262,7 @@
         out_ref[:, o] = acc.astype(out_ref.dtype).reshape(n_s, n_p, n_q)
         return carry
 
+    taps_load.wait()
     lax.fori_loop(0, n_o, mix, 0)
 
 
@@ -250,9 +270,13 @@
     return pl.pallas_call(
         receive_kernel,
         out_shape=jax.ShapeDtypeStruct((n_s, n_o, n_p, n_q), jnp.bfloat16),
-        in_specs=[pl.BlockSpec(memory_space=pltpu.VMEM)] * 3,
+        in_specs=[pl.BlockSpec(memory_space=pltpu.VMEM)] * 2 + [pl.BlockSpec(memory_space=pl.ANY)],
         out_specs=pl.BlockSpec(memory_space=pltpu.VMEM),
-        scratch_shapes=[pltpu.VMEM((n_s * n_o * n_p, n_q), jnp.float32)],
+        scratch_shapes=[
+            pltpu.VMEM((n_s * n_o * n_p, n_q), jnp.float32),
+            pltpu.VMEM(lw.shape, lw.dtype),
+            pltpu.SemaphoreType.DMA(()),
+        ],
         compiler_params=pltpu.CompilerParams(vmem_limit_bytes=48 * 1024 * 1024),
     )(received, sel, lw)
 

time: 160 us -> 159 us (level)
    pallas_call x1, Pallas kernels: 25.6 us -> 23.8 us  [receive_mix(): pl.pallas_call(receive_kernel, out_shape=jax.ShapeDtypeStruct((n_s, n_o,...]
where the time goes in v11:
time: 159 us; the launch traced here: 158 us
  Pallas kernels  61.6 us (39%)
  waiting for transfers between devices  53.8 us (34%)
  local copies, waits for them, and re-layouts  19.9 us (13%)
  starting transfers between devices  13.2 us (8%)
  other arithmetic  9.16 us (6%)
    all_to_all x1, waiting for transfers between devices, per_device(): lax.all_to_all(outgoing, ('il', 'xl'), split_axis=0, concat_axis=0, tiled...  33.4 us
    pallas_call x1, Pallas kernels, receive_mix(): pl.pallas_call(receive_kernel, out_shape=jax.ShapeDtypeStruct((n_s, n_o,...  23.8 us
    pallas_call x1, Pallas kernels, encode_to_send(): pl.pallas_call(functools.partial(encoder_kernel, n_il, n_xl, bins), out_s...  21.1 us
    all_to_all x1, waiting for transfers between devices, per_device(): lax.all_to_all(picked, ('il', 'xl'), split_axis=0, concat_axis=0, tiled=T...  20.3 us
    pallas_call x1, Pallas kernels, exchange(): pl.pallas_call(functools.partial(exchange_kernel, n_il, n_xl), out_shape=...  16.8 us
    all_to_all x1, starting transfers between devices, per_device(): lax.all_to_all(picked, ('il', 'xl'), split_axis=0, concat_axis=0, tiled=T...  7.6 us
    unnamed x27, local copies, waits for them, and re-layouts  7.35 us
    all_to_all x1, starting transfers between devices, per_device(): lax.all_to_all(outgoing, ('il', 'xl'), split_axis=0, concat_axis=0, tiled...  5.64 us
  transfers between devices with their start and end apart: 2, of which 2 were waited for; matrix products, arithmetic and copies ran while one was open for 8% of the time, Pallas kernels for 0%

profile of v11, /device:TPU:1, one launch (start us, length us, event | category | flops | bytes accessed | tf_op | source)
XLA Modules:
  0.0 158.5 jit_solution(14951965027171603420)
XLA Ops:
  0.0 0.9 copy.30
  1.9 1.4 scatter_custom_fusion
  3.3 0.7 reshape.473.x_ref
  4.0 16.8 %shard_map.82 = s32[128,4]{1,0:T(8,128)} custom-call(s32[128,4]{1,0:T(8,128)} %reshape.473.x_ref), custom_call_target="tpu_custom_call" | custom-call | tf_op jit(solution)/shard_map/pallas_call | solution.py:57
  20.8 0.9 reshape.483
  21.8 2.1 %gather_fusion = bf16[512,1536]{1,0:T(8,128)(2,1)S(1)} fusion(bf16[512,1536]{1,0:T(8,128)(2,1)S(1)} %copy-done, s32[1024]{0:T(1024)S(1)} %pad_clamp_fusion), kind=kCustom, calls=%fused_computation | custom fusion | bytes 3147776 | tf_op jit(solution)/shard_map/jit(_take)/gather | solution.py:307
  24.0 1.3 reshape.482
  25.3 7.6 %all-to-all-start = ((bf16[128,4,1536]{2,1,0:T(4,128)(2,1)}), bf16[128,4,1536]{2,1,0:T(4,128)(2,1)}, u32[]{:S(2)}, u32[]{:S(2)}) async-start(bf16[128,4,1536]{2,1,0:T(4,128)(2,1)} %reshape.482), calls=%async_computation | async-start | bytes 3145728 | tf_op jit(solution)/shard_map/all_to_all | solution.py:308
  35.5 1.5 copy.38.b1_hbm
  37.0 20.3 %all-to-all-done = bf16[128,4,1536]{2,1,0:T(4,128)(2,1)} async-done(((bf16[128,4,1536]{2,1,0:T(4,128)(2,1)}), bf16[128,4,1536]{2,1,0:T(4,128)(2,1)}, u32[]{:S(2)}, u32[]{:S(2)}) %all-to-all-start) | async-done | bytes 1572896 | tf_op jit(solution)/shard_map/all_to_all | solution.py:308
  57.3 2.7 %reshape.474.arrived_ref = bf16[512,1536]{1,0:T(8,128)(2,1)S(1)} reshape(bf16[128,4,1536]{2,1,0:T(4,128)(2,1)} %all-to-all-done) | data formatting | bytes 3145728 | tf_op jit(solution)/shard_map/reshape | solution.py:309
  60.1 1.3 copy-done.2
  61.3 1.0 copy-done.4
  62.3 0.8 copy-done.5
  63.2 0.9 copy-done.6
  64.1 0.8 copy-done.7
  64.9 21.1 %shard_map.83 = bf16[16,8,3,32,128]{4,3,2,1,0:T(8,128)(2,1)} custom-call(bf16[512,1536]{1,0:T(8,128)(2,1)S(1)} %reshape.474.arrived_ref, bf16[64,512]{1,0:T(8,128)(2,1)S(1)} %copy-done.5, s32[64,1]{1,0:T(8,128)S(1)} %copy-done.7, bf16[9,256,256]{2,1,0:T(8,128)(2,1)S(1)} %copy-done.2, bf16[512,256]{1,0:T(8,128)(2,1)S(1)} %copy-done.6, ...), custom_call_target="tpu_custom_call" | custom-call | tf_op jit(solution)/shard_map/pallas_call | solution.py:179
  86.0 5.6 %all-to-all-start.1 = ((bf16[128,3,32,128]{3,2,1,0:T(8,128)(2,1)}), bf16[128,3,32,128]{3,2,1,0:T(8,128)(2,1)}, u32[]{:S(2)}, u32[]{:S(2)}) async-start(bf16[128,3,32,128]{3,2,1,0:T(8,128)(2,1)} %bitcast.28), calls=%async_computation.1 | async-start | bytes 6291456 | tf_op jit(solution)/shard_map/all_to_all | solution.py:322
  92.1 2.7 %reduce-precision_convert_fusion = (bf16[32,3,1,128,128]{4,3,2,1,0:T(8,128)(2,1)S(1)}, bf16[32,3,1,128,128]{4,3,2,1,0:T(8,128)(2,1)S(1)}) fusion(f32[32,3]{1,0:T(8,128)S(1)} %bitcast.34, f32[32,3]{1,0:T(8,128)S(1)} %bitcast.33, f32[32,3]{1,0:T(8,128)S(1)} %bitcast.32, pred[128,128]{1,0:T(8,128)(4,1)S(1)} %get-tuple-element.14, ...), kind=kLoop, calls=%fused_computation.3 | loop fusion | flops 14155776 | bytes 6341760 | tf_op jit(solution)/shard_map/convert_element_type | solution.py:219
  94.7 3.2 %pad_maximum_fusion.taps_hbm = bf16[32,3,2,128,128]{4,3,2,1,0:T(8,128)(2,1)} fusion(bf16[32,3,1,128,128]{4,3,2,1,0:T(8,128)(2,1)S(1)} %get-tuple-element.6, bf16[32,3,1,128,128]{4,3,2,1,0:T(8,128)(2,1)S(1)} %get-tuple-element.5), kind=kLoop, calls=%fused_computation.5 | loop fusion | flops 3145728 | bytes 12582912 | tf_op jit(solution)/shard_map/stack | solution.py:219
  98.0 1.7 %fusion.1.sel_ref = bf16[4,256,1024]{2,1,0:T(8,128)(2,1)} fusion(s32[4,256]{1,0:T(4,128)S(1)} %add_add_fusion), kind=kLoop, calls=%fused_computation.8 | loop fusion | flops 2097152 | bytes 2101248 | tf_op jit(solution)/shard_map/convert_element_type | solution.py:208
  99.7 33.4 %all-to-all-done.1 = bf16[128,3,32,128]{3,2,1,0:T(8,128)(2,1)} async-done(((bf16[128,3,32,128]{3,2,1,0:T(8,128)(2,1)}), bf16[128,3,32,128]{3,2,1,0:T(8,128)(2,1)}, u32[]{:S(2)}, u32[]{:S(2)}) %all-to-all-start.1) | async-done | bytes 3145760 | tf_op jit(solution)/shard_map/all_to_all | solution.py:322
  133.1 1.6 %copy-done.1 = bf16[4,256,1024]{2,1,0:T(8,128)(2,1)S(1)} copy-done((bf16[4,256,1024]{2,1,0:T(8,128)(2,1)S(1)}, bf16[4,256,1024]{2,1,0:T(8,128)(2,1)}, u32[]{:S(2)}) %copy-start.1) | copy-done | bytes 2097176
  134.7 23.8 %shard_map.84 = bf16[6,32,64,128]{3,2,1,0:T(8,128)(2,1)} custom-call(bf16[16,8,96,128]{3,2,1,0:T(8,128)(2,1)} %bitcast.9.recv_ref, bf16[4,256,1024]{2,1,0:T(8,128)(2,1)S(1)} %copy-done.1, bf16[32,3,2,128,128]{4,3,2,1,0:T(8,128)(2,1)} %pad_maximum_fusion.taps_hbm), custom_call_target="tpu_custom_call" | custom-call | tf_op jit(solution)/shard_map/pallas_call | solution.py:270
  (61 shorter events, 3.9 us)
Async XLA Ops:
  0.0 21.8 %copy-start = (bf16[512,1536]{1,0:T(8,128)(2,1)S(1)}, bf16[512,1536]{1,0:T(8,128)(2,1)}, u32[]{:S(2)}) copy-start(bf16[512,1536]{1,0:T(8,128)(2,1)} %param.8) | copy-start | bytes 4718596
  23.9 9.1 %copy-start.8 = (s32[4,16,4]{1,2,0:T(4,128)S(1)}, s32[4,16,4]{1,2,0:T(4,128)}, u32[]{:S(2)}) copy-start(s32[4,16,4]{1,2,0:T(4,128)} %param.9) | copy-start | bytes 3076
  24.0 9.1 %copy-start.9 = (s32[4,16]{1,0:T(4,128)S(1)}, s32[4,16]{1,0:T(4,128)}, u32[]{:S(2)}) copy-start(s32[4,16]{1,0:T(4,128)} %param.10) | copy-start | bytes 772
  24.0 11.0 %copy-start.11 = (bf16[8,64]{1,0:T(8,128)(2,1)S(1)}, bf16[8,64]{1,0:T(8,128)(2,1)}, u32[]{:S(2)}) copy-start(bf16[8,64]{1,0:T(8,128)(2,1)} %param.11) | copy-start | bytes 3076
  25.3 32.0 %all-to-all-start = ((bf16[128,4,1536]{2,1,0:T(4,128)(2,1)}), bf16[128,4,1536]{2,1,0:T(4,128)(2,1)}, u32[]{:S(2)}, u32[]{:S(2)}) async-start(bf16[128,4,1536]{2,1,0:T(4,128)(2,1)} %reshape.482), calls=%async_computation | async-start | bytes 3145728 | tf_op jit(solution)/shard_map/all_to_all | solution.py:308
  35.0 25.1 %copy-start.3 = (bf16[768,256]{1,0:T(8,128)(2,1)S(1)}, bf16[768,256]{1,0:T(8,128)(2,1)}, u32[]{:S(2)}) copy-start(bf16[768,256]{1,0:T(8,128)(2,1)} %w3_hbm.1) | copy-start | bytes 1179652
  60.1 1.3 copy-start.2
  61.3 1.0 copy-start.4
  62.3 0.8 copy-start.5
  63.2 0.9 copy-start.6
  64.1 0.8 copy-start.7
  86.0 5.7 %copy-start.10 = (f32[32,9]{0,1:T(8,128)S(1)}, f32[32,9]{0,1:T(8,128)}, u32[]{:S(2)}) copy-start(f32[32,9]{0,1:T(8,128)} %param.15) | copy-start | bytes 3460
  86.0 47.2 %all-to-all-start.1 = ((bf16[128,3,32,128]{3,2,1,0:T(8,128)(2,1)}), bf16[128,3,32,128]{3,2,1,0:T(8,128)(2,1)}, u32[]{:S(2)}, u32[]{:S(2)}) async-start(bf16[128,3,32,128]{3,2,1,0:T(8,128)(2,1)} %bitcast.28), calls=%async_computation.1 | async-start | bytes 6291456 | tf_op jit(solution)/shard_map/all_to_all | solution.py:322
  133.1 1.6 %copy-start.1 = (bf16[4,256,1024]{2,1,0:T(8,128)(2,1)S(1)}, bf16[4,256,1024]{2,1,0:T(8,128)(2,1)}, u32[]{:S(2)}) copy-start(bf16[4,256,1024]{2,1,0:T(8,128)(2,1)} %fusion.1.sel_ref) | copy-start | bytes 6291460

commit v12 on v11

--- a/solution.py
+++ b/solution.py
@@ -99,7 +99,9 @@
         paired[pl.ds(m * bins, bins), :] = stacked[:, pl.ds(m * 128, 256)]
 
     def gelu(x):
-        return jax.nn.gelu(x)
+        half = 0.5 * x
+        inner = x * (np.float32(np.sqrt(2.0 / np.pi)) + np.float32(np.sqrt(2.0 / np.pi) * 0.044715) * (x * x))
+        return half + half * jnp.tanh(inner)
 
     def layer1(c, carry):
         y = jnp.dot(paired[...], b1_ref[c], preferred_element_type=f32)

time: 159 us -> 159 us (level)
  no operation moved by 1% of the time
where the time goes in v12:
time: 159 us; the launch traced here: 158 us
  Pallas kernels  61 us (38%)
  waiting for transfers between devices  53.8 us (34%)
  local copies, waits for them, and re-layouts  19.9 us (13%)
  starting transfers between devices  13.2 us (8%)
  other arithmetic  9.16 us (6%)
    all_to_all x1, waiting for transfers between devices, per_device(): lax.all_to_all(outgoing, ('il', 'xl'), split_axis=0, concat_axis=0, tiled...  33.4 us
    pallas_call x1, Pallas kernels, receive_mix(): pl.pallas_call(receive_kernel, out_shape=jax.ShapeDtypeStruct((n_s, n_o,...  23.8 us
    pallas_call x1, Pallas kernels, encode_to_send(): pl.pallas_call(functools.partial(encoder_kernel, n_il, n_xl, bins), out_s...  20.4 us
    all_to_all x1, waiting for transfers between devices, per_device(): lax.all_to_all(picked, ('il', 'xl'), split_axis=0, concat_axis=0, tiled=T...  20.3 us
    pallas_call x1, Pallas kernels, exchange(): pl.pallas_call(functools.partial(exchange_kernel, n_il, n_xl), out_shape=...  16.8 us
    all_to_all x1, starting transfers between devices, per_device(): lax.all_to_all(picked, ('il', 'xl'), split_axis=0, concat_axis=0, tiled=T...  7.6 us
    unnamed x27, local copies, waits for them, and re-layouts  7.35 us
    all_to_all x1, starting transfers between devices, per_device(): lax.all_to_all(outgoing, ('il', 'xl'), split_axis=0, concat_axis=0, tiled...  5.64 us
  transfers between devices with their start and end apart: 2, of which 2 were waited for; matrix products, arithmetic and copies ran while one was open for 8% of the time, Pallas kernels for 0%

profile of v12, /device:TPU:1, one launch (start us, length us, event | category | flops | bytes accessed | tf_op | source)
XLA Modules:
  0.0 157.9 jit_solution(11995560980265561021)
XLA Ops:
  0.0 0.9 copy.30
  1.9 1.4 scatter_custom_fusion
  3.3 0.7 reshape.473.x_ref
  4.0 16.8 %shard_map.82 = s32[128,4]{1,0:T(8,128)} custom-call(s32[128,4]{1,0:T(8,128)} %reshape.473.x_ref), custom_call_target="tpu_custom_call" | custom-call | tf_op jit(solution)/shard_map/pallas_call | solution.py:57
  20.8 0.9 reshape.483
  21.8 2.1 %gather_fusion = bf16[512,1536]{1,0:T(8,128)(2,1)S(1)} fusion(bf16[512,1536]{1,0:T(8,128)(2,1)S(1)} %copy-done, s32[1024]{0:T(1024)S(1)} %pad_clamp_fusion), kind=kCustom, calls=%fused_computation | custom fusion | bytes 3147776 | tf_op jit(solution)/shard_map/jit(_take)/gather | solution.py:309
  24.0 1.3 reshape.482
  25.3 7.6 %all-to-all-start = ((bf16[128,4,1536]{2,1,0:T(4,128)(2,1)}), bf16[128,4,1536]{2,1,0:T(4,128)(2,1)}, u32[]{:S(2)}, u32[]{:S(2)}) async-start(bf16[128,4,1536]{2,1,0:T(4,128)(2,1)} %reshape.482), calls=%async_computation | async-start | bytes 3145728 | tf_op jit(solution)/shard_map/all_to_all | solution.py:310
  35.5 1.5 copy.38.b1_hbm
  37.0 20.3 %all-to-all-done = bf16[128,4,1536]{2,1,0:T(4,128)(2,1)} async-done(((bf16[128,4,1536]{2,1,0:T(4,128)(2,1)}), bf16[128,4,1536]{2,1,0:T(4,128)(2,1)}, u32[]{:S(2)}, u32[]{:S(2)}) %all-to-all-start) | async-done | bytes 1572896 | tf_op jit(solution)/shard_map/all_to_all | solution.py:310
  57.3 2.7 %reshape.474.arrived_ref = bf16[512,1536]{1,0:T(8,128)(2,1)S(1)} reshape(bf16[128,4,1536]{2,1,0:T(4,128)(2,1)} %all-to-all-done) | data formatting | bytes 3145728 | tf_op jit(solution)/shard_map/reshape | solution.py:311
  60.1 1.3 copy-done.2
  61.3 1.0 copy-done.4
  62.3 0.8 copy-done.5
  63.2 0.9 copy-done.6
  64.1 0.8 copy-done.7
  64.9 20.4 %shard_map.83 = bf16[16,8,3,32,128]{4,3,2,1,0:T(8,128)(2,1)} custom-call(bf16[512,1536]{1,0:T(8,128)(2,1)S(1)} %reshape.474.arrived_ref, bf16[64,512]{1,0:T(8,128)(2,1)S(1)} %copy-done.5, s32[64,1]{1,0:T(8,128)S(1)} %copy-done.7, bf16[9,256,256]{2,1,0:T(8,128)(2,1)S(1)} %copy-done.2, bf16[512,256]{1,0:T(8,128)(2,1)S(1)} %copy-done.6, ...), custom_call_target="tpu_custom_call" | custom-call | tf_op jit(solution)/shard_map/pallas_call | solution.py:181
  85.3 5.6 %all-to-all-start.1 = ((bf16[128,3,32,128]{3,2,1,0:T(8,128)(2,1)}), bf16[128,3,32,128]{3,2,1,0:T(8,128)(2,1)}, u32[]{:S(2)}, u32[]{:S(2)}) async-start(bf16[128,3,32,128]{3,2,1,0:T(8,128)(2,1)} %bitcast.28), calls=%async_computation.1 | async-start | bytes 6291456 | tf_op jit(solution)/shard_map/all_to_all | solution.py:324
  91.4 2.7 %reduce-precision_convert_fusion = (bf16[32,3,1,128,128]{4,3,2,1,0:T(8,128)(2,1)S(1)}, bf16[32,3,1,128,128]{4,3,2,1,0:T(8,128)(2,1)S(1)}) fusion(f32[32,3]{1,0:T(8,128)S(1)} %bitcast.34, f32[32,3]{1,0:T(8,128)S(1)} %bitcast.33, f32[32,3]{1,0:T(8,128)S(1)} %bitcast.32, pred[128,128]{1,0:T(8,128)(4,1)S(1)} %get-tuple-element.14, ...), kind=kLoop, calls=%fused_computation.3 | loop fusion | flops 14155776 | bytes 6341760 | tf_op jit(solution)/shard_map/convert_element_type | solution.py:221
  94.1 3.2 %pad_maximum_fusion.taps_hbm = bf16[32,3,2,128,128]{4,3,2,1,0:T(8,128)(2,1)} fusion(bf16[32,3,1,128,128]{4,3,2,1,0:T(8,128)(2,1)S(1)} %get-tuple-element.6, bf16[32,3,1,128,128]{4,3,2,1,0:T(8,128)(2,1)S(1)} %get-tuple-element.5), kind=kLoop, calls=%fused_computation.5 | loop fusion | flops 3145728 | bytes 12582912 | tf_op jit(solution)/shard_map/stack | solution.py:221
  97.3 1.7 %fusion.1.sel_ref = bf16[4,256,1024]{2,1,0:T(8,128)(2,1)} fusion(s32[4,256]{1,0:T(4,128)S(1)} %add_add_fusion), kind=kLoop, calls=%fused_computation.8 | loop fusion | flops 2097152 | bytes 2101248 | tf_op jit(solution)/shard_map/convert_element_type | solution.py:210
  99.0 33.4 %all-to-all-done.1 = bf16[128,3,32,128]{3,2,1,0:T(8,128)(2,1)} async-done(((bf16[128,3,32,128]{3,2,1,0:T(8,128)(2,1)}), bf16[128,3,32,128]{3,2,1,0:T(8,128)(2,1)}, u32[]{:S(2)}, u32[]{:S(2)}) %all-to-all-start.1) | async-done | bytes 3145760 | tf_op jit(solution)/shard_map/all_to_all | solution.py:324
  132.5 1.6 %copy-done.1 = bf16[4,256,1024]{2,1,0:T(8,128)(2,1)S(1)} copy-done((bf16[4,256,1024]{2,1,0:T(8,128)(2,1)S(1)}, bf16[4,256,1024]{2,1,0:T(8,128)(2,1)}, u32[]{:S(2)}) %copy-start.1) | copy-done | bytes 2097176
  134.1 23.8 %shard_map.84 = bf16[6,32,64,128]{3,2,1,0:T(8,128)(2,1)} custom-call(bf16[16,8,96,128]{3,2,1,0:T(8,128)(2,1)} %bitcast.9.recv_ref, bf16[4,256,1024]{2,1,0:T(8,128)(2,1)S(1)} %copy-done.1, bf16[32,3,2,128,128]{4,3,2,1,0:T(8,128)(2,1)} %pad_maximum_fusion.taps_hbm), custom_call_target="tpu_custom_call" | custom-call | tf_op jit(solution)/shard_map/pallas_call | solution.py:272
  (61 shorter events, 3.9 us)
Async XLA Ops:
  0.0 21.8 %copy-start = (bf16[512,1536]{1,0:T(8,128)(2,1)S(1)}, bf16[512,1536]{1,0:T(8,128)(2,1)}, u32[]{:S(2)}) copy-start(bf16[512,1536]{1,0:T(8,128)(2,1)} %param.8) | copy-start | bytes 4718596
  23.9 9.1 %copy-start.8 = (s32[4,16,4]{1,2,0:T(4,128)S(1)}, s32[4,16,4]{1,2,0:T(4,128)}, u32[]{:S(2)}) copy-start(s32[4,16,4]{1,2,0:T(4,128)} %param.9) | copy-start | bytes 3076
  24.0 9.1 %copy-start.9 = (s32[4,16]{1,0:T(4,128)S(1)}, s32[4,16]{1,0:T(4,128)}, u32[]{:S(2)}) copy-start(s32[4,16]{1,0:T(4,128)} %param.10) | copy-start | bytes 772
  24.0 11.0 %copy-start.11 = (bf16[8,64]{1,0:T(8,128)(2,1)S(1)}, bf16[8,64]{1,0:T(8,128)(2,1)}, u32[]{:S(2)}) copy-start(bf16[8,64]{1,0:T(8,128)(2,1)} %param.11) | copy-start | bytes 3076
  25.3 32.0 %all-to-all-start = ((bf16[128,4,1536]{2,1,0:T(4,128)(2,1)}), bf16[128,4,1536]{2,1,0:T(4,128)(2,1)}, u32[]{:S(2)}, u32[]{:S(2)}) async-start(bf16[128,4,1536]{2,1,0:T(4,128)(2,1)} %reshape.482), calls=%async_computation | async-start | bytes 3145728 | tf_op jit(solution)/shard_map/all_to_all | solution.py:310
  35.0 25.1 %copy-start.3 = (bf16[768,256]{1,0:T(8,128)(2,1)S(1)}, bf16[768,256]{1,0:T(8,128)(2,1)}, u32[]{:S(2)}) copy-start(bf16[768,256]{1,0:T(8,128)(2,1)} %w3_hbm.1) | copy-start | bytes 1179652
  60.1 1.3 copy-start.2
  61.3 1.0 copy-start.4
  62.3 0.8 copy-start.5
  63.2 0.9 copy-start.6
  64.1 0.8 copy-start.7
  85.3 5.7 %copy-start.10 = (f32[32,9]{0,1:T(8,128)S(1)}, f32[32,9]{0,1:T(8,128)}, u32[]{:S(2)}) copy-start(f32[32,9]{0,1:T(8,128)} %param.15) | copy-start | bytes 3460
  85.3 47.2 %all-to-all-start.1 = ((bf16[128,3,32,128]{3,2,1,0:T(8,128)(2,1)}), bf16[128,3,32,128]{3,2,1,0:T(8,128)(2,1)}, u32[]{:S(2)}, u32[]{:S(2)}) async-start(bf16[128,3,32,128]{3,2,1,0:T(8,128)(2,1)} %bitcast.28), calls=%async_computation.1 | async-start | bytes 6291456 | tf_op jit(solution)/shard_map/all_to_all | solution.py:324
  132.5 1.6 %copy-start.1 = (bf16[4,256,1024]{2,1,0:T(8,128)(2,1)S(1)}, bf16[4,256,1024]{2,1,0:T(8,128)(2,1)}, u32[]{:S(2)}) copy-start(bf16[4,256,1024]{2,1,0:T(8,128)(2,1)} %fusion.1.sel_ref) | copy-start | bytes 6291460
